TPU v7x, 32 devices: a whole 2x2x4 slice. The times are simulated.
32 devices in a mesh: batch: 8 (over z, y), head: 4 (over x, core).
Axes of the slice: x: 2, y: 2, z: 4, core: 2. Of those that a mesh axis runs over, the one named last changes fastest.
Arguments:
- tokens_in: bfloat16 [32768, 768], P(('batch', 'head')), may hold values from -5.6 to 5.6
- doc_ids: int32 [32768], P('batch'), may hold values from 0 to 3, as said below
- landmark_ids: int32 [32768], P('batch'), may hold values from 0 to 63, as said below
- pad_mask: int32 [32768], P('batch'), may hold values from 0 to 1, as said below
- w_query: bfloat16 [768, 768], P(None, 'head'), may hold values from -0.21875 to 0.21875
- w_key: bfloat16 [768, 768], P(None, 'head'), may hold values from -0.21875 to 0.21875
- w_value: bfloat16 [768, 768], P(None, 'head'), may hold values from -0.21875 to 0.21875
- w_output: bfloat16 [768, 768], P('head'), may hold values from -0.625 to 0.625
- conv_weight: bfloat16 [12, 33], P('head'), may hold values from -0.47851562 to 0.47851562
- first_gain: float32 [768], replicated, may hold values from 0.5 to 1.5
- first_bias: float32 [768], replicated, may hold values from -1.2 to 1.2
- w_inner: bfloat16 [768, 3072], replicated, may hold values from -0.21875 to 0.21875
- w_outer: bfloat16 [3072, 768], replicated, may hold values from -0.109375 to 0.109375
- second_gain: float32 [768], replicated, may hold values from 0.5 to 1.5
- second_bias: float32 [768], replicated, may hold values from -1.2 to 1.2
- out_grad: bfloat16 [32768, 768], P(('batch', 'head')), may hold values from -6 to 6
Outputs:
- layer_out: bfloat16 [32768, 768], P(('batch', 'head'))
- input_grad: bfloat16 [32768, 768], P(('batch', 'head'))
- grad_query: float32 [768, 768], P(None, 'head')
- grad_key: float32 [768, 768], P(None, 'head')
- grad_value: float32 [768, 768], P(None, 'head')
- grad_output: float32 [768, 768], P('head')
- grad_conv: float32 [12, 33], P('head')
- grad_first_gain: float32 [768], replicated
- grad_first_bias: float32 [768], replicated
- grad_inner: float32 [768, 3072], P(None, 'head')
- grad_outer: float32 [3072, 768], P('head')
- grad_second_gain: float32 [768], replicated
- grad_second_bias: float32 [768], replicated
Inputs may be any that keep to these rules, and one draw needn't show every extreme that they name: `doc_ids`: within a row of 4096 tokens document numbers never fall, and each document has 128 real tokens or more. `landmark_ids`: within a document landmark numbers never fall, and every landmark of every document has 2 or more real tokens. `pad_mask`: the padding of a row is its last tokens, at least one, and counts to its last document.
All inputs are finite; a program needn't handle non-finite values.
Results may differ from a plain program's by a relative error of at most 0.018.
Values may be sent and summed in bfloat16 or wider, within the bound.
No kernel may reach another device: no remote copies, remote signals or barrier semaphores. Data moves between devices by JAX's collectives and lax.ppermute only.
A program may use at most 256 MiB of HBM per device.

v0:
```python
import jax
import jax.numpy as jnp
from jax import lax
from jax.sharding import PartitionSpec as P

LAND = 64
KW = 33
HEAD_DIM = 64
NEWTON = 6
DOCS = 4


EXACT_PRECISION = lax.Precision.HIGHEST
NEG_FILL = -1e30
NORM_EPS = 1e-05


def newton_inverse(kernel):
    square_sum = jnp.sum(kernel * kernel, axis=(-2, -1), keepdims=True)
    estimate = jnp.swapaxes(kernel, -1, -2) / square_sum
    identity = jnp.eye(kernel.shape[-1], dtype=kernel.dtype)
    for step_count in range(NEWTON):
        product = jnp.matmul(kernel, estimate, precision=EXACT_PRECISION)
        factor_term = 7.0 * identity - product
        factor_term = 15.0 * identity - jnp.matmul(product, factor_term, precision=EXACT_PRECISION)
        factor_term = 13.0 * identity - jnp.matmul(product, factor_term, precision=EXACT_PRECISION)
        estimate = 0.25 * jnp.matmul(estimate, factor_term, precision=EXACT_PRECISION)
    return estimate


def norm_forward(hidden, scale_vec, shift_vec):
    center = hidden - jnp.mean(hidden, axis=-1, keepdims=True)
    inv_spread = lax.rsqrt(jnp.mean(center * center, axis=-1, keepdims=True) + NORM_EPS)
    normed = center * inv_spread
    return (normed * scale_vec + shift_vec, normed, inv_spread)


def norm_backward(upstream, normed, inv_spread, scale_vec):
    scaled = upstream * scale_vec
    result_grad = inv_spread * (
        scaled
        - jnp.mean(scaled, axis=-1, keepdims=True)
        - normed * jnp.mean(scaled * normed, axis=-1, keepdims=True)
    )
    return (result_grad, jnp.sum(upstream * normed, axis=0), jnp.sum(upstream, axis=0))


def exact_gelu(inputs):
    return jax.nn.gelu(inputs, approximate=False)


def softmax_back(prob_rows, upstream):
    return prob_rows * (upstream - jnp.sum(upstream * prob_rows, axis=-1, keepdims=True))


def shards(
    tokens_in,
    doc_ids,
    landmark_ids,
    pad_mask,
    w_query,
    w_key,
    w_value,
    w_output,
    conv_weight,
    first_gain,
    first_bias,
    w_inner,
    w_outer,
    second_gain,
    second_bias,
    out_grad,
):
    all_tokens = lax.all_gather(tokens_in, "head", axis=0, tiled=True)
    row_len = all_tokens.shape[0]
    local_heads = w_query.shape[1] // HEAD_DIM
    qk_scale = HEAD_DIM ** (-0.25)
    real_rows = pad_mask > 0
    real_float = real_rows.astype(jnp.float32)

    def project(weight, factor):
        mapped = jnp.dot(all_tokens, weight, preferred_element_type=jnp.float32) * factor
        return mapped.astype(jnp.bfloat16).reshape(row_len, local_heads, HEAD_DIM)

    queries = project(w_query, qk_scale)
    key_rows = project(w_key, qk_scale)
    values = project(w_value, 1.0)
    land_total = DOCS * LAND
    columns = jnp.arange(land_total, dtype=jnp.int32)
    segment = doc_ids * LAND + landmark_ids
    member = jnp.logical_and(segment[:, None] == columns[None, :], real_rows[:, None])
    member_float = member.astype(jnp.float32)
    member_low = member.astype(jnp.bfloat16)
    counts = jnp.sum(member_float, axis=0)
    same_doc = doc_ids[:, None] == (columns // LAND)[None, :]
    key_valid = jnp.logical_and(same_doc, real_rows[:, None])

    def landmark_mean(rows_in):
        summed_rows = jnp.einsum(
            "ts,thd->shd", member_low, rows_in, preferred_element_type=jnp.float32
        )
        return (summed_rows / counts[:, None, None]).astype(jnp.bfloat16)

    land_query = landmark_mean(queries)
    land_key = landmark_mean(key_rows)

    def first_scores():
        raw_scores = jnp.einsum(
            "thd,shd->hts", queries, land_key, preferred_element_type=jnp.float32
        )
        return jnp.where(same_doc[None], raw_scores, NEG_FILL)

    def third_scores():
        raw_scores = jnp.einsum(
            "shd,thd->hst", land_query, key_rows, preferred_element_type=jnp.float32
        )
        return jnp.where(key_valid.T[None], raw_scores, NEG_FILL)

    scores_now = first_scores()
    first_lse = jax.nn.logsumexp(scores_now, axis=-1, keepdims=True)
    first_low = jnp.exp(scores_now - first_lse).astype(jnp.bfloat16)
    scores_now = third_scores()
    third_lse = jax.nn.logsumexp(scores_now, axis=-1, keepdims=True)
    third_low = jnp.exp(scores_now - third_lse).astype(jnp.bfloat16)
    carried = jnp.einsum("hst,thd->hsd", third_low, values, preferred_element_type=jnp.float32)

    def small_kernel(land_q, land_k):
        doc_q = land_q.reshape(DOCS, LAND, local_heads, HEAD_DIM)
        doc_k = land_k.reshape(DOCS, LAND, local_heads, HEAD_DIM)
        small_scores = jnp.einsum("aihd,ajhd->haij", doc_q, doc_k, precision=EXACT_PRECISION)
        return newton_inverse(jax.nn.softmax(small_scores, axis=-1))

    inverse, inverse_pull = jax.vjp(
        small_kernel, land_query.astype(jnp.float32), land_key.astype(jnp.float32)
    )
    carried_docs = carried.reshape(local_heads, DOCS, LAND, HEAD_DIM)
    mixed_low = jnp.einsum("haij,hajd->haid", inverse, carried_docs, precision=EXACT_PRECISION)
    mixed_low = mixed_low.reshape(local_heads, land_total, HEAD_DIM).astype(jnp.bfloat16)
    attention = jnp.einsum("hts,hsd->thd", first_low, mixed_low, preferred_element_type=jnp.float32)
    half_width = KW // 2
    conv_float = conv_weight.astype(jnp.float32)
    padded_values = jnp.pad(values.astype(jnp.float32), ((half_width, half_width), (0, 0), (0, 0)))
    padded_docs = jnp.pad(doc_ids, (half_width, half_width), constant_values=-1)
    padded_real = jnp.pad(real_float, (half_width, half_width))
    valid_list = []
    conv_out = jnp.zeros(attention.shape, jnp.float32)
    for offset in range(KW):
        is_valid = jnp.where(
            padded_docs[offset : offset + row_len] == doc_ids,
            padded_real[offset : offset + row_len],
            0.0,
        )
        valid_list.append(is_valid)
        conv_out = conv_out + conv_float[:, offset][None, :, None] * (
            padded_values[offset : offset + row_len] * is_valid[:, None, None]
        )
    heads_out = ((attention + conv_out) * real_float[:, None, None]).astype(jnp.bfloat16)
    heads_out = heads_out.reshape(row_len, local_heads * HEAD_DIM)
    projected = lax.psum_scatter(
        jnp.dot(heads_out, w_output, preferred_element_type=jnp.float32).astype(jnp.bfloat16),
        "head",
        scatter_dimension=0,
        tiled=True,
    ).astype(jnp.float32)
    first_out, first_normed, first_inv = norm_forward(
        tokens_in.astype(jnp.float32) + projected, first_gain, first_bias
    )
    norm_low = first_out.astype(jnp.bfloat16)
    inner_pre = jnp.dot(norm_low, w_inner, preferred_element_type=jnp.float32)
    gelu_values, gelu_pull = jax.vjp(exact_gelu, inner_pre)
    inner_act = gelu_values.astype(jnp.bfloat16)
    outer_out = jnp.dot(inner_act, w_outer, preferred_element_type=jnp.float32)
    second_out, second_normed, second_inv = norm_forward(
        first_out + outer_out, second_gain, second_bias
    )
    layer_out = second_out.astype(jnp.bfloat16)
    second_grad, grad_second_gain, grad_second_bias = norm_backward(
        out_grad.astype(jnp.float32), second_normed, second_inv, second_gain
    )
    outer_low = second_grad.astype(jnp.bfloat16)
    act_grad = jnp.einsum("td,fd->tf", outer_low, w_outer, preferred_element_type=jnp.float32)
    pre_low = gelu_pull(act_grad)[0].astype(jnp.bfloat16)
    first_grad = second_grad + jnp.einsum(
        "tf,df->td", pre_low, w_inner, preferred_element_type=jnp.float32
    )
    first_in_grad, grad_first_gain, grad_first_bias = norm_backward(
        first_grad, first_normed, first_inv, first_gain
    )
    full_inner = jnp.einsum("td,tf->df", norm_low, pre_low, preferred_element_type=jnp.float32)
    full_outer = jnp.einsum("tf,td->fd", inner_act, outer_low, preferred_element_type=jnp.float32)
    grad_inner, grad_outer = (
        lax.psum_scatter(
            full_inner.astype(jnp.bfloat16), "head", scatter_dimension=1, tiled=True
        ).astype(jnp.float32),
        lax.psum_scatter(
            full_outer.astype(jnp.bfloat16), "head", scatter_dimension=0, tiled=True
        ).astype(jnp.float32),
    )
    proj_all = lax.all_gather(first_in_grad.astype(jnp.bfloat16), "head", axis=0, tiled=True)
    grad_output = jnp.einsum("tc,td->cd", heads_out, proj_all, preferred_element_type=jnp.float32)
    heads_grad = jnp.einsum("td,cd->tc", proj_all, w_output, preferred_element_type=jnp.float32)
    heads_grad = heads_grad.astype(jnp.bfloat16).reshape(row_len, local_heads, HEAD_DIM)
    heads_grad = jnp.where(real_rows[:, None, None], heads_grad, jnp.zeros_like(heads_grad))
    mixed_grad = jnp.einsum(
        "hts,thd->hsd", first_low, heads_grad, preferred_element_type=jnp.float32
    )
    first_prob = jnp.exp(first_scores() - first_lse)
    first_weight_grad = jnp.einsum(
        "thd,hsd->hts", heads_grad, mixed_low, preferred_element_type=jnp.float32
    )
    first_score_grad = softmax_back(first_prob, first_weight_grad).astype(jnp.bfloat16)
    grad_queries = jnp.einsum(
        "hts,shd->thd", first_score_grad, land_key, preferred_element_type=jnp.float32
    )
    land_key_grad = jnp.einsum(
        "hts,thd->shd", first_score_grad, queries, preferred_element_type=jnp.float32
    )
    mixed_docs = mixed_grad.reshape(local_heads, DOCS, LAND, HEAD_DIM)
    inverse_grad = jnp.einsum(
        "haid,hajd->haij", mixed_docs, carried_docs, precision=EXACT_PRECISION
    )
    carried_low = jnp.einsum("haij,haid->hajd", inverse, mixed_docs, precision=EXACT_PRECISION)
    carried_low = carried_low.reshape(local_heads, land_total, HEAD_DIM).astype(jnp.bfloat16)
    third_prob = jnp.exp(third_scores() - third_lse)
    third_weight_grad = jnp.einsum(
        "hsd,thd->hst", carried_low, values, preferred_element_type=jnp.float32
    )
    third_score_grad = softmax_back(third_prob, third_weight_grad).astype(jnp.bfloat16)
    land_query_grad = jnp.einsum(
        "hst,thd->shd", third_score_grad, key_rows, preferred_element_type=jnp.float32
    )
    grad_keys = jnp.einsum(
        "hst,shd->thd", third_score_grad, land_query, preferred_element_type=jnp.float32
    )
    grad_values = jnp.einsum(
        "hst,hsd->thd", third_low, carried_low, preferred_element_type=jnp.float32
    )
    small_query, small_key = inverse_pull(inverse_grad)
    land_query_grad = (land_query_grad + small_query) / counts[:, None, None]
    land_key_grad = (land_key_grad + small_key) / counts[:, None, None]
    grad_queries = grad_queries + jnp.einsum(
        "ts,shd->thd", member_float, land_query_grad, precision=EXACT_PRECISION
    )
    grad_keys = grad_keys + jnp.einsum(
        "ts,shd->thd", member_float, land_key_grad, precision=EXACT_PRECISION
    )
    heads_float = heads_grad.astype(jnp.float32)
    padded_heads = jnp.pad(heads_float, ((half_width, half_width), (0, 0), (0, 0)))
    conv_back = jnp.zeros(heads_float.shape, jnp.float32)
    conv_terms = []
    for offset in range(KW):
        weighted = heads_float * valid_list[offset][:, None, None]
        conv_terms.append(jnp.sum(weighted * padded_values[offset : offset + row_len], axis=(0, 2)))
        start = 2 * half_width - offset
        shifted_valid = jnp.pad(valid_list[offset], (half_width, half_width))[
            start : start + row_len
        ]
        shifted_weighted = padded_heads[start : start + row_len] * shifted_valid[:, None, None]
        conv_back = conv_back + shifted_weighted * conv_float[:, offset][None, :, None]
    grad_conv = jnp.stack(conv_terms, axis=1)
    grad_values = grad_values + conv_back
    query_low = grad_queries.astype(jnp.bfloat16).reshape(row_len, local_heads * HEAD_DIM)
    key_low = grad_keys.astype(jnp.bfloat16).reshape(row_len, local_heads * HEAD_DIM)
    value_low = grad_values.astype(jnp.bfloat16).reshape(row_len, local_heads * HEAD_DIM)
    grad_query = qk_scale * jnp.einsum(
        "tc,tk->ck", all_tokens, query_low, preferred_element_type=jnp.float32
    )
    grad_key = qk_scale * jnp.einsum(
        "tc,tk->ck", all_tokens, key_low, preferred_element_type=jnp.float32
    )
    grad_value = jnp.einsum("tc,tk->ck", all_tokens, value_low, preferred_element_type=jnp.float32)
    scaled_part = jnp.einsum("tc,dc->td", query_low, w_query, preferred_element_type=jnp.float32)
    scaled_part = scaled_part + jnp.einsum(
        "tc,dc->td", key_low, w_key, preferred_element_type=jnp.float32
    )
    attn_input = lax.psum_scatter(
        (
            qk_scale * scaled_part
            + jnp.einsum("tc,dc->td", value_low, w_value, preferred_element_type=jnp.float32)
        ).astype(jnp.bfloat16),
        "head",
        scatter_dimension=0,
        tiled=True,
    ).astype(jnp.float32)
    input_grad = (first_in_grad + attn_input).astype(jnp.bfloat16)
    summed = lax.psum(
        (grad_query, grad_key, grad_value, grad_output, grad_conv, grad_inner, grad_outer), "batch"
    )
    norm_totals = lax.psum(
        (grad_first_gain, grad_first_bias, grad_second_gain, grad_second_bias), ("batch", "head")
    )
    return (
        layer_out,
        input_grad,
        summed[0],
        summed[1],
        summed[2],
        summed[3],
        summed[4],
        norm_totals[0],
        norm_totals[1],
        summed[5],
        summed[6],
        norm_totals[2],
        norm_totals[3],
    )


def solution(mesh):
    placed = (
        P(("batch", "head"), None),
        P("batch"),
        P("batch"),
        P("batch"),
        P(None, "head"),
        P(None, "head"),
        P(None, "head"),
        P("head", None),
        P("head", None),
        P(),
        P(),
        P(),
        P(),
        P(),
        P(),
        P(("batch", "head"), None),
    )
    return jax.shard_map(
        shards,
        mesh=mesh,
        in_specs=placed,
        out_specs=(
            P(("batch", "head"), None),
            P(("batch", "head"), None),
            P(None, "head"),
            P(None, "head"),
            P(None, "head"),
            P("head", None),
            P("head", None),
            P(),
            P(),
            P(None, "head"),
            P("head", None),
            P(),
            P(),
        ),
        check_vma=False,
    )
```

profile of v0, /device:TPU:0, one launch (start us, length us, event | category | flops | bytes accessed | tf_op | source)
XLA Modules:
  0.0 913.9 jit_solution(11133062830195507953)
XLA Ops:
  24.1 34.7 %all-gather.3.cloned.1.call-done = bf16[4096,768]{1,0:T(8,128)(2,1)} async-done(((bf16[1024,768]{1,0:T(8,128)(2,1)}), bf16[4096,768]{1,0:T(8,128)(2,1)}) %all-gather.3.cloned.1.call-update) | async-done | bytes 6291472 | tf_op jit(solution)/shard_map/all_gather | solution.py:74
  85.9 12.5 %convolution_multiply_fusion.6 = f32[3,4,64,64]{3,2,1,0:T(8,128)S(1)} fusion(f32[3,4,64,64]{3,2,1,0:T(8,128)S(1)} %convolution_multiply_fusion.7, f32[3,4,64,64]{3,2,1,0:T(8,128)S(1)} %convolution_subtract_fusion.2), kind=kOutput, calls=%fused_computation.274 | convolution fusion | flops 37797888 | bytes 589824 | tf_op jit(solution)/shard_map/jvp()/dot_general | solution.py:27
  101.8 6.7 select_reduce_fusion.1
  108.5 8.1 exponential_reduce_fusion.1
  130.2 7.4 select_reduce_fusion
  137.7 7.2 exponential_reduce_fusion
  145.5 34.2 %fusion.14 = bf16[4096,3,64]{0,2,1:T(8,128)(2,1)} fusion(bf16[3,256,64]{2,1,0:T(8,128)(2,1)S(1)} %bitcast.347, f32[4096]{0:T(1024)} %get-tuple-element.146, f32[3]{0:T(128)} %get-tuple-element.67, f32[4096]{0:T(1024)} %get-tuple-element.145, f32[3]{0:T(128)} %get-tuple-element.68, f32[4096]{0:T(1024)} %get-tuple-element.144, f32[3]{0:T(128)} %get-tuple-element.69, ...), kind=kOutput, calls=%fused_computation.78 | convolution fusion | flops 492306432 | bytes 20611468 | tf_op jit(solution)/shard_map/hts,hsd->thd/dot_general | solution.py:139
  179.8 6.0 convolution_convert_fusion
  185.9 58.4 %reduce-scatter.5.cloned.1.call-done = bf16[1024,768]{1,0:T(8,128)(2,1)} async-done(((bf16[4096,768]{1,0:T(8,128)(2,1)}), bf16[1024,768]{1,0:T(8,128)(2,1)}) %reduce-scatter.5.cloned.1.call-update) | async-done | bytes 1572880 | tf_op jit(solution)/shard_map/reduce_scatter | solution.py:159
  247.2 37.5 %multiply_convert_fusion.2 = (bf16[1024,3072]{1,0:T(8,128)(2,1)S(1)}, f32[1024,3072]{1,0:T(8,128)}, f32[1024,3072]{1,0:T(8,128)}) fusion(bf16[768,3072]{1,0:T(8,128)(2,1)} %param.27, f32[768]{0:T(1024)S(1)} %copy-done.141, f32[768]{0:T(1024)S(1)} %copy-done.122, f32[1024]{0:T(1024)S(1)} %add_rsqrt_fusion.1, f32[1024]{0:T(1024)S(1)} %broadcast_multiply_fusion.5, ...), kind=kOutput, calls=%fused_computation.42 | convolution fusion | flops 5042601984 | bytes 39335936 | tf_op jit(solution)/shard_map/dot_general | solution.py:169
  296.2 17.6 %add_convert_fusion.1 = bf16[1024,3072]{1,0:T(8,128)(2,1)} fusion(f32[1024,3072]{1,0:T(8,128)} %get-tuple-element.111, f32[1024,3072]{1,0:T(8,128)} %get-tuple-element.155, bf16[3072,768]{1,0:T(8,128)(2,1)} %param.28, bf16[1024,768]{1,0:T(8,128)(2,1)} %param.31, f32[1024,768]{1,0:T(8,128)} %copy-done.26, f32[1024]{0:T(1024)S(1)} %broadcast_multiply_fusion.2, ...), kind=kOutput, calls=%fused_computation.41 | convolution fusion | flops 4882956288 | bytes 40913920 | tf_op jit(solution)/shard_map/td,fd->tf/dot_general | solution.py:181
  313.7 12.2 %multiply_reduce_fusion.2 = (f32[768]{0:T(1024)}, f32[1024]{0:T(1024)S(1)}, f32[1024]{0:T(1024)S(1)}, f32[768]{0:T(1024)}, f32[1024,768]{1,0:T(8,128)S(1)}) fusion(f32[1024]{0:T(1024)S(1)} %add_rsqrt_fusion.1, f32[1024]{0:T(1024)S(1)} %broadcast_multiply_fusion.5, bf16[1024,768]{1,0:T(8,128)(2,1)S(1)} %copy-done.10, bf16[1024,768]{1,0:T(8,128)(2,1)S(1)} %copy-done.6, ...), kind=kOutput, calls=%fused_computation.186 | convolution fusion | flops 4848349184 | bytes 22065152 | tf_op jit(solution)/shard_map/tf,df->td/dot_general | solution.py:183
  329.9 12.1 %convolution_convert_fusion.1 = bf16[3072,768]{1,0:T(8,128)(2,1)} fusion(bf16[1024,3072]{1,0:T(8,128)(2,1)} %copy-done.142, bf16[1024,768]{1,0:T(8,128)(2,1)} %param.31, f32[1024,768]{1,0:T(8,128)} %copy-done.26, f32[1024]{0:T(1024)S(1)} %broadcast_multiply_fusion.2, f32[1024]{0:T(1024)S(1)} %broadcast_multiply_fusion.3, f32[768]{0:T(1024)S(1)} %copy-done.136, ...), kind=kOutput, calls=%fused_computation.76 | convolution fusion | flops 4841275392 | bytes 15748096 | tf_op jit(solution)/shard_map/tf,td->fd/dot_general | solution.py:190
  366.0 10.2 %convolution_convert_fusion.2 = bf16[768,3072]{1,0:T(8,128)(2,1)} fusion(bf16[1024,3072]{1,0:T(8,128)(2,1)} %add_convert_fusion.1, f32[768]{0:T(1024)S(1)} %copy-done.141, f32[768]{0:T(1024)S(1)} %copy-done.122, bf16[1024,768]{1,0:T(8,128)(2,1)S(1)} %copy-done.10, bf16[1024,768]{1,0:T(8,128)(2,1)S(1)} %copy-done.6, f32[1024]{0:T(1024)S(1)} %add_rsqrt_fusion.1, ...), kind=kOutput, calls=%fused_computation.77 | convolution fusion | flops 4840488960 | bytes 14170112 | tf_op jit(solution)/shard_map/td,tf->df/dot_general | solution.py:189
  377.0 6.1 multiply_reduce_fusion.3
  383.1 9.0 fusion.175
  426.8 8.7 multiply_reduce_fusion.1
  445.6 10.8 %multiply_reduce_fusion = (f32[3,256]{1,0:T(4,128)S(1)}, f32[3,256,4096]{2,1,0:T(8,128)}) fusion(f32[3,256,4096]{2,1,0:T(8,128)} %get-tuple-element.152, f32[3,256]{1,0:T(4,128)S(1)} %copy-done.111, pred[256,4096]{1,0:T(8,128)(4,1)S(1)} %copy-done.5, bf16[3,256,64]{2,1,0:T(8,128)(2,1)S(1)} %bitcast.343, bf16[4096,3,64]{0,2,1:T(8,128)(2,1)} %bitcast.328), kind=kOutput, calls=%fused_computation.38 | convolution fusion | flops 415235328 | bytes 27891712 | tf_op jit(solution)/shard_map/hsd,thd->hst/dot_general | solution.py:225
  458.2 10.2 %multiply_convert_fusion.1 = bf16[3,4096,256]{1,2,0:T(8,128)(2,1)S(1)} fusion(f32[3,4096,256]{1,2,0:T(8,128)} %get-tuple-element.166, f32[3,4096,256]{1,2,0:T(8,128)} %get-tuple-element.154, f32[3,4096]{1,0:T(4,128)S(1)} %copy-done.109, f32[3,4096]{1,0:T(4,128)S(1)} %copy-done.95, pred[4096,256]{0,1:T(8,128)(4,1)} %broadcast_compare_fusion), kind=kLoop, calls=%fused_computation.39 | loop fusion | flops 15728640 | bytes 32604160 | tf_op jit(solution)/shard_map/convert_element_type | solution.py:211
  470.5 7.5 multiply_convert_fusion
  480.1 5.9 fusion.24
  488.1 5.9 fusion.26
  496.7 6.5 fusion.295
  503.1 6.3 fusion.294
  511.4 58.6 %fusion.17 = bf16[4096,3,64]{0,2,1:T(8,128)(2,1)S(1)} fusion(bf16[3,256,64]{2,1,0:T(8,128)(2,1)S(1)} %bitcast.344, f32[4096,3,64]{0,2,1:T(8,128)} %fusion.270, f32[4096]{0:T(1024)} %get-tuple-element.171, f32[4096]{0:T(1024)} %get-tuple-element.172, f32[4096]{0:T(1024)} %get-tuple-element.173, f32[4096]{0:T(1024)} %get-tuple-element.174, ...), kind=kOutput, calls=%fused_computation.81 | convolution fusion | flops 492306432 | bytes 20569484 | tf_op jit(solution)/shard_map/hst,hsd->thd/dot_general | solution.py:235
  571.2 12.4 %add_convert_fusion = bf16[4096,768]{1,0:T(8,128)(2,1)} fusion(f32[4096,768]{1,0:T(8,128)} %fusion.294, f32[4096,768]{1,0:T(8,128)} %fusion.295, bf16[4096,192]{0,1:T(8,128)(2,1)S(1)} %bitcast.337, bf16[768,192]{0,1:T(8,128)(2,1)S(1)} %copy-done.104), kind=kOutput, calls=%fused_computation.36 | convolution fusion | flops 1220542464 | bytes 33325056 | tf_op jit(solution)/shard_map/tc,dc->td/dot_general | solution.py:279
  584.3 40.5 %all-reduce.36 = (f32[768]{0:T(1024)}, f32[768]{0:T(1024)}, f32[768]{0:T(1024)}, f32[768]{0:T(1024)}) all-reduce(f32[768]{0:T(1024)S(1)} %copy-done.137, f32[768]{0:T(1024)S(1)} %copy-done.138, f32[768]{0:T(1024)S(1)} %copy-done.124, f32[768]{0:T(1024)S(1)} %copy-done.125), channel_id=1, replica_groups=mesh['batch'=8,'head'=4] {'batch','head'}, use_global_device_ids=true, to_apply=%region_62.63 | all-reduce | flops 3072 | bytes 24576 | tf_op jit(solution)/shard_map/psum | solution.py:289
  624.9 8.3 fusion.117
  633.8 8.3 fusion.115
  658.2 8.3 fusion.113
  668.6 9.2 %fusion.111 = (f32[3]{0:T(128)}, f32[3]{0:T(128)}, f32[3]{0:T(128)}, f32[3]{0:T(128)}, f32[3]{0:T(128)}, /*index=5*/f32[3]{0:T(128)}, f32[3]{0:T(128)}, f32[3]{0:T(128)}) fusion(f32[4096]{0:T(1024)} %get-tuple-element.143, f32[4096,3,64]{0,2,1:T(8,128)S(1)} %copy-done.2, bf16[4096,3,64]{0,2,1:T(8,128)(2,1)} %bitcast.320, pred[4096]{0:T(1024)(128)(4,1)S(1)} %copy-done.91, ...), kind=kLoop, calls=%fused_computation.179 | loop fusion | flops 20447208 | bytes 4853856 | tf_op jit(solution)/shard_map/reduce_sum | solution.py:253
  685.5 209.9 %all-reduce.43 = (f32[3,33]{1,0:T(4,128)}, f32[768,768]{1,0:T(8,128)}, f32[768,768]{1,0:T(8,128)}) all-reduce(f32[3,33]{1,0:T(4,128)S(1)} %stack.135, bf16[768,768]{1,0:T(8,128)(2,1)} %reduce-scatter.9.cloned.1.call-done, bf16[768,768]{1,0:T(8,128)(2,1)} %reduce-scatter.11.cloned.1.call-done), channel_id=1, replica_groups=mesh['batch'=8,'head'=4] {'batch'}, use_global_device_ids=true, to_apply=%region_60.61 | all-reduce | flops 1179747 | bytes 7078680 | tf_op jit(solution)/shard_map/psum | solution.py:286
  (535 shorter events, 199.4 us)
Async XLA Ops:
  7.2 172.6 %copy-start = (bf16[192,768]{1,0:T(8,128)(2,1)S(1)}, bf16[192,768]{1,0:T(8,128)(2,1)}, u32[]{:S(2)}) copy-start(bf16[192,768]{1,0:T(8,128)(2,1)} %param.23) | copy-start | bytes 884740
  7.2 51.5 %copy-start.107 = (bf16[768,192]{0,1:T(8,128)(2,1)S(1)}, bf16[768,192]{0,1:T(8,128)(2,1)}, u32[]{:S(2)}) copy-start(bf16[768,192]{0,1:T(8,128)(2,1)} %param.20) | copy-start | bytes 884740
  7.2 51.5 %all-gather.3.cloned.1.call-start = ((), (), s32[]{:S(2)}) async-start(), calls=%async_computation.4 | async-start | bytes 7864320 | tf_op jit(solution)/shard_map/all_gather | solution.py:74
  8.0 236.4 %reduce-scatter.5.cloned.1.call-start = ((), (), s32[]{:S(2)}) async-start(), calls=%async_computation.5 | async-start | bytes 7864320 | tf_op jit(solution)/shard_map/reduce_scatter | solution.py:159
  10.6 88.6 %copy-start.44 = (f32[64,64]{1,0:T(8,128)}, f32[64,64]{1,0:T(8,128)S(1)}, u32[]{:S(2)}) copy-start(f32[64,64]{1,0:T(8,128)S(1)} %get-tuple-element.169) | copy-start | bytes 49156
  11.4 56.1 %copy-start.90 = (pred[4096]{0:T(1024)(128)(4,1)}, pred[4096]{0:T(1024)(128)(4,1)S(1)}, u32[]{:S(2)}) copy-start(pred[4096]{0:T(1024)(128)(4,1)S(1)} %get-tuple-element.113) | copy-start | bytes 12292
  11.4 134.1 %copy-start.99 = (f32[4096]{0:T(1024)}, f32[4096]{0:T(1024)S(1)}, u32[]{:S(2)}) copy-start(f32[4096]{0:T(1024)S(1)} %get-tuple-element.112) | copy-start | bytes 49156
  12.1 55.3 %copy-start.96 = (s32[4096]{0:T(1024)}, s32[4096]{0:T(1024)S(1)}, u32[]{:S(2)}) copy-start(s32[4096]{0:T(1024)S(1)} %multiply_add_fusion.1) | copy-start | bytes 49156
  13.6 55.3 %copy-start.120 = (f32[256]{0:T(256)}, f32[256]{0:T(256)S(1)}, u32[]{:S(2)}) copy-start(f32[256]{0:T(256)S(1)} %convert_reduce_fusion.1) | copy-start | bytes 3076
  24.0 77.7 %copy-start.4 = (pred[256,4096]{1,0:T(8,128)(4,1)}, pred[256,4096]{1,0:T(8,128)(4,1)S(1)}, u32[]{:S(2)}) copy-start(pred[256,4096]{1,0:T(8,128)(4,1)S(1)} %compare_and_fusion) | copy-start | bytes 3145732
  68.9 61.3 %copy-start.75 = (bf16[256,3,64]{0,2,1:T(8,128)(2,1)}, bf16[256,3,64]{0,2,1:T(8,128)(2,1)S(1)}, u32[]{:S(2)}) copy-start(bf16[256,3,64]{0,2,1:T(8,128)(2,1)S(1)} %get-tuple-element.147) | copy-start | bytes 294916
  185.8 58.5 %copy-start.6 = (bf16[1024,768]{1,0:T(8,128)(2,1)S(1)}, bf16[1024,768]{1,0:T(8,128)(2,1)}, u32[]{:S(2)}) copy-start(bf16[1024,768]{1,0:T(8,128)(2,1)} %param.16) | copy-start | bytes 4718596
  185.8 61.3 %copy-start.122 = (f32[768]{0:T(1024)S(1)}, f32[768]{0:T(1024)}, u32[]{:S(2)}) copy-start(f32[768]{0:T(1024)} %param.25) | copy-start | bytes 9220
  185.8 61.3 %copy-start.141 = (f32[768]{0:T(1024)S(1)}, f32[768]{0:T(1024)}, u32[]{:S(2)}) copy-start(f32[768]{0:T(1024)} %param.26) | copy-start | bytes 9220
  185.8 190.7 %all-gather.5.cloned.1.call-start = ((), (), s32[]{:S(2)}) async-start(), calls=%async_computation.6 | async-start | bytes 7864320 | tf_op jit(solution)/shard_map/all_gather | solution.py:199
  244.3 40.4 %slice-start.13 = ((s8[4718592]{0:T(1024)(128)(4,1)}), s8[4194304]{0:T(1024)(128)(4,1)S(1)}, s32[]{:S(2)}) async-start(s8[4718592]{0:T(1024)(128)(4,1)} %bitcast.394), calls=%async_computation.24 | async-start | bytes 8388608
  246.4 119.6 %copy-start.112 = (f32[1024]{0:T(1024)}, f32[1024]{0:T(1024)S(1)}, u32[]{:S(2)}) copy-start(f32[1024]{0:T(1024)S(1)} %broadcast_multiply_fusion.5) | copy-start | bytes 12292
  247.2 118.8 %copy-start.114 = (f32[1024]{0:T(1024)}, f32[1024]{0:T(1024)S(1)}, u32[]{:S(2)}) copy-start(f32[1024]{0:T(1024)S(1)} %add_rsqrt_fusion.1) | copy-start | bytes 12292
  247.2 37.5 %slice-start.14 = ((s8[4718592]{0:T(1024)(128)(4,1)}), s8[524288]{0:T(1024)(128)(4,1)S(1)}, s32[]{:S(2)}) async-start(s8[4718592]{0:T(1024)(128)(4,1)} %bitcast.394), calls=%async_computation.25 | async-start | bytes 1048576
  329.8 355.7 %reduce-scatter.11.cloned.1.call-start = ((), (), s32[]{:S(2)}) async-start(), calls=%async_computation.9 | async-start | bytes 5898240 | tf_op jit(solution)/shard_map/reduce_scatter | solution.py:195
  342.0 343.5 %reduce-scatter.9.cloned.1.call-start = ((), (), s32[]{:S(2)}) async-start(), calls=%async_computation.8 | async-start | bytes 5898240 | tf_op jit(solution)/shard_map/reduce_scatter | solution.py:192
  376.3 519.1 %reduce-scatter.7.cloned.1.call-start = ((), (), s32[]{:S(2)}) async-start(), calls=%async_computation.7 | async-start | bytes 7864320 | tf_op jit(solution)/shard_map/reduce_scatter | solution.py:276
  383.1 128.3 %copy-start.3 = (bf16[4096,192]{0,1:T(8,128)(2,1)}, bf16[4096,192]{0,1:T(8,128)(2,1)S(1)}, u32[]{:S(2)}) copy-start(bf16[4096,192]{0,1:T(8,128)(2,1)S(1)} %get-tuple-element.168) | copy-start | bytes 4718596
  511.4 59.8 %copy-start.104 = (bf16[768,192]{0,1:T(8,128)(2,1)S(1)}, bf16[768,192]{0,1:T(8,128)(2,1)}, u32[]{:S(2)}) copy-start(bf16[768,192]{0,1:T(8,128)(2,1)} %param.22) | copy-start | bytes 884740
  583.6 41.2 %copy-start.2 = (f32[4096,3,64]{0,2,1:T(8,128)S(1)}, f32[4096,3,64]{0,2,1:T(8,128)}, u32[]{:S(2)}) copy-start(f32[4096,3,64]{0,2,1:T(8,128)} %convert_element_type.180) | copy-start | bytes 9437188
  583.7 316.3 %all-reduce.42.cloned.1.call-start = ((), (), s32[]{:S(2)}) async-start(), calls=%async_computation.10 | async-start | bytes 4718592 | tf_op jit(solution)/shard_map/psum | solution.py:286
  668.6 226.8 %copy-start.113 = (f32[1024]{0:T(1024)S(1)}, f32[1024]{0:T(1024)}, u32[]{:S(2)}) copy-start(f32[1024]{0:T(1024)} %copy-done.112) | copy-start | bytes 12292
  668.6 226.8 %copy-start.115 = (f32[1024]{0:T(1024)S(1)}, f32[1024]{0:T(1024)}, u32[]{:S(2)}) copy-start(f32[1024]{0:T(1024)} %copy-done.114) | copy-start | bytes 12292
  668.6 226.8 %copy-start.117 = (f32[1024]{0:T(1024)S(1)}, f32[1024]{0:T(1024)}, u32[]{:S(2)}) copy-start(f32[1024]{0:T(1024)} %copy-done.116) | copy-start | bytes 12292
  668.6 226.8 %copy-start.119 = (f32[1024]{0:T(1024)S(1)}, f32[1024]{0:T(1024)}, u32[]{:S(2)}) copy-start(f32[1024]{0:T(1024)} %copy-done.118) | copy-start | bytes 12292
  668.6 226.9 %copy-start.123 = (f32[768]{0:T(1024)S(1)}, f32[768]{0:T(1024)}, u32[]{:S(2)}) copy-start(f32[768]{0:T(1024)} %param.25) | copy-start | bytes 9220
  677.8 217.6 %copy-start.7 = (bf16[1024,768]{1,0:T(8,128)(2,1)S(1)}, bf16[1024,768]{1,0:T(8,128)(2,1)}, u32[]{:S(2)}) copy-start(bf16[1024,768]{1,0:T(8,128)(2,1)} %param.16) | copy-start | bytes 4718596
  (133 other events, 876.7 us)
Sparse Core Ops, SparseCore 0:
  9.6 49.0 all-gather.2
  185.9 58.3 reduce-scatter.4
  330.0 46.4 all-gather.4
  379.0 47.8 reduce-scatter.10
  429.3 47.8 reduce-scatter.8
  583.8 59.5 reduce-scatter.6
  658.3 148.6 all-reduce.41
where the time goes:
time: 925 us; the launch traced here: 914 us
  matrix products  393 us (42%)
  blocking collectives  250 us (27%)
  other arithmetic  101 us (11%)
  waiting for transfers between devices  94.1 us (10%)
  local copies, waits for them, and re-layouts  57.7 us (6%)
  between operations  17.2 us (2%)
    psum x1, blocking collectives, shards(): lax.psum((grad_query, grad_key, grad_value, grad_output, grad_conv, grad_...  210 us
    dot_general x1, matrix products, shards(): jnp.einsum('hst,hsd->thd', third_low, carried_low, preferred_element_type...  58.6 us
    reduce_scatter x1, waiting for transfers between devices, shards(): lax.psum_scatter(jnp.dot(heads_out, w_output, preferred_element_type=jnp....  58.4 us
    psum x1, blocking collectives, shards(): lax.psum((grad_first_gain, grad_first_bias, grad_second_gain, grad_second...  40.5 us
    dot_general x1, matrix products, shards(): inner_pre = jnp.dot(norm_low, w_inner, preferred_element_type=jnp.float32)  37.5 us
    all_gather x1, waiting for transfers between devices, shards(): all_tokens = lax.all_gather(tokens_in, 'head', axis=0, tiled=True)  34.7 us
    reduce_sum x5, other arithmetic, shards(): jnp.sum(weighted * padded_values[offset:offset + row_len], axis=(0, 2))  34.2 us
    dot_general x1, matrix products, shards(): jnp.einsum('hts,hsd->thd', first_low, mixed_low, preferred_element_type=j...  34.2 us
  transfers between devices with their start and end apart: 7, of which 3 were waited for; matrix products, arithmetic and copies ran while one was open for 36% of the time, Pallas kernels for 0%

commit v1 on v0

v1 whole, which is shorter than its diff:
```python
import functools

import jax
import jax.numpy as jnp
from jax import lax
from jax.experimental import pallas as pl
from jax.experimental.pallas import tpu as pltpu
from jax.sharding import PartitionSpec as P

LAND = 64
KW = 33
HALF = KW // 2
HEAD_DIM = 64
NEWTON = 6
DOCS = 4
SEGS = DOCS * LAND
WIDE = 2 * SEGS
BLOCK = 128
CHUNK = 256
QK_SCALE = HEAD_DIM ** (-0.25)

EXACT_PRECISION = lax.Precision.HIGHEST
NEG_FILL = -1e30
NORM_EPS = 1e-05
BF = jnp.bfloat16
F32 = jnp.float32


def newton_inverse(kernel):
    square_sum = jnp.sum(kernel * kernel, axis=(-2, -1), keepdims=True)
    estimate = jnp.swapaxes(kernel, -1, -2) / square_sum
    identity = jnp.eye(kernel.shape[-1], dtype=kernel.dtype)
    for step_count in range(NEWTON):
        product = jnp.matmul(kernel, estimate, precision=EXACT_PRECISION)
        factor_term = 7.0 * identity - product
        factor_term = 15.0 * identity - jnp.matmul(product, factor_term, precision=EXACT_PRECISION)
        factor_term = 13.0 * identity - jnp.matmul(product, factor_term, precision=EXACT_PRECISION)
        estimate = 0.25 * jnp.matmul(estimate, factor_term, precision=EXACT_PRECISION)
    return estimate


def norm_forward(hidden, scale_vec, shift_vec):
    center = hidden - jnp.mean(hidden, axis=-1, keepdims=True)
    inv_spread = lax.rsqrt(jnp.mean(center * center, axis=-1, keepdims=True) + NORM_EPS)
    normed = center * inv_spread
    return (normed * scale_vec + shift_vec, normed, inv_spread)


def norm_backward(upstream, normed, inv_spread, scale_vec):
    scaled = upstream * scale_vec
    result_grad = inv_spread * (
        scaled
        - jnp.mean(scaled, axis=-1, keepdims=True)
        - normed * jnp.mean(scaled * normed, axis=-1, keepdims=True)
    )
    return (result_grad, jnp.sum(upstream * normed, axis=0), jnp.sum(upstream, axis=0))


def nn(a, b):
    return lax.dot_general(a, b, (((1,), (0,)), ((), ())), preferred_element_type=F32)


def nt(a, b):
    return lax.dot_general(a, b, (((1,), (1,)), ((), ())), preferred_element_type=F32)


def tn(a, b):
    return lax.dot_general(a, b, (((0,), (0,)), ((), ())), preferred_element_type=F32)


def pair_block(ref):
    zero = jnp.zeros((HEAD_DIM, SEGS), BF)
    top = jnp.concatenate([ref[0].astype(BF), zero], axis=1)
    low = jnp.concatenate([zero, ref[1].astype(BF)], axis=1)
    return jnp.concatenate([top, low], axis=0)


def put_pair(ref, value):
    ref[0] = value[:HEAD_DIM, :SEGS].astype(ref.dtype)
    ref[1] = value[HEAD_DIM:, SEGS:].astype(ref.dtype)


def doc_bias(code):
    lane_doc = lax.broadcasted_iota(jnp.int32, (code.shape[0], SEGS), 1) // LAND
    return jnp.where(code == lane_doc, 0.0, NEG_FILL)


def rows_of(i, size, base=0):
    return pl.ds(pl.multiple_of(base + i * size, 16), size)


def third_kernel(code_ref, k_ref, v_ref, lq_ref, c_ref, st_ref, e_ref, s_scr, acc):
    steps = k_ref.shape[0] // CHUNK
    lq2 = pair_block(lq_ref)

    def scores(i, top):
        r = rows_of(i, CHUNK)
        bias = doc_bias(code_ref[r, :])
        s = nn(k_ref[r, :], lq2) + jnp.concatenate([bias, bias], axis=1)
        s_scr[r, :] = s
        return jnp.maximum(top, jnp.max(s, axis=0, keepdims=True))

    top = lax.fori_loop(0, steps, scores, jnp.full((1, WIDE), 3.0 * NEG_FILL, F32))
    acc[...] = jnp.zeros_like(acc)

    def weigh(i, total):
        r = rows_of(i, CHUNK)
        e = jnp.exp(s_scr[r, :] - top)
        low = e.astype(BF)
        e_ref[r, :] = low
        acc[...] += tn(v_ref[rows_of(i, CHUNK, HALF), :], low)
        return total + jnp.sum(e, axis=0, keepdims=True)

    total = lax.fori_loop(0, steps, weigh, jnp.zeros((1, WIDE), F32))
    put_pair(c_ref, acc[...] / total)
    st_ref[0, 0:1, :] = top[:, :SEGS]
    st_ref[1, 0:1, :] = top[:, SEGS:]
    st_ref[0, 1:2, :] = total[:, :SEGS]
    st_ref[1, 1:2, :] = total[:, SEGS:]


def skew(x, left):
    row = lax.broadcasted_iota(jnp.int32, x.shape, 0)
    lanes = x.shape[1]
    for bit in range(x.shape[0].bit_length() - 1):
        step = 1 << bit
        moved = pltpu.roll(x, lanes - step if left else step, 1)
        x = jnp.where((row & step) != 0, moved, x)
    return x


def band(w_ref, index):
    return skew(jnp.broadcast_to(w_ref[index], (BLOCK, 2 * BLOCK)), False).astype(BF)


def band_mask(code_ref, line_ref, i):
    line = line_ref[:, pl.ds(pl.multiple_of(i * BLOCK, BLOCK), 2 * BLOCK)]
    return code_ref[rows_of(i, BLOCK), :] == line


def first_kernel(code_ref, line_ref, q_ref, v_ref, lk_ref, w_ref, p_ref, conv_ref, t_scr):
    lk2 = pair_block(lk_ref)
    t_scr[0] = band(w_ref, 0)
    t_scr[1] = band(w_ref, 1)
    left_lane = lax.broadcasted_iota(jnp.int32, (BLOCK, BLOCK), 1) < HEAD_DIM

    def convolve(i, carry):
        mask = band_mask(code_ref, line_ref, i)
        window = v_ref[rows_of(i, BLOCK), :], v_ref[rows_of(i + 1, BLOCK), :]
        window = jnp.concatenate(window, axis=0)
        zero = jnp.zeros((BLOCK, 2 * BLOCK), BF)
        one = nn(jnp.where(mask, t_scr[0], zero), window)
        two = nn(jnp.where(mask, t_scr[1], zero), window)
        conv_ref[rows_of(i, BLOCK), :] = jnp.where(left_lane, one, two)
        return carry

    lax.fori_loop(0, q_ref.shape[0] // BLOCK, convolve, 0)

    def weigh(i, carry):
        r = rows_of(i, CHUNK)
        bias = doc_bias(code_ref[r, :])
        s = nn(q_ref[r, :], lk2)
        for side in (0, 1):
            cols = slice(side * SEGS, (side + 1) * SEGS)
            part = s[:, cols] + bias
            e = jnp.exp(part - jnp.max(part, axis=1, keepdims=True))
            p_ref[r, cols] = (e * (1.0 / jnp.sum(e, axis=1, keepdims=True))).astype(BF)
        return carry

    lax.fori_loop(0, q_ref.shape[0] // CHUNK, weigh, 0)


def heads_kernel(code_ref, p_ref, mix_ref, conv_ref, out_ref):
    mix2 = pair_block(mix_ref)

    def body(i, carry):
        r = rows_of(i, CHUNK)
        total = nt(p_ref[r, :], mix2) + conv_ref[r, :]
        out_ref[r, :] = jnp.where(code_ref[r, :] >= 0, total, 0.0).astype(BF)
        return carry

    lax.fori_loop(0, p_ref.shape[0] // CHUNK, body, 0)


def mixed_grad_kernel(hg_ref, p_ref, mg_ref):
    put_pair(mg_ref, tn(hg_ref[...], p_ref[...]))


def first_back_kernel(hg_ref, p_ref, q_ref, mix_ref, lk_ref, dq_ref, lkg_ref, acc):
    mix2 = pair_block(mix_ref)
    lk2 = pair_block(lk_ref)
    acc[...] = jnp.zeros_like(acc)

    def body(i, carry):
        r = rows_of(i, CHUNK)
        g = nn(hg_ref[r, :], mix2)
        parts = []
        for side in (0, 1):
            cols = slice(side * SEGS, (side + 1) * SEGS)
            p = p_ref[r, cols].astype(F32)
            gp = g[:, cols] * p
            parts.append((gp - p * jnp.sum(gp, axis=1, keepdims=True)).astype(BF))
        ds = jnp.concatenate(parts, axis=1)
        dq_ref[r, :] = nt(ds, lk2).astype(BF)
        acc[...] += tn(q_ref[r, :], ds)
        return carry

    lax.fori_loop(0, p_ref.shape[0] // CHUNK, body, 0)
    put_pair(lkg_ref, acc[...])


def conv_back_kernel(code_ref, line_ref, hgx_ref, v_ref, w_ref, back_ref, tap_ref, t_scr, acc):
    t_scr[0] = band(w_ref, 0)
    t_scr[1] = band(w_ref, 1)
    acc[...] = jnp.zeros_like(acc)
    left_lane = lax.broadcasted_iota(jnp.int32, (BLOCK, BLOCK), 1) < HEAD_DIM

    def body(i, carry):
        mask = band_mask(code_ref, line_ref, i)
        grads = hgx_ref[rows_of(i, BLOCK), :], hgx_ref[rows_of(i + 1, BLOCK), :]
        grads = jnp.concatenate(grads, axis=0)
        vals = v_ref[rows_of(i, BLOCK), :], v_ref[rows_of(i + 1, BLOCK), :]
        vals = jnp.concatenate(vals, axis=0)
        zero = jnp.zeros((BLOCK, 2 * BLOCK), BF)
        one = nn(jnp.where(mask, t_scr[0], zero), grads)
        two = nn(jnp.where(mask, t_scr[1], zero), grads)
        back_ref[rows_of(i, BLOCK), :] = jnp.where(left_lane, one, two)
        here = hgx_ref[rows_of(i, BLOCK, HALF), :]
        none = jnp.zeros_like(here)
        acc[0] += jnp.where(mask, nt(jnp.where(left_lane, here, none), vals), 0.0)
        acc[1] += jnp.where(mask, nt(jnp.where(left_lane, none, here), vals), 0.0)
        return carry

    lax.fori_loop(0, back_ref.shape[0] // BLOCK, body, 0)
    for side in (0, 1):
        tap_ref[side, 0:1, :] = jnp.sum(skew(acc[side], True), axis=0, keepdims=True)


def third_back_kernel(
    k_ref, v_ref, e_ref, f_ref, d_ref, cg_ref, lq_ref, back_ref, dk_ref, dv_ref, lqg_ref, acc
):
    cg2 = pair_block(cg_ref)
    lq2 = pair_block(lq_ref)
    factor = jnp.concatenate([f_ref[0], f_ref[1]], axis=1)
    delta = jnp.concatenate([d_ref[0], d_ref[1]], axis=1)
    acc[...] = jnp.zeros_like(acc)

    def body(i, carry):
        r = rows_of(i, CHUNK)
        h = nn(v_ref[rows_of(i, CHUNK, HALF), :], cg2)
        p = e_ref[r, :].astype(F32) * factor
        ds = (p * (h - delta)).astype(BF)
        dk_ref[r, :] = nt(ds, lq2).astype(BF)
        dv_ref[r, :] = (nt(p.astype(BF), cg2) + back_ref[r, :]).astype(BF)
        acc[...] += tn(k_ref[r, :], ds)
        return carry

    lax.fori_loop(0, e_ref.shape[0] // CHUNK, body, 0)
    put_pair(lqg_ref, acc[...])


def feed_kernel(x_ref, wi_ref, wo_ref, act_ref, slope_ref, out_ref):
    @pl.when(pl.program_id(0) == 0)
    def _():
        out_ref[...] = jnp.zeros_like(out_ref)

    def body(i, carry):
        r = rows_of(i, CHUNK)
        pre = nn(x_ref[r, :], wi_ref[...])
        cdf = 0.5 * (1.0 + lax.erf(pre * (0.5**0.5)))
        pdf = jnp.exp(-0.5 * pre * pre) * 0.3989422804014327
        act = (pre * cdf).astype(BF)
        act_ref[r, :] = act
        slope_ref[r, :] = (cdf + pre * pdf).astype(BF)
        out_ref[r, :] += nn(act, wo_ref[...])
        return carry

    lax.fori_loop(0, x_ref.shape[0] // CHUNK, body, 0)


def feed_back_kernel(
    table, og_ref, x_ref, wi_ref, wo_ref, act_ref, slope_ref, prev_ref, gi_ref, go_ref, fg_ref, pg
):
    @pl.when(pl.program_id(0) == 0)
    def _():
        fg_ref[...] = prev_ref[...]

    def body(i, carry):
        r = rows_of(i, CHUNK)
        grad = nt(og_ref[r, :], wo_ref[...])
        low = (slope_ref[r, :].astype(F32) * grad).astype(BF)
        pg[r, :] = low
        fg_ref[r, :] += nt(low, wi_ref[...])
        return carry

    lax.fori_loop(0, og_ref.shape[0] // CHUNK, body, 0)
    gi_ref[0] = tn(x_ref[...], pg[...]).astype(BF)
    go_ref[0] = tn(act_ref[...], og_ref[...]).astype(BF)


def call(body, grid, ins, outs, scratch=(), flops=0, moved=0, exps=0, limit=40):
    return pl.pallas_call(
        body,
        grid=grid,
        in_specs=[spec for spec in ins],
        out_specs=[spec for spec, _ in outs],
        out_shape=[shape for _, shape in outs],
        scratch_shapes=list(scratch),
        compiler_params=pltpu.CompilerParams(vmem_limit_bytes=limit << 20),
        cost_estimate=pl.CostEstimate(flops=flops, bytes_accessed=moved, transcendentals=exps),
    )


def whole(shape):
    return pl.BlockSpec(shape, lambda p: (0,) * len(shape))


def column(rows, width):
    return pl.BlockSpec((rows, width), lambda p: (0, p))


def heads_spec(rows, cols):
    return pl.BlockSpec((2, rows, cols), lambda p: (p, 0, 0))


def shape_of(shape, dtype):
    return jax.ShapeDtypeStruct(shape, dtype)


def shards(
    batch_size,
    tokens_in,
    doc_ids,
    landmark_ids,
    pad_mask,
    w_query,
    w_key,
    w_value,
    w_output,
    conv_weight,
    first_gain,
    first_bias,
    w_inner,
    w_outer,
    second_gain,
    second_bias,
    out_grad,
):
    groups = 4
    rows, width = tokens_in.shape
    local = w_query.shape[1]
    own = local // HEAD_DIM
    side = 2 * own
    side_cols = 2 * local
    pairs = side // 2
    ext = rows + BLOCK
    ff = w_inner.shape[1]
    me = lax.axis_index("head")
    bat = lax.axis_index("batch")
    core = me & 1

    def swap(value, bit):
        return lax.ppermute(value, "head", [(i, i ^ bit) for i in range(groups)])

    def swap_batch(value, bit):
        return lax.ppermute(value, "batch", [(i, i ^ bit) for i in range(batch_size)])

    def spread(value):
        two = swap(value, 2)
        return value, swap(value, 1), two, swap(two, 1)

    def add_low(a, b):
        return (a.astype(F32) + b.astype(F32)).astype(BF)

    def ordered(low_bit, mine, other):
        first = jnp.where(low_bit == 0, mine, other)
        second = jnp.where(low_bit == 0, other, mine)
        return jnp.concatenate([first, second], axis=0)

    def head_sum(value):
        half = value.shape[0] // 2
        mine = lax.dynamic_slice_in_dim(value, core * half, half, 0)
        other = lax.dynamic_slice_in_dim(value, (1 - core) * half, half, 0)
        mine = add_low(mine, swap(other, 1))
        mine = add_low(mine, swap(mine, 2))
        return ordered(core, mine, swap(mine, 1))

    def batch_sum(value):
        bits = [1 << b for b in range(batch_size.bit_length() - 1)]
        for bit in bits:
            half = value.shape[0] // 2
            flag = jnp.where((bat & bit) != 0, 1, 0)
            mine = lax.dynamic_slice_in_dim(value, flag * half, half, 0)
            other = lax.dynamic_slice_in_dim(value, (1 - flag) * half, half, 0)
            value = add_low(mine, swap_batch(other, bit))
        for bit in reversed(bits):
            flag = jnp.where((bat & bit) != 0, 1, 0)
            value = ordered(flag, value, swap_batch(value, bit))
        return value.astype(F32)

    def slot_sum(keep, send):
        got = add_low(keep, swap(send, 1))
        return batch_sum(add_low(got[0], swap(got[1], 2)))

    code_row = jnp.where(pad_mask > 0, doc_ids, -1)
    outside = jnp.full((BLOCK - HALF,), -2, jnp.int32)
    code_pad = jnp.concatenate([outside[:HALF], code_row, outside])
    line = lax.dynamic_slice_in_dim(code_pad, me * rows, ext, 0)
    code = line[HALF : HALF + rows].reshape(rows, 1)
    line = line.reshape(1, ext)
    segment_row = jnp.where(pad_mask > 0, doc_ids * LAND + landmark_ids, -1)
    columns = jnp.arange(SEGS, dtype=jnp.int32)
    counts = jnp.sum((segment_row[:, None] == columns[None, :]).astype(F32), axis=0)
    segment = lax.dynamic_slice_in_dim(segment_row, me * rows, rows, 0)
    member = (segment[:, None] == columns[None, :]).astype(BF)

    packed = jnp.concatenate([w_query.T, w_key.T, w_value.T], axis=0)
    got = spread(packed)
    taps = spread(conv_weight.astype(F32))
    wo_parts = spread(w_output)

    def weight_half(half, index):
        return jnp.concatenate(
            [got[2 * half + j][index * local : (index + 1) * local] for j in (0, 1)], axis=0
        )

    wq, wk, wv = ([weight_half(half, index) for half in (0, 1)] for index in range(3))
    wo = [jnp.concatenate(wo_parts[2 * half : 2 * half + 2], axis=0) for half in (0, 1)]
    tap_rows = [jnp.concatenate(taps[2 * half : 2 * half + 2], axis=0) for half in (0, 1)]

    def tap_lines(value):
        value = jnp.pad(value, ((0, 0), (0, 2 * BLOCK - KW)))
        return value.reshape(side, 1, 2 * BLOCK)

    def with_edges(value):
        before = lax.ppermute(value[-HALF:], "head", [(i, i + 1) for i in range(groups - 1)])
        after = lax.ppermute(value[:HALF], "head", [(i + 1, i) for i in range(groups - 1)])
        rest = jnp.zeros((BLOCK - 2 * HALF, value.shape[1]), value.dtype)
        return jnp.concatenate([before, value, after, rest], axis=0)

    tokens_ext = with_edges(tokens_in)

    land_part = tn(member, tokens_in) / counts[:, None]
    land_tokens = head_sum(land_part.astype(BF))

    queries, keys, values, land_q, land_k = [], [], [], [], []
    for half in (0, 1):
        queries.append((nt(tokens_in, wq[half]) * QK_SCALE).astype(BF))
        keys.append((nt(tokens_in, wk[half]) * QK_SCALE).astype(BF))
        values.append(nt(tokens_ext, wv[half]).astype(BF))
        for weight, target in ((wq, land_q), (wk, land_k)):
            mapped = (nt(weight[half], land_tokens) * QK_SCALE).astype(BF)
            target.append(mapped.reshape(side, HEAD_DIM, SEGS))

    third_call = call(
        third_kernel,
        (pairs,),
        [whole((rows, 1)), column(rows, BLOCK), column(ext, BLOCK), heads_spec(HEAD_DIM, SEGS)],
        [
            (heads_spec(HEAD_DIM, SEGS), shape_of((side, HEAD_DIM, SEGS), BF)),
            (heads_spec(8, SEGS), shape_of((side, 8, SEGS), F32)),
            (column(rows, WIDE), shape_of((rows, side * SEGS), BF)),
        ],
        [pltpu.VMEM((rows, WIDE), F32), pltpu.VMEM((BLOCK, WIDE), F32)],
        flops=4 * rows * side_cols * SEGS,
        moved=2 * rows * (side_cols * 2 + side * SEGS),
        exps=rows * side * SEGS,
    )
    carry_low, stats, third_exp = [], [], []
    for half in (0, 1):
        c_out, st_out, e_out = third_call(code, keys[half], values[half], land_q[half])
        carry_low.append(c_out)
        stats.append(st_out[:, :2])
        third_exp.append(e_out)

    def join(c_a, st_a, c_b, st_b):
        top = jnp.maximum(st_a[..., 0, :], st_b[..., 0, :])
        share_a = st_a[..., 1, :] * jnp.exp(st_a[..., 0, :] - top)
        share_b = st_b[..., 1, :] * jnp.exp(st_b[..., 0, :] - top)
        total = share_a + share_b
        joined = (
            c_a.astype(F32) * share_a[..., None, :] + c_b.astype(F32) * share_b[..., None, :]
        ) / total[..., None, :]
        return joined, jnp.stack([top, total], axis=-2)

    c_keep = jnp.stack([carry_low[0][:own], carry_low[1][:own]])
    c_send = jnp.stack([carry_low[0][own:], carry_low[1][own:]])
    st_keep = jnp.stack([stats[0][:own], stats[1][:own]])
    st_send = jnp.stack([stats[0][own:], stats[1][own:]])
    c_join, st_join = join(c_keep, st_keep, swap(c_send, 1), swap(st_send, 1))
    c_far, st_far = swap(c_join[1].astype(BF), 2), swap(st_join[1], 2)
    carried, st_all = join(c_join[0], st_join[0], c_far, st_far)
    third_lse = st_all[:, 0] + jnp.log(st_all[:, 1])

    def small_kernel(q_t, k_t):
        q_docs = q_t.reshape(own, HEAD_DIM, DOCS, LAND)
        k_docs = k_t.reshape(own, HEAD_DIM, DOCS, LAND)
        small_scores = jnp.einsum("hdai,hdaj->haij", q_docs, k_docs, precision=EXACT_PRECISION)
        return newton_inverse(jax.nn.softmax(small_scores, axis=-1))

    inverse, inverse_pull = jax.vjp(
        small_kernel, land_q[0][:own].astype(F32), land_k[0][:own].astype(F32)
    )
    carried_docs = carried.reshape(own, HEAD_DIM, DOCS, LAND)
    mixed_own = jnp.einsum("haij,hdaj->hdai", inverse, carried_docs, precision=EXACT_PRECISION)
    mixed_own = mixed_own.reshape(own, HEAD_DIM, SEGS).astype(BF)

    def spread_halves(value):
        parts = spread(value)
        return [jnp.concatenate(parts[2 * half : 2 * half + 2], axis=0) for half in (0, 1)]

    mixed = spread_halves(mixed_own)
    lse_all = spread_halves(third_lse)

    first_call = call(
        first_kernel,
        (pairs,),
        [
            whole((rows, 1)),
            whole((1, ext)),
            column(rows, BLOCK),
            column(ext, BLOCK),
            heads_spec(HEAD_DIM, SEGS),
            heads_spec(1, 2 * BLOCK),
        ],
        [
            (column(rows, WIDE), shape_of((rows, side * SEGS), BF)),
            (column(rows, BLOCK), shape_of((rows, side_cols), F32)),
        ],
        [pltpu.VMEM((2, BLOCK, 2 * BLOCK), BF)],
        flops=4 * rows * side_cols * SEGS,
        moved=2 * rows * (side_cols * 4 + side * SEGS),
        exps=rows * side * SEGS,
    )
    heads_call = call(
        heads_kernel,
        (pairs,),
        [whole((rows, 1)), column(rows, WIDE), heads_spec(HEAD_DIM, SEGS), column(rows, BLOCK)],
        [(column(rows, BLOCK), shape_of((rows, side_cols), BF))],
        flops=2 * rows * side_cols * SEGS,
        moved=2 * rows * (side_cols * 3 + side * SEGS),
    )
    first_low, heads_out = [], []
    for half in (0, 1):
        p_out, conv_out = first_call(
            code, line, queries[half], values[half], land_k[half], tap_lines(tap_rows[half])
        )
        first_low.append(p_out)
        heads_out.append(heads_call(code, p_out, mixed[half], conv_out)[0])

    projected = nn(heads_out[0], wo[0]) + nn(heads_out[1], wo[1])
    first_out, first_normed, first_inv = norm_forward(
        tokens_in.astype(F32) + projected, first_gain, first_bias
    )
    norm_low = first_out.astype(BF)

    block = 512 if ff % 512 == 0 else ff
    act, slope, outer_out = call(
        feed_kernel,
        (ff // block,),
        [whole((rows, width)), column(width, block), pl.BlockSpec((block, width), lambda p: (p, 0))],
        [
            (column(rows, block), shape_of((rows, ff), BF)),
            (column(rows, block), shape_of((rows, ff), BF)),
            (whole((rows, width)), shape_of((rows, width), F32)),
        ],
        flops=4 * rows * width * ff,
        moved=2 * (2 * width * ff + 2 * rows * ff + 3 * rows * width),
        exps=2 * rows * ff,
    )(norm_low, w_inner, w_outer)
    second_out, second_normed, second_inv = norm_forward(
        first_out + outer_out, second_gain, second_bias
    )
    layer_out = second_out.astype(BF)
    second_grad, grad_second_gain, grad_second_bias = norm_backward(
        out_grad.astype(F32), second_normed, second_inv, second_gain
    )
    outer_low = second_grad.astype(BF)

    share = ff // groups
    cut = share // 2

    def feed_back(slots, previous):
        table = jnp.stack([(me ^ slot) * 2 + part for slot in slots for part in (0, 1)])
        grid_spec = pltpu.PrefetchScalarGridSpec(
            num_scalar_prefetch=1,
            grid=(2 * len(slots),),
            in_specs=[
                pl.BlockSpec((rows, width), lambda p, t: (0, 0)),
                pl.BlockSpec((rows, width), lambda p, t: (0, 0)),
                pl.BlockSpec((width, cut), lambda p, t: (0, t[p])),
                pl.BlockSpec((cut, width), lambda p, t: (t[p], 0)),
                pl.BlockSpec((rows, cut), lambda p, t: (0, t[p])),
                pl.BlockSpec((rows, cut), lambda p, t: (0, t[p])),
                pl.BlockSpec((rows, width), lambda p, t: (0, 0)),
            ],
            out_specs=[
                pl.BlockSpec((1, width, cut), lambda p, t: (p // 2, 0, p % 2)),
                pl.BlockSpec((1, cut, width), lambda p, t: (p // 2, p % 2, 0)),
                pl.BlockSpec((rows, width), lambda p, t: (0, 0)),
            ],
            scratch_shapes=[pltpu.VMEM((rows, cut), BF)],
        )
        return pl.pallas_call(
            feed_back_kernel,
            grid_spec=grid_spec,
            out_shape=[
                shape_of((len(slots), width, share), BF),
                shape_of((len(slots), share, width), BF),
                shape_of((rows, width), F32),
            ],
            compiler_params=pltpu.CompilerParams(vmem_limit_bytes=48 << 20),
            cost_estimate=pl.CostEstimate(
                flops=8 * rows * width * share * len(slots),
                bytes_accessed=2 * len(slots) * share * (4 * width + 2 * rows) + 12 * rows * width,
                transcendentals=0,
            ),
        )(table, outer_low, norm_low, w_inner, w_outer, act, slope, previous)

    gi_send, go_send, first_grad = feed_back((1, 3), second_grad)
    gi_keep, go_keep, first_grad = feed_back((0, 2), first_grad)
    grad_inner = slot_sum(gi_keep, gi_send)
    grad_outer = slot_sum(go_keep, go_send)

    first_in_grad, grad_first_gain, grad_first_bias = norm_backward(
        first_grad, first_normed, first_inv, first_gain
    )
    proj_low = first_in_grad.astype(BF)

    def slots_of(parts):
        cut_rows = parts[0].shape[0] // 2
        keep = jnp.stack([part[:cut_rows] for part in parts])
        send = jnp.stack([part[cut_rows:] for part in parts])
        return keep, send

    grad_output = slot_sum(*slots_of([tn(part, proj_low).astype(BF) for part in heads_out]))
    proj_ext = with_edges(proj_low)
    real_ext = line.reshape(ext, 1) >= 0
    heads_grad_ext = [
        jnp.where(real_ext, nt(proj_ext, wo[half]), 0.0).astype(BF) for half in (0, 1)
    ]
    heads_grad = [part[HALF : HALF + rows] for part in heads_grad_ext]

    mixed_grad_call = call(
        mixed_grad_kernel,
        (pairs,),
        [column(rows, BLOCK), column(rows, WIDE)],
        [(heads_spec(HEAD_DIM, SEGS), shape_of((side, HEAD_DIM, SEGS), BF))],
        flops=2 * rows * side_cols * SEGS,
        moved=2 * rows * (side_cols + side * SEGS),
    )
    mixed_part = [mixed_grad_call(heads_grad[half], first_low[half])[0] for half in (0, 1)]

    def own_sum(parts):
        keep = jnp.stack([part[:own] for part in parts])
        send = jnp.stack([part[own:] for part in parts])
        got = keep.astype(F32) + swap(send, 1).astype(F32)
        return got[0] + swap(got[1].astype(BF), 2).astype(F32)

    mixed_grad = own_sum(mixed_part).reshape(own, HEAD_DIM, DOCS, LAND)
    inverse_grad = jnp.einsum("hdai,hdaj->haij", mixed_grad, carried_docs, precision=EXACT_PRECISION)
    carried_low = jnp.einsum("haij,hdai->hdaj", inverse, mixed_grad, precision=EXACT_PRECISION)
    carried_low = carried_low.reshape(own, HEAD_DIM, SEGS).astype(BF)
    third_delta = jnp.sum(carried_low.astype(F32) * carried, axis=1)
    carried_grad = spread_halves(carried_low)
    delta_all = spread_halves(third_delta)
    small_query, small_key = inverse_pull(inverse_grad)

    first_back_call = call(
        first_back_kernel,
        (pairs,),
        [
            column(rows, BLOCK),
            column(rows, WIDE),
            column(rows, BLOCK),
            heads_spec(HEAD_DIM, SEGS),
            heads_spec(HEAD_DIM, SEGS),
        ],
        [
            (column(rows, BLOCK), shape_of((rows, side_cols), BF)),
            (heads_spec(HEAD_DIM, SEGS), shape_of((side, HEAD_DIM, SEGS), F32)),
        ],
        [pltpu.VMEM((BLOCK, WIDE), F32)],
        flops=6 * rows * side_cols * SEGS,
        moved=2 * rows * (side_cols * 3 + side * SEGS),
    )
    conv_back_call = call(
        conv_back_kernel,
        (pairs,),
        [
            whole((rows, 1)),
            whole((1, ext)),
            column(ext, BLOCK),
            column(ext, BLOCK),
            heads_spec(1, 2 * BLOCK),
        ],
        [
            (column(rows, BLOCK), shape_of((rows, side_cols), F32)),
            (heads_spec(8, 2 * BLOCK), shape_of((side, 8, 2 * BLOCK), F32)),
        ],
        [pltpu.VMEM((2, BLOCK, 2 * BLOCK), BF), pltpu.VMEM((2, BLOCK, 2 * BLOCK), F32)],
        flops=4 * rows * side_cols * SEGS,
        moved=2 * rows * side_cols * 4,
    )
    third_back_call = call(
        third_back_kernel,
        (pairs,),
        [
            column(rows, BLOCK),
            column(ext, BLOCK),
            column(rows, WIDE),
            heads_spec(1, SEGS),
            heads_spec(1, SEGS),
            heads_spec(HEAD_DIM, SEGS),
            heads_spec(HEAD_DIM, SEGS),
            column(rows, BLOCK),
        ],
        [
            (column(rows, BLOCK), shape_of((rows, side_cols), BF)),
            (column(rows, BLOCK), shape_of((rows, side_cols), BF)),
            (heads_spec(HEAD_DIM, SEGS), shape_of((side, HEAD_DIM, SEGS), F32)),
        ],
        [pltpu.VMEM((BLOCK, WIDE), F32)],
        flops=8 * rows * side_cols * SEGS,
        moved=2 * rows * (side_cols * 6 + side * SEGS),
    )
    query_low, key_low, value_low, land_qg, land_kg, tap_grads = [], [], [], [], [], []
    for half in (0, 1):
        dq, lkg = first_back_call(
            heads_grad[half], first_low[half], queries[half], mixed[half], land_k[half]
        )
        back, tap_out = conv_back_call(
            code, line, heads_grad_ext[half], values[half], tap_lines(tap_rows[half][:, ::-1])
        )
        factor = jnp.exp(stats[half][:, 0] - lse_all[half]).reshape(side, 1, SEGS)
        dk, dv, lqg = third_back_call(
            keys[half],
            values[half],
            third_exp[half],
            factor,
            delta_all[half].reshape(side, 1, SEGS),
            carried_grad[half],
            land_q[half],
            back,
        )
        if half == 0:
            lqg = jnp.concatenate([lqg[:own] + small_query, lqg[own:]], axis=0)
            lkg = jnp.concatenate([lkg[:own] + small_key, lkg[own:]], axis=0)
        query_low.append(dq)
        key_low.append(dk)
        value_low.append(dv)
        land_qg.append(lqg.reshape(side_cols, SEGS).astype(BF))
        land_kg.append(lkg.reshape(side_cols, SEGS).astype(BF))
        tap_grads.append(tap_out[:, 0, :KW])

    def weight_grad(lows, lands, factor):
        parts = []
        for half in (0, 1):
            part = tn(lows[half], tokens_in)
            if lands is not None:
                part = part + nn(lands[half], land_tokens)
            parts.append((part * factor).astype(BF))
        return slot_sum(*slots_of(parts)).T

    grad_value = weight_grad(value_low, None, 1.0)
    grad_key = weight_grad(key_low, land_kg, QK_SCALE)
    grad_query = weight_grad(query_low, land_qg, QK_SCALE)

    land_back = sum(tn(land_qg[half], wq[half]) + tn(land_kg[half], wk[half]) for half in (0, 1))
    land_back = head_sum((QK_SCALE * land_back / counts[:, None]).astype(BF))
    scaled = sum(nn(query_low[half], wq[half]) + nn(key_low[half], wk[half]) for half in (0, 1))
    plain = sum(nn(value_low[half], wv[half]) for half in (0, 1))
    input_grad = (first_in_grad + QK_SCALE * scaled + plain + nn(member, land_back)).astype(BF)

    tap_keep = jnp.stack([part[:own] for part in tap_grads])
    tap_send = jnp.stack([part[own:] for part in tap_grads])
    tap_got = tap_keep + swap(tap_send, 1)
    tap_own = tap_got[0] + swap(tap_got[1], 2)
    norms = jnp.stack([grad_first_gain, grad_first_bias, grad_second_gain, grad_second_bias])
    for bit in (1, 2):
        norms = norms + swap(norms, bit)
    small = jnp.concatenate([norms, jnp.pad(tap_own, ((0, 0), (0, width - KW)))], axis=0)
    for b in range(batch_size.bit_length() - 1):
        small = small + swap_batch(small, 1 << b)
    return (
        layer_out,
        input_grad,
        grad_query,
        grad_key,
        grad_value,
        grad_output,
        small[4 : 4 + own, :KW],
        small[0],
        small[1],
        grad_inner,
        grad_outer,
        small[2],
        small[3],
    )


def solution(mesh):
    tokens = P(("batch", "head"), None)
    row = P("batch")
    cols = P(None, "head")
    lines = P("head", None)
    rep = P()
    return jax.shard_map(
        functools.partial(shards, mesh.shape["batch"]),
        mesh=mesh,
        in_specs=(
            tokens, row, row, row, cols, cols, cols, lines, lines,
            rep, rep, rep, rep, rep, rep, tokens,
        ),
        out_specs=(
            tokens, tokens, cols, cols, cols, lines, lines, rep, rep, cols, lines, rep, rep,
        ),
        check_vma=False,
    )
```

time: 925 us -> 644 us (0.70)
  matrix products: 393 us -> 113 us
  blocking collectives: 250 us -> 0 us
  Pallas kernels: 0 us -> 162 us
  starting transfers between devices: 0.29 us -> 86.1 us
  waiting for transfers between devices: 94.1 us -> 162 us
  other arithmetic: 101 us -> 53.5 us
  between operations: 17.2 us -> 5.26 us
    psum x2 -> x0, blocking collectives: 250 us -> none  [the longest x1 210 us: shards(): lax.psum((grad_query, grad_key, grad_value, grad_output, grad_conv, grad_...]
    dot_general x34 -> x44, matrix products: 299 us -> 55.5 us  [the longest x13 18.1 us: nn(): lax.dot_general(a, b, (((1,), (0,)), ((), ())), preferred_element_type=F32)]
    ppermute x0 -> x92, waiting for transfers between devices: none -> 162 us  [the longest x49 91.1 us: swap(): return lax.ppermute(value, 'head', [(i, i ^ bit) for i in range(groups)])]
    pallas_call x0 -> x17, Pallas kernels: none -> 162 us  [the longest x2 47.2 us: feed_back(): pl.pallas_call(feed_back_kernel, grid_spec=grid_spec, out_shape=[shape_of...]
    ppermute x0 -> x92, starting transfers between devices: none -> 86.1 us  [the longest x39 50 us: swap_batch(): lax.ppermute(value, 'batch', [(i, i ^ bit) for i in range(batch_size)])]
    reduce_scatter x4 -> x0, waiting for transfers between devices: 58.5 us -> none  [the longest x1 58.4 us: shards(): lax.psum_scatter(jnp.dot(heads_out, w_output, preferred_element_type=jnp....]
    reduce_sum x8 -> x2, other arithmetic: 51 us -> 3.59 us  [the longest x1 1.86 us: shards(): jnp.sum((segment_row[:, None] == columns[None, :]).astype(F32), axis=0)]
    all_gather x2 -> x0, waiting for transfers between devices: 34.8 us -> none  [the longest x1 34.7 us: shards(): all_tokens = lax.all_gather(tokens_in, 'head', axis=0, tiled=True)]
  transfers between devices with their start and end apart: 7 -> 92, of which waited for: 3 -> 42; matrix products, arithmetic and copies ran while one was open for 36% -> 25% of each run, Pallas kernels for 0% -> 13%
where the time goes in v1:
time: 644 us; the launch traced here: 638 us
  waiting for transfers between devices  162 us (25%)
  Pallas kernels  162 us (25%)
  matrix products  113 us (18%)
  starting transfers between devices  86.1 us (13%)
  local copies, waits for them, and re-layouts  56.9 us (9%)
  other arithmetic  53.5 us (8%)
    ppermute x49, waiting for transfers between devices, swap(): return lax.ppermute(value, 'head', [(i, i ^ bit) for i in range(groups)])  91.1 us
    ppermute x39, waiting for transfers between devices, swap_batch(): lax.ppermute(value, 'batch', [(i, i ^ bit) for i in range(batch_size)])  71 us
    ppermute x39, starting transfers between devices, swap_batch(): lax.ppermute(value, 'batch', [(i, i ^ bit) for i in range(batch_size)])  50 us
    pallas_call x2, Pallas kernels, feed_back(): pl.pallas_call(feed_back_kernel, grid_spec=grid_spec, out_shape=[shape_of...  47.2 us
    unnamed x417, local copies, waits for them, and re-layouts  30.1 us
    ppermute x49, starting transfers between devices, swap(): return lax.ppermute(value, 'head', [(i, i ^ bit) for i in range(groups)])  28.8 us
    dot_general x36, matrix products, newton_inverse(): jnp.matmul(product, factor_term, precision=EXACT_PRECISION)  27.1 us
    pallas_call x2, Pallas kernels, shards(): first_call(code, line, queries[half], values[half], land_k[half], tap_lin...  25.3 us
  transfers between devices with their start and end apart: 92, of which 42 were waited for; matrix products, arithmetic and copies ran while one was open for 25% of the time, Pallas kernels for 13%

profile of v1, /device:TPU:0, one launch (start us, length us, event | category | flops | bytes accessed | tf_op | source)
XLA Modules:
  0.0 638.1 jit_solution(16977316856395053303)
XLA Ops:
  26.5 17.6 %collective-permute-done.4 = bf16[128,768]{1,0:T(8,128)(2,1)S(1)} collective-permute-done((bf16[128,768]{1,0:T(8,128)(2,1)S(1)}, bf16[128,768]{1,0:T(8,128)(2,1)S(1)}, u32[]{:S(2)}, u32[]{:S(2)}) %collective-permute-start.4) | collective-permute-done | bytes 196640 | tf_op jit(solution)/shard_map/ppermute | solution.py:363
  78.6 6.3 shard_map.256
  86.6 12.5 %shard_map.255 = (bf16[1024,1536]{1,0:T(8,128)(2,1)S(1)}, f32[1024,384]{1,0:T(8,128)S(1)}) custom-call(s32[1024,1]{1,0:T(8,128)S(1)} %copy.162.code_ref, s32[1,1152]{1,0:T(1,128)S(1)} %reshape.215.line_ref, bf16[1024,384]{1,0:T(8,128)(2,1)S(1)} %fusion.25.q_ref, bf16[1152,384]{1,0:T(8,128)(2,1)S(1)} %convolution_convert_fusion.1.v_ref, ...), custom_call_target="tpu_custom_call" | custom-call | flops 402653184 | bytes 6291456 | tf_op jit(solution)/shard_map/pallas_call | solution.py:545
  108.7 6.3 shard_map.257
  121.8 12.7 %shard_map.259 = (bf16[1024,1536]{1,0:T(8,128)(2,1)S(1)}, f32[1024,384]{1,0:T(8,128)S(1)}) custom-call(s32[1024,1]{1,0:T(8,128)S(1)} %copy-done.4, s32[1,1152]{1,0:T(1,128)S(1)} %reshape.215.line_ref, bf16[1024,384]{1,0:T(8,128)(2,1)S(1)} %fusion.28.q_ref, bf16[1152,384]{1,0:T(8,128)(2,1)S(1)} %convolution_convert_fusion.v_ref, ...), custom_call_target="tpu_custom_call" | custom-call | flops 402653184 | bytes 6291456 | tf_op jit(solution)/shard_map/pallas_call | solution.py:545
  135.9 3.5 collective-permute-done.28
  141.4 4.2 collective-permute-done.12
  171.0 20.1 %shard_map.261 = (bf16[1024,3072]{1,0:T(8,128)(2,1)}, bf16[1024,3072]{1,0:T(8,128)(2,1)}, f32[1024,768]{1,0:T(8,128)S(1)}) custom-call(bf16[1024,768]{1,0:T(8,128)(2,1)S(1)} %fusion.11.x_ref, bf16[768,3072]{1,0:T(8,128)(2,1)S(1)} %bitcast.409, bf16[3072,768]{1,0:T(8,128)(2,1)S(1)} %bitcast.411), custom_call_target="tpu_custom_call" | custom-call | flops 9663676416 | bytes 26738688 | tf_op jit(solution)/shard_map/pallas_call | solution.py:558
  200.1 23.2 %shard_map.262 = (bf16[2,768,768]{2,1,0:T(8,128)(2,1)}, bf16[2,768,768]{2,1,0:T(8,128)(2,1)}, f32[1024,768]{1,0:T(8,128)}) custom-call(s32[4]{0:T(128)S(1)} %copy-done.43, bf16[1024,768]{1,0:T(8,128)(2,1)S(1)} %get-tuple-element.96.og_ref, bf16[1024,768]{1,0:T(8,128)(2,1)S(1)} %fusion.11.x_ref, bf16[768,3072]{1,0:T(8,128)(2,1)} %wi_ref.5, ...), custom_call_target="tpu_custom_call" | custom-call | flops 9663676416 | bytes 25165824 | tf_op jit(solution)/shard_map/pallas_call | solution.py:604
  223.3 24.0 %shard_map.263 = (bf16[2,768,768]{2,1,0:T(8,128)(2,1)S(1)}, bf16[2,768,768]{2,1,0:T(8,128)(2,1)}, f32[1024,768]{1,0:T(8,128)}) custom-call(s32[4]{0:T(128)S(1)} %copy-done.42, bf16[1024,768]{1,0:T(8,128)(2,1)S(1)} %get-tuple-element.96.og_ref, bf16[1024,768]{1,0:T(8,128)(2,1)S(1)} %fusion.11.x_ref, bf16[768,3072]{1,0:T(8,128)(2,1)} %wi_ref.5, ...), custom_call_target="tpu_custom_call" | custom-call | flops 9663676416 | bytes 25165824 | tf_op jit(solution)/shard_map/pallas_call | solution.py:604
  247.3 3.9 multiply_reduce_fusion
  269.3 6.6 %shard_map.269 = (bf16[1024,384]{1,0:T(8,128)(2,1)S(1)}, f32[6,64,256]{2,1,0:T(8,128)S(1)}) custom-call(bf16[1024,384]{1,0:T(8,128)(2,1)S(1)} %slice.416.hg_ref, bf16[1024,1536]{1,0:T(8,128)(2,1)S(1)} %get-tuple-element.52.p_ref, bf16[1024,384]{1,0:T(8,128)(2,1)S(1)} %copy-done.30, bf16[6,64,256]{2,1,0:T(8,128)(2,1)S(1)} %constant_dynamic-update-slice_fusion.4.mix_ref, ...), custom_call_target="tpu_custom_call" | custom-call | flops 603979776 | bytes 5505024 | tf_op jit(solution)/shard_map/pallas_call | solution.py:729
  281.4 10.6 %shard_map.267 = (f32[1024,384]{1,0:T(8,128)S(1)}, f32[6,8,256]{2,1,0:T(8,128)S(1)}) custom-call(s32[1024,1]{1,0:T(8,128)S(1)} %copy-done.6, s32[1,1152]{1,0:T(1,128)S(1)} %reshape.215.line_ref, bf16[1152,384]{1,0:T(8,128)(2,1)S(1)} %fusion.8.hgx_ref, bf16[1152,384]{1,0:T(8,128)(2,1)S(1)} %copy-done.10, f32[6,1,256]{2,1,0:T(1,128)S(1)} %copy-done.40), custom_call_target="tpu_custom_call" | custom-call | flops 402653184 | bytes 3145728 | tf_op jit(solution)/shard_map/pallas_call | solution.py:732
  293.2 10.6 %shard_map.270 = (f32[1024,384]{1,0:T(8,128)S(1)}, f32[6,8,256]{2,1,0:T(8,128)S(1)}) custom-call(s32[1024,1]{1,0:T(8,128)S(1)} %copy-done.6, s32[1,1152]{1,0:T(1,128)S(1)} %reshape.215.line_ref, bf16[1152,384]{1,0:T(8,128)(2,1)S(1)} %fusion.9.hgx_ref, bf16[1152,384]{1,0:T(8,128)(2,1)S(1)} %copy-done.8, f32[6,1,256]{2,1,0:T(1,128)S(1)} %copy-done.41), custom_call_target="tpu_custom_call" | custom-call | flops 402653184 | bytes 3145728 | tf_op jit(solution)/shard_map/pallas_call | solution.py:732
  306.9 6.8 %shard_map.264 = (bf16[1024,384]{1,0:T(8,128)(2,1)S(1)}, f32[6,64,256]{2,1,0:T(8,128)S(1)}) custom-call(bf16[1024,384]{1,0:T(8,128)(2,1)S(1)} %slice.413.hg_ref, bf16[1024,1536]{1,0:T(8,128)(2,1)S(1)} %copy-done.2, bf16[1024,384]{1,0:T(8,128)(2,1)S(1)} %copy-done.28, bf16[6,64,256]{2,1,0:T(8,128)(2,1)S(1)} %constant_dynamic-update-slice_fusion.mix_ref, ...), custom_call_target="tpu_custom_call" | custom-call | flops 603979776 | bytes 5505024 | tf_op jit(solution)/shard_map/pallas_call | solution.py:729
  314.7 3.2 collective-permute-done.72
  332.6 3.6 collective-permute-done.25
  410.6 6.3 shard_map.268
  425.9 6.5 %shard_map.271 = (bf16[1024,384]{1,0:T(8,128)(2,1)S(1)}, bf16[1024,384]{1,0:T(8,128)(2,1)S(1)}, f32[6,64,256]{2,1,0:T(8,128)S(1)}) custom-call(bf16[1024,384]{1,0:T(8,128)(2,1)S(1)} %copy-done.32, bf16[1152,384]{1,0:T(8,128)(2,1)S(1)} %copy-done.8, bf16[1024,1536]{1,0:T(8,128)(2,1)S(1)} %copy-done.12, f32[6,1,256]{2,1,0:T(1,128)S(1)} %copy-done.39, ...), custom_call_target="tpu_custom_call" | custom-call | flops 805306368 | bytes 7864320 | tf_op jit(solution)/shard_map/pallas_call | solution.py:736
  442.1 7.8 %collective-permute-done.62 = bf16[192,768]{1,0:T(8,128)(2,1)S(1)} collective-permute-done((bf16[192,768]{1,0:T(8,128)(2,1)S(1)}, bf16[192,768]{1,0:T(8,128)(2,1)S(1)}, u32[]{:S(2)}, u32[]{:S(2)}) %collective-permute-start.62) | collective-permute-done | bytes 294944 | tf_op jit(solution)/shard_map/ppermute | solution.py:363
  451.2 5.1 collective-permute-done.63
  456.8 6.1 collective-permute-done.35
  489.2 4.1 collective-permute-done.68
  537.2 20.8 %collective-permute-done.77 = bf16[768,768]{1,0:T(8,128)(2,1)S(1)} collective-permute-done((bf16[768,768]{1,0:T(8,128)(2,1)S(1)}, bf16[768,768]{1,0:T(8,128)(2,1)S(1)}, u32[]{:S(2)}, u32[]{:S(2)}) %collective-permute-start.77) | collective-permute-done | bytes 1179680 | tf_op jit(solution)/shard_map/ppermute | solution.py:363
  559.3 15.3 %collective-permute-done.85 = bf16[768,768]{1,0:T(8,128)(2,1)S(1)} collective-permute-done((bf16[768,768]{1,0:T(8,128)(2,1)S(1)}, bf16[768,768]{1,0:T(8,128)(2,1)S(1)}, u32[]{:S(2)}, u32[]{:S(2)}) %collective-permute-start.85) | collective-permute-done | bytes 1179680 | tf_op jit(solution)/shard_map/ppermute | solution.py:363
  576.6 8.3 %collective-permute-done.86 = bf16[384,768]{1,0:T(8,128)(2,1)S(1)} collective-permute-done((bf16[384,768]{1,0:T(8,128)(2,1)S(1)}, bf16[384,768]{1,0:T(8,128)(2,1)S(1)}, u32[]{:S(2)}, u32[]{:S(2)}) %collective-permute-start.86) | collective-permute-done | bytes 589856 | tf_op jit(solution)/shard_map/ppermute | solution.py:366
  588.0 6.9 %collective-permute-done.87 = bf16[192,768]{1,0:T(8,128)(2,1)S(1)} collective-permute-done((bf16[192,768]{1,0:T(8,128)(2,1)S(1)}, bf16[192,768]{1,0:T(8,128)(2,1)S(1)}, u32[]{:S(2)}, u32[]{:S(2)}) %collective-permute-start.87) | collective-permute-done | bytes 294944 | tf_op jit(solution)/shard_map/ppermute | solution.py:366
  598.2 6.4 %collective-permute-done.88 = bf16[96,768]{1,0:T(8,128)(2,1)S(1)} collective-permute-done((bf16[96,768]{1,0:T(8,128)(2,1)S(1)}, bf16[96,768]{1,0:T(8,128)(2,1)S(1)}, u32[]{:S(2)}, u32[]{:S(2)}) %collective-permute-start.88) | collective-permute-done | bytes 147488 | tf_op jit(solution)/shard_map/ppermute | solution.py:366
  607.0 4.8 collective-permute-done.89
  612.0 4.0 collective-permute-done.82
  621.5 8.2 %collective-permute-done.83 = bf16[384,768]{1,0:T(8,128)(2,1)S(1)} collective-permute-done((bf16[384,768]{1,0:T(8,128)(2,1)S(1)}, bf16[384,768]{1,0:T(8,128)(2,1)S(1)}, u32[]{:S(2)}, u32[]{:S(2)}) %collective-permute-start.83) | collective-permute-done | bytes 589856 | tf_op jit(solution)/shard_map/ppermute | solution.py:366
  631.5 4.5 collective-permute-done.91
  (949 shorter events, 341.9 us)
Async XLA Ops:
  1.3 18.2 %collective-permute-start.15 = (f32[3,33]{1,0:T(4,128)S(1)}, f32[3,33]{1,0:T(4,128)S(1)}, u32[]{:S(2)}, u32[]{:S(2)}) collective-permute-start(f32[3,33]{1,0:T(4,128)S(1)} %convert_element_type.528), channel_id=1, source_target_pairs={{0,2},{1,3},{2,0},{3,1},{4,6},{5,7},{6,4},{7,5},{8,10},{9,11},{10,... | collective-permute-start | bytes 1196 | tf_op jit(solution)/shard_map/ppermute | solution.py:363
  4.3 40.0 %collective-permute-start.14 = (bf16[192,768]{1,0:T(8,128)(2,1)}, bf16[192,768]{1,0:T(8,128)(2,1)}, u32[]{:S(2)}, u32[]{:S(2)}) collective-permute-start(bf16[192,768]{1,0:T(8,128)(2,1)} %param.23), channel_id=1, source_target_pairs={{0,1},{1,0},{2,3},{3,2},{4,5},{5,4},{6,7},{7,6},{8,9},{9,8},{10,11... | collective-permute-start | bytes 884744 | tf_op jit(solution)/shard_map/ppermute | solution.py:363
  4.8 18.3 %collective-permute-start.19 = (bf16[192,768]{1,0:T(8,128)(2,1)}, bf16[192,768]{1,0:T(8,128)(2,1)}, u32[]{:S(2)}, u32[]{:S(2)}) collective-permute-start(bf16[192,768]{1,0:T(8,128)(2,1)} %param.23), channel_id=1, source_target_pairs={{0,2},{1,3},{2,0},{3,1},{4,6},{5,7},{6,4},{7,5},{8,10},{9,11},{10,... | collective-permute-start | bytes 884744 | tf_op jit(solution)/shard_map/ppermute | solution.py:363
  17.4 57.5 %collective-permute-start.7 = (bf16[576,768]{1,0:T(8,128)(2,1)}, bf16[576,768]{1,0:T(8,128)(2,1)}, u32[]{:S(2)}, u32[]{:S(2)}) collective-permute-start(bf16[576,768]{1,0:T(8,128)(2,1)} %pad_maximum_fusion), channel_id=1, source_target_pairs={{0,2},{1,3},{2,0},{3,1},{4,6},{5,7},{6,4},{7,5},{8,10},{9,11},{10,... | collective-permute-start | bytes 2654216 | tf_op jit(solution)/shard_map/ppermute | solution.py:363
  20.7 28.0 %collective-permute-start = (bf16[576,768]{1,0:T(8,128)(2,1)}, bf16[576,768]{1,0:T(8,128)(2,1)}, u32[]{:S(2)}, u32[]{:S(2)}) collective-permute-start(bf16[576,768]{1,0:T(8,128)(2,1)} %pad_maximum_fusion), channel_id=1, source_target_pairs={{0,1},{1,0},{2,3},{3,2},{4,5},{5,4},{6,7},{7,6},{8,9},{9,8},{10,11... | collective-permute-start | bytes 2654216 | tf_op jit(solution)/shard_map/ppermute | solution.py:363
  22.0 22.2 %collective-permute-start.4 = (bf16[128,768]{1,0:T(8,128)(2,1)S(1)}, bf16[128,768]{1,0:T(8,128)(2,1)S(1)}, u32[]{:S(2)}, u32[]{:S(2)}) collective-permute-start(bf16[128,768]{1,0:T(8,128)(2,1)S(1)} %add_convert_fusion.15), channel_id=1, source_target_pairs={{0,2},{1,3},{2,0},{3,1},{4,6},{5,7},{6,4},{7,5},{8,10},{9,11},{10,... | collective-permute-start | bytes 589832 | tf_op jit(solution)/shard_map/ppermute | solution.py:363
  23.0 53.0 %collective-permute-start.1 = (bf16[16,768]{1,0:T(8,128)(2,1)}, bf16[16,768]{1,0:T(8,128)(2,1)}, u32[]{:S(2)}, u32[]{:S(2)}) collective-permute-start(bf16[16,768]{1,0:T(8,128)(2,1)} %get-tuple-element.111), channel_id=1, source_target_pairs={{0,1},{1,2},{2,3},{4,5},{5,6},{6,7},{8,9},{9,10},{10,11},{12,13},{... | collective-permute-start | bytes 73736 | tf_op jit(solution)/shard_map/ppermute | solution.py:436
  46.5 29.5 %collective-permute-start.2 = (bf16[16,768]{1,0:T(8,128)(2,1)}, bf16[16,768]{1,0:T(8,128)(2,1)}, u32[]{:S(2)}, u32[]{:S(2)}) collective-permute-start(bf16[16,768]{1,0:T(8,128)(2,1)} %get-tuple-element.112), channel_id=1, source_target_pairs={{1,0},{2,1},{3,2},{5,4},{6,5},{7,6},{9,8},{10,9},{11,10},{13,12},{... | collective-permute-start | bytes 73736 | tf_op jit(solution)/shard_map/ppermute | solution.py:437
  74.9 28.7 %collective-permute-start.8 = (bf16[576,768]{1,0:T(8,128)(2,1)}, bf16[576,768]{1,0:T(8,128)(2,1)S(1)}, u32[]{:S(2)}, u32[]{:S(2)}) collective-permute-start(bf16[576,768]{1,0:T(8,128)(2,1)} %collective-permute-done.7), channel_id=1, source_target_pairs={{0,1},{1,0},{2,3},{3,2},{4,5},{5,4},{6,7},{7,6},{8,9},{9,8},{10,11... | collective-permute-start | bytes 2654216 | tf_op jit(solution)/shard_map/ppermute | solution.py:363
  116.9 23.6 %collective-permute-start.10 = (bf16[2,3,64,256]{3,2,1,0:T(8,128)(2,1)S(1)}, bf16[2,3,64,256]{3,2,1,0:T(8,128)(2,1)S(1)}, u32[]{:S(2)}, u32[]{:S(2)}) collective-permute-start(bf16[2,3,64,256]{3,2,1,0:T(8,128)(2,1)S(1)} %pad_maximum_fusion.20), channel_id=1, source_target_pairs={{0,1},{1,0},{2,3},{3,2},{4,5},{5,4},{6,7},{7,6},{8,9},{9,8},{10,11... | collective-permute-start | bytes 589832 | tf_op jit(solution)/shard_map/ppermute | solution.py:363
  118.1 17.6 %collective-permute-start.11 = (f32[3,2,256]{2,0,1:T(4,128)S(1)}, f32[3,2,256]{2,0,1:T(4,128)S(1)}, u32[]{:S(2)}, u32[]{:S(2)}) collective-permute-start(f32[3,2,256]{2,0,1:T(4,128)S(1)} %get-tuple-element.195), channel_id=1, source_target_pairs={{0,2},{1,3},{2,0},{3,1},{4,6},{5,7},{6,4},{7,5},{8,10},{9,11},{10,... | collective-permute-start | bytes 18440 | tf_op jit(solution)/shard_map/ppermute | solution.py:363
  261.4 178.1 %collective-permute-start.61 = (bf16[2,192,768]{2,1,0:T(8,128)(2,1)}, bf16[2,192,768]{2,1,0:T(8,128)(2,1)}, u32[]{:S(2)}, u32[]{:S(2)}) collective-permute-start(bf16[2,192,768]{2,1,0:T(8,128)(2,1)} %pad_maximum_fusion.10), channel_id=1, source_target_pairs={{0,1},{1,0},{2,3},{3,2},{4,5},{5,4},{6,7},{7,6},{8,9},{9,8},{10,11... | collective-permute-start | bytes 1769480 | tf_op jit(solution)/shard_map/ppermute | solution.py:363
  263.5 263.0 %collective-permute-start.76 = (bf16[2,768,768]{2,1,0:T(8,128)(2,1)}, bf16[2,768,768]{2,1,0:T(8,128)(2,1)}, u32[]{:S(2)}, u32[]{:S(2)}) collective-permute-start(bf16[2,768,768]{2,1,0:T(8,128)(2,1)} %get-tuple-element.76), channel_id=1, source_target_pairs={{0,1},{1,0},{2,3},{3,2},{4,5},{5,4},{6,7},{7,6},{8,9},{9,8},{10,11... | collective-permute-start | bytes 7077896 | tf_op jit(solution)/shard_map/ppermute | solution.py:363
  263.5 267.6 %collective-permute-start.84 = (bf16[2,768,768]{2,1,0:T(8,128)(2,1)}, bf16[2,768,768]{2,1,0:T(8,128)(2,1)}, u32[]{:S(2)}, u32[]{:S(2)}) collective-permute-start(bf16[2,768,768]{2,1,0:T(8,128)(2,1)} %get-tuple-element.78), channel_id=1, source_target_pairs={{0,1},{1,0},{2,3},{3,2},{4,5},{5,4},{6,7},{7,6},{8,9},{9,8},{10,11... | collective-permute-start | bytes 7077896 | tf_op jit(solution)/shard_map/ppermute | solution.py:363
  264.1 50.1 %collective-permute-start.70 = (f32[4,768]{1,0:T(4,128)S(1)}, f32[4,768]{1,0:T(4,128)S(1)}, u32[]{:S(2)}, u32[]{:S(2)}) collective-permute-start(f32[4,768]{1,0:T(4,128)S(1)} %fusion.129), channel_id=1, source_target_pairs={{0,2},{1,3},{2,0},{3,1},{4,6},{5,7},{6,4},{7,5},{8,10},{9,11},{10,... | collective-permute-start | bytes 36872 | tf_op jit(solution)/shard_map/ppermute | solution.py:363
  313.8 17.6 %collective-permute-start.24 = (bf16[2,3,64,256]{3,2,1,0:T(8,128)(2,1)S(1)}, bf16[2,3,64,256]{3,2,1,0:T(8,128)(2,1)S(1)}, u32[]{:S(2)}, u32[]{:S(2)}) collective-permute-start(bf16[2,3,64,256]{3,2,1,0:T(8,128)(2,1)S(1)} %pad_maximum_fusion.21), channel_id=1, source_target_pairs={{0,1},{1,0},{2,3},{3,2},{4,5},{5,4},{6,7},{7,6},{8,9},{9,8},{10,11... | collective-permute-start | bytes 589832 | tf_op jit(solution)/shard_map/ppermute | solution.py:363
  382.2 19.6 %collective-permute-start.30 = (f32[3,256]{1,0:T(4,128)}, f32[3,256]{1,0:T(4,128)}, u32[]{:S(2)}, u32[]{:S(2)}) collective-permute-start(f32[3,256]{1,0:T(4,128)} %multiply_reduce_fusion.7), channel_id=1, source_target_pairs={{0,2},{1,3},{2,0},{3,1},{4,6},{5,7},{6,4},{7,5},{8,10},{9,11},{10,... | collective-permute-start | bytes 9224 | tf_op jit(solution)/shard_map/ppermute | solution.py:363
  382.6 20.8 %collective-permute-start.26 = (f32[3,256]{1,0:T(4,128)}, f32[3,256]{1,0:T(4,128)}, u32[]{:S(2)}, u32[]{:S(2)}) collective-permute-start(f32[3,256]{1,0:T(4,128)} %multiply_reduce_fusion.7), channel_id=1, source_target_pairs={{0,1},{1,0},{2,3},{3,2},{4,5},{5,4},{6,7},{7,6},{8,9},{9,8},{10,11... | collective-permute-start | bytes 9224 | tf_op jit(solution)/shard_map/ppermute | solution.py:363
  401.8 22.2 %collective-permute-start.32 = (bf16[3,64,256]{2,1,0:T(8,128)(2,1)}, bf16[3,64,256]{2,1,0:T(8,128)(2,1)S(1)}, u32[]{:S(2)}, u32[]{:S(2)}) collective-permute-start(bf16[3,64,256]{2,1,0:T(8,128)(2,1)} %convert_element_type.559), channel_id=1, source_target_pairs={{0,2},{1,3},{2,0},{3,1},{4,6},{5,7},{6,4},{7,5},{8,10},{9,11},{10,... | collective-permute-start | bytes 294920 | tf_op jit(solution)/shard_map/ppermute | solution.py:363
  434.2 39.2 %collective-permute-start.53 = (bf16[2,192,768]{2,1,0:T(8,128)(2,1)}, bf16[2,192,768]{2,1,0:T(8,128)(2,1)S(1)}, u32[]{:S(2)}, u32[]{:S(2)}) collective-permute-start(bf16[2,192,768]{2,1,0:T(8,128)(2,1)} %pad_maximum_fusion.9), channel_id=1, source_target_pairs={{0,1},{1,0},{2,3},{3,2},{4,5},{5,4},{6,7},{7,6},{8,9},{9,8},{10,11... | collective-permute-start | bytes 1769480 | tf_op jit(solution)/shard_map/ppermute | solution.py:363
  435.3 14.8 %collective-permute-start.34 = (bf16[128,768]{1,0:T(8,128)(2,1)S(1)}, bf16[128,768]{1,0:T(8,128)(2,1)S(1)}, u32[]{:S(2)}, u32[]{:S(2)}) collective-permute-start(bf16[128,768]{1,0:T(8,128)(2,1)S(1)} %constant_dynamic-slice_fusion.18), channel_id=1, source_target_pairs={{0,1},{1,0},{2,3},{3,2},{4,5},{5,4},{6,7},{7,6},{8,9},{9,8},{10,11... | collective-permute-start | bytes 589832 | tf_op jit(solution)/shard_map/ppermute | solution.py:363
  449.9 26.2 %collective-permute-start.45 = (bf16[2,192,768]{2,1,0:T(8,128)(2,1)}, bf16[2,192,768]{2,1,0:T(8,128)(2,1)S(1)}, u32[]{:S(2)}, u32[]{:S(2)}) collective-permute-start(bf16[2,192,768]{2,1,0:T(8,128)(2,1)} %pad_maximum_fusion.8), channel_id=1, source_target_pairs={{0,1},{1,0},{2,3},{3,2},{4,5},{5,4},{6,7},{7,6},{8,9},{9,8},{10,11... | collective-permute-start | bytes 1769480 | tf_op jit(solution)/shard_map/ppermute | solution.py:363
  468.7 14.9 %collective-permute-start.37 = (bf16[2,192,768]{2,1,0:T(8,128)(2,1)}, bf16[2,192,768]{2,1,0:T(8,128)(2,1)}, u32[]{:S(2)}, u32[]{:S(2)}) collective-permute-start(bf16[2,192,768]{2,1,0:T(8,128)(2,1)} %pad_maximum_fusion.7), channel_id=1, source_target_pairs={{0,1},{1,0},{2,3},{3,2},{4,5},{5,4},{6,7},{7,6},{8,9},{9,8},{10,11... | collective-permute-start | bytes 1769480 | tf_op jit(solution)/shard_map/ppermute | solution.py:363
  476.1 19.7 %collective-permute-start.54 = (bf16[192,768]{1,0:T(8,128)(2,1)S(1)}, bf16[192,768]{1,0:T(8,128)(2,1)S(1)}, u32[]{:S(2)}, u32[]{:S(2)}) collective-permute-start(bf16[192,768]{1,0:T(8,128)(2,1)S(1)} %slice_bitcast_fusion.10), channel_id=1, source_target_pairs={{0,2},{1,3},{2,0},{3,1},{4,6},{5,7},{6,4},{7,5},{8,10},{9,11},{10,... | collective-permute-start | bytes 884744 | tf_op jit(solution)/shard_map/ppermute | solution.py:363
  483.2 13.9 %collective-permute-start.46 = (bf16[192,768]{1,0:T(8,128)(2,1)S(1)}, bf16[192,768]{1,0:T(8,128)(2,1)S(1)}, u32[]{:S(2)}, u32[]{:S(2)}) collective-permute-start(bf16[192,768]{1,0:T(8,128)(2,1)S(1)} %slice_bitcast_fusion.16), channel_id=1, source_target_pairs={{0,2},{1,3},{2,0},{3,1},{4,6},{5,7},{6,4},{7,5},{8,10},{9,11},{10,... | collective-permute-start | bytes 884744 | tf_op jit(solution)/shard_map/ppermute | solution.py:363
  521.4 13.8 %collective-permute-start.43 = (bf16[48,768]{1,0:T(8,128)(2,1)S(1)}, bf16[48,768]{1,0:T(8,128)(2,1)S(1)}, u32[]{:S(2)}, u32[]{:S(2)}) collective-permute-start(bf16[48,768]{1,0:T(8,128)(2,1)S(1)} %pad_maximum_fusion.30), channel_id=1, source_target_pairs={{0,8},{4,12},{8,0},{12,4},{16,24},{20,28},{24,16},{28,20},{1,9},{5... | collective-permute-start | bytes 221192 | tf_op jit(solution)/shard_map/ppermute | solution.py:366
  528.9 29.2 %collective-permute-start.77 = (bf16[768,768]{1,0:T(8,128)(2,1)S(1)}, bf16[768,768]{1,0:T(8,128)(2,1)S(1)}, u32[]{:S(2)}, u32[]{:S(2)}) collective-permute-start(bf16[768,768]{1,0:T(8,128)(2,1)S(1)} %slice_bitcast_fusion.2), channel_id=1, source_target_pairs={{0,2},{1,3},{2,0},{3,1},{4,6},{5,7},{6,4},{7,5},{8,10},{9,11},{10,... | collective-permute-start | bytes 3538952 | tf_op jit(solution)/shard_map/ppermute | solution.py:363
  533.7 40.8 %collective-permute-start.85 = (bf16[768,768]{1,0:T(8,128)(2,1)S(1)}, bf16[768,768]{1,0:T(8,128)(2,1)S(1)}, u32[]{:S(2)}, u32[]{:S(2)}) collective-permute-start(bf16[768,768]{1,0:T(8,128)(2,1)S(1)} %slice_bitcast_fusion), channel_id=1, source_target_pairs={{0,2},{1,3},{2,0},{3,1},{4,6},{5,7},{6,4},{7,5},{8,10},{9,11},{10,... | collective-permute-start | bytes 3538952 | tf_op jit(solution)/shard_map/ppermute | solution.py:363
  535.3 40.4 %collective-permute-start.44 = (bf16[96,768]{1,0:T(8,128)(2,1)S(1)}, bf16[96,768]{1,0:T(8,128)(2,1)S(1)}, u32[]{:S(2)}, u32[]{:S(2)}) collective-permute-start(bf16[96,768]{1,0:T(8,128)(2,1)S(1)} %pad_maximum_fusion.26), channel_id=1, source_target_pairs={{0,4},{4,0},{8,12},{12,8},{16,20},{20,16},{24,28},{28,24},{1,5},{5... | collective-permute-start | bytes 442376 | tf_op jit(solution)/shard_map/ppermute | solution.py:366
  558.4 17.4 %collective-permute-start.78 = (bf16[384,768]{1,0:T(8,128)(2,1)S(1)}, bf16[384,768]{1,0:T(8,128)(2,1)S(1)}, u32[]{:S(2)}, u32[]{:S(2)}) collective-permute-start(bf16[384,768]{1,0:T(8,128)(2,1)S(1)} %constant_dynamic-slice_fusion.5), channel_id=1, source_target_pairs={{0,4},{4,0},{8,12},{12,8},{16,20},{20,16},{24,28},{28,24},{1,5},{5... | collective-permute-start | bytes 1769480 | tf_op jit(solution)/shard_map/ppermute | solution.py:366
  616.1 13.6 %collective-permute-start.83 = (bf16[384,768]{1,0:T(8,128)(2,1)S(1)}, bf16[384,768]{1,0:T(8,128)(2,1)S(1)}, u32[]{:S(2)}, u32[]{:S(2)}) collective-permute-start(bf16[384,768]{1,0:T(8,128)(2,1)S(1)} %pad_maximum_fusion.11), channel_id=1, source_target_pairs={{0,4},{4,0},{8,12},{12,8},{16,20},{20,16},{24,28},{28,24},{1,5},{5... | collective-permute-start | bytes 1769480 | tf_op jit(solution)/shard_map/ppermute | solution.py:366
  619.3 16.7 %collective-permute-start.91 = (bf16[384,768]{1,0:T(8,128)(2,1)S(1)}, bf16[384,768]{1,0:T(8,128)(2,1)S(1)}, u32[]{:S(2)}, u32[]{:S(2)}) collective-permute-start(bf16[384,768]{1,0:T(8,128)(2,1)S(1)} %pad_maximum_fusion.12), channel_id=1, source_target_pairs={{0,4},{4,0},{8,12},{12,8},{16,20},{20,16},{24,28},{28,24},{1,5},{5... | collective-permute-start | bytes 1769480 | tf_op jit(solution)/shard_map/ppermute | solution.py:366
  (266 other events, 1422.4 us)

commit v2 on v1

--- a/solution.py
+++ b/solution.py
@@ -19,24 +19,10 @@
 CHUNK = 256
 QK_SCALE = HEAD_DIM ** (-0.25)
 
-EXACT_PRECISION = lax.Precision.HIGHEST
 NEG_FILL = -1e30
 NORM_EPS = 1e-05
 BF = jnp.bfloat16
 F32 = jnp.float32
-
-
-def newton_inverse(kernel):
-    square_sum = jnp.sum(kernel * kernel, axis=(-2, -1), keepdims=True)
-    estimate = jnp.swapaxes(kernel, -1, -2) / square_sum
-    identity = jnp.eye(kernel.shape[-1], dtype=kernel.dtype)
-    for step_count in range(NEWTON):
-        product = jnp.matmul(kernel, estimate, precision=EXACT_PRECISION)
-        factor_term = 7.0 * identity - product
-        factor_term = 15.0 * identity - jnp.matmul(product, factor_term, precision=EXACT_PRECISION)
-        factor_term = 13.0 * identity - jnp.matmul(product, factor_term, precision=EXACT_PRECISION)
-        estimate = 0.25 * jnp.matmul(estimate, factor_term, precision=EXACT_PRECISION)
-    return estimate
 
 
 def norm_forward(hidden, scale_vec, shift_vec):
@@ -70,8 +56,8 @@
 
 def pair_block(ref):
     zero = jnp.zeros((HEAD_DIM, SEGS), BF)
-    top = jnp.concatenate([ref[0].astype(BF), zero], axis=1)
-    low = jnp.concatenate([zero, ref[1].astype(BF)], axis=1)
+    top = jnp.concatenate([ref[0, :HEAD_DIM, :].astype(BF), zero], axis=1)
+    low = jnp.concatenate([zero, ref[1, :HEAD_DIM, :].astype(BF)], axis=1)
     return jnp.concatenate([top, low], axis=0)
 
 
@@ -89,7 +75,7 @@
     return pl.ds(pl.multiple_of(base + i * size, 16), size)
 
 
-def third_kernel(code_ref, k_ref, v_ref, lq_ref, c_ref, st_ref, e_ref, s_scr, acc):
+def third_kernel(code_ref, k_ref, v_ref, lq_ref, c_ref, e_ref, s_scr, acc):
     steps = k_ref.shape[0] // CHUNK
     lq2 = pair_block(lq_ref)
 
@@ -100,7 +86,7 @@
         s_scr[r, :] = s
         return jnp.maximum(top, jnp.max(s, axis=0, keepdims=True))
 
-    top = lax.fori_loop(0, steps, scores, jnp.full((1, WIDE), 3.0 * NEG_FILL, F32))
+    top = lax.fori_loop(0, steps, scores, jnp.full((1, WIDE), 3.0 * NEG_FILL, F32), unroll=True)
     acc[...] = jnp.zeros_like(acc)
 
     def weigh(i, total):
@@ -111,12 +97,13 @@
         acc[...] += tn(v_ref[rows_of(i, CHUNK, HALF), :], low)
         return total + jnp.sum(e, axis=0, keepdims=True)
 
-    total = lax.fori_loop(0, steps, weigh, jnp.zeros((1, WIDE), F32))
-    put_pair(c_ref, acc[...] / total)
-    st_ref[0, 0:1, :] = top[:, :SEGS]
-    st_ref[1, 0:1, :] = top[:, SEGS:]
-    st_ref[0, 1:2, :] = total[:, :SEGS]
-    st_ref[1, 1:2, :] = total[:, SEGS:]
+    total = lax.fori_loop(0, steps, weigh, jnp.zeros((1, WIDE), F32), unroll=True)
+    mean = acc[...] / total
+    for side in (0, 1):
+        cols = slice(side * SEGS, (side + 1) * SEGS)
+        c_ref[side, :HEAD_DIM, :] = mean[side * HEAD_DIM : (side + 1) * HEAD_DIM, cols]
+        low = [top[:, cols], total[:, cols], jnp.zeros((6, SEGS), F32)]
+        c_ref[side, HEAD_DIM:, :] = jnp.concatenate(low, axis=0)
 
 
 def skew(x, left):
@@ -154,7 +141,7 @@
         conv_ref[rows_of(i, BLOCK), :] = jnp.where(left_lane, one, two)
         return carry
 
-    lax.fori_loop(0, q_ref.shape[0] // BLOCK, convolve, 0)
+    lax.fori_loop(0, q_ref.shape[0] // BLOCK, convolve, 0, unroll=True)
 
     def weigh(i, carry):
         r = rows_of(i, CHUNK)
@@ -167,7 +154,7 @@
             p_ref[r, cols] = (e * (1.0 / jnp.sum(e, axis=1, keepdims=True))).astype(BF)
         return carry
 
-    lax.fori_loop(0, q_ref.shape[0] // CHUNK, weigh, 0)
+    lax.fori_loop(0, q_ref.shape[0] // CHUNK, weigh, 0, unroll=True)
 
 
 def heads_kernel(code_ref, p_ref, mix_ref, conv_ref, out_ref):
@@ -179,7 +166,7 @@
         out_ref[r, :] = jnp.where(code_ref[r, :] >= 0, total, 0.0).astype(BF)
         return carry
 
-    lax.fori_loop(0, p_ref.shape[0] // CHUNK, body, 0)
+    lax.fori_loop(0, p_ref.shape[0] // CHUNK, body, 0, unroll=True)
 
 
 def mixed_grad_kernel(hg_ref, p_ref, mg_ref):
@@ -205,7 +192,7 @@
         acc[...] += tn(q_ref[r, :], ds)
         return carry
 
-    lax.fori_loop(0, p_ref.shape[0] // CHUNK, body, 0)
+    lax.fori_loop(0, p_ref.shape[0] // CHUNK, body, 0, unroll=True)
     put_pair(lkg_ref, acc[...])
 
 
@@ -231,7 +218,7 @@
         acc[1] += jnp.where(mask, nt(jnp.where(left_lane, none, here), vals), 0.0)
         return carry
 
-    lax.fori_loop(0, back_ref.shape[0] // BLOCK, body, 0)
+    lax.fori_loop(0, back_ref.shape[0] // BLOCK, body, 0, unroll=True)
     for side in (0, 1):
         tap_ref[side, 0:1, :] = jnp.sum(skew(acc[side], True), axis=0, keepdims=True)
 
@@ -255,7 +242,7 @@
         acc[...] += tn(k_ref[r, :], ds)
         return carry
 
-    lax.fori_loop(0, e_ref.shape[0] // CHUNK, body, 0)
+    lax.fori_loop(0, e_ref.shape[0] // CHUNK, body, 0, unroll=True)
     put_pair(lqg_ref, acc[...])
 
 
@@ -275,7 +262,7 @@
         out_ref[r, :] += nn(act, wo_ref[...])
         return carry
 
-    lax.fori_loop(0, x_ref.shape[0] // CHUNK, body, 0)
+    lax.fori_loop(0, x_ref.shape[0] // CHUNK, body, 0, unroll=True)
 
 
 def feed_back_kernel(
@@ -293,9 +280,164 @@
         fg_ref[r, :] += nt(low, wi_ref[...])
         return carry
 
-    lax.fori_loop(0, og_ref.shape[0] // CHUNK, body, 0)
+    lax.fori_loop(0, og_ref.shape[0] // CHUNK, body, 0, unroll=True)
     gi_ref[0] = tn(x_ref[...], pg[...]).astype(BF)
     go_ref[0] = tn(act_ref[...], og_ref[...]).astype(BF)
+
+
+def split_low(a):
+    high = a.astype(BF)
+    return high, (a - high.astype(F32)).astype(BF)
+
+
+def spread_docs(a):
+    tall = jnp.concatenate([a] * DOCS, axis=0)
+    row = lax.broadcasted_iota(jnp.int32, tall.shape, 0) // LAND
+    lane = lax.broadcasted_iota(jnp.int32, tall.shape, 1) // LAND
+    return jnp.where(row == lane, tall, jnp.zeros_like(tall))
+
+
+def fold_docs(a):
+    lane = lax.broadcasted_iota(jnp.int32, (LAND, SEGS), 1) // LAND
+    out = a[:LAND]
+    for doc in range(1, DOCS):
+        out = jnp.where(lane == doc, a[doc * LAND : (doc + 1) * LAND], out)
+    return out
+
+
+def blocks_of(a):
+    high, low = split_low(a)
+    return spread_docs(high), spread_docs(low)
+
+
+def times(a, blocks, form=nn):
+    high, low = split_low(a)
+    both = form(jnp.concatenate([high, low], axis=0), blocks[0])
+    return both[:LAND] + (both[LAND:] + form(high, blocks[1]))
+
+
+def cross(a, b):
+    ah, al = split_low(a)
+    bh, bl = split_low(b)
+    return tn(ah, bh) + (tn(ah, bl) + tn(al, bh))
+
+
+def doc_sum(a):
+    line = jnp.sum(a, axis=0, keepdims=True)
+    lane = lax.broadcasted_iota(jnp.int32, line.shape, 1) // LAND
+    out = jnp.zeros_like(line)
+    for doc in range(DOCS):
+        part = jnp.sum(jnp.where(lane == doc, line, 0.0), axis=1, keepdims=True)
+        out = jnp.where(lane == doc, part, out)
+    return out
+
+
+def eye_docs():
+    row = lax.broadcasted_iota(jnp.int32, (LAND, SEGS), 0)
+    lane = lax.broadcasted_iota(jnp.int32, (LAND, SEGS), 1) % LAND
+    return jnp.where(row == lane, 1.0, 0.0)
+
+
+def newton_kernel(lq_ref, lk_ref, inv_ref, at_ref, save_ref):
+    heads = lq_ref.shape[0]
+    eye = eye_docs()
+    fixed, state = [], []
+    for h in range(heads):
+        scores = fold_docs(tn(lk_ref[h], lq_ref[h]))
+        e = jnp.exp(scores - jnp.max(scores, axis=0, keepdims=True))
+        at = e / jnp.sum(e, axis=0, keepdims=True)
+        at_ref[h] = at
+        blocks = blocks_of(at)
+        fixed.append(blocks)
+        state.append(times(eye, blocks, nt) / doc_sum(at * at))
+    for step in range(NEWTON):
+        x = [times(w, b) for w, b in zip(state, fixed)]
+        t2 = [15.0 * eye - times(a, blocks_of(7.0 * eye - a)) for a in x]
+        t3 = [13.0 * eye - times(a, blocks_of(b)) for a, b in zip(x, t2)]
+        for h in range(heads):
+            save_ref[step, h, 0] = state[h]
+            save_ref[step, h, 1] = x[h]
+            save_ref[step, h, 2] = t2[h]
+            save_ref[step, h, 3] = t3[h]
+        state = [0.25 * times(t, blocks_of(w)) for t, w in zip(t3, state)]
+    for h in range(heads):
+        inv_ref[h] = state[h]
+
+
+def join_packs(a, b):
+    top_a, top_b = a[HEAD_DIM : HEAD_DIM + 1], b[HEAD_DIM : HEAD_DIM + 1]
+    top = jnp.maximum(top_a, top_b)
+    share_a = a[HEAD_DIM + 1 : HEAD_DIM + 2] * jnp.exp(top_a - top)
+    share_b = b[HEAD_DIM + 1 : HEAD_DIM + 2] * jnp.exp(top_b - top)
+    total = share_a + share_b
+    mean = (a[:HEAD_DIM] * share_a + b[:HEAD_DIM] * share_b) / total
+    return mean, top, total
+
+
+def join_kernel(a_ref, b_ref, o_ref):
+    for h in range(a_ref.shape[0]):
+        mean, top, total = join_packs(a_ref[h], b_ref[h])
+        rest = jnp.zeros((6, SEGS), F32)
+        o_ref[h] = jnp.concatenate([mean, top, total, rest], axis=0)
+
+
+def three_parts(a):
+    one = a.astype(BF)
+    left = a - one.astype(F32)
+    two = left.astype(BF)
+    three = (left - two.astype(F32)).astype(BF)
+    rows = [one.astype(F32), two.astype(F32), three.astype(F32), jnp.zeros((13, a.shape[1]), F32)]
+    return jnp.concatenate(rows, axis=0).astype(BF)
+
+
+def mix_kernel(a_ref, b_ref, inv_ref, mix_ref, carried_ref):
+    for h in range(a_ref.shape[0]):
+        mean, top, total = join_packs(a_ref[h], b_ref[h])
+        carried_ref[h] = mean
+        mix_ref[h, :HEAD_DIM, :] = times(mean, blocks_of(inv_ref[h])).astype(BF)
+        mix_ref[h, HEAD_DIM:, :] = three_parts(top + jnp.log(total))
+
+
+def carry_back_kernel(a_ref, b_ref, carried_ref, inv_ref, mg_ref, cg_ref):
+    for h in range(a_ref.shape[0]):
+        mg = a_ref[h] + b_ref[h]
+        mg_ref[h] = mg
+        cg = times(mg, blocks_of(inv_ref[h]), nt).astype(BF)
+        cg_ref[h, :HEAD_DIM, :] = cg
+        delta = jnp.sum(cg.astype(F32) * carried_ref[h], axis=0, keepdims=True)
+        cg_ref[h, HEAD_DIM:, :] = three_parts(delta)
+
+
+def newton_back_kernel(mg_ref, carried_ref, at_ref, save_ref, lq_ref, lk_ref, dq_ref, dk_ref, acc):
+    heads = mg_ref.shape[0]
+    eye = eye_docs()
+    at = [at_ref[h] for h in range(heads)]
+    fixed = [blocks_of(a) for a in at]
+    grad = [fold_docs(cross(carried_ref[h], mg_ref[h])) for h in range(heads)]
+    for step in reversed(range(NEWTON)):
+        w, x, t2, t3 = ([save_ref[step, h, kind] for h in range(heads)] for kind in range(4))
+        t3g = [0.25 * times(g, blocks_of(a), nt) for g, a in zip(grad, w)]
+        wg = [0.25 * times(a, blocks_of(g)) for a, g in zip(t3, grad)]
+        t2g = [-times(a, blocks_of(g)) for a, g in zip(x, t3g)]
+        xg = [-times(g, blocks_of(a)) for g, a in zip(t3g, t2)]
+        t1g = [-times(a, blocks_of(g)) for a, g in zip(x, t2g)]
+        xg = [
+            a - times(g, blocks_of(7.0 * eye - b)) - c
+            for a, g, b, c in zip(xg, t2g, x, t1g)
+        ]
+        grad = [a + times(g, b, nt) for a, g, b in zip(wg, xg, fixed)]
+        for h in range(heads):
+            part = cross(w[h], xg[h])
+            acc[h] = part if step == NEWTON - 1 else acc[h] + part
+    for h in range(heads):
+        square = doc_sum(at[h] * at[h])
+        start = times(eye, fixed[h], nt)
+        start_grad = grad[h] / square - start * (2.0 * doc_sum(grad[h] * start) / (square * square))
+        atg = fold_docs(acc[h]) + times(eye, blocks_of(start_grad), nt)
+        sg = at[h] * (atg - jnp.sum(atg * at[h], axis=0, keepdims=True))
+        blocks = blocks_of(sg)
+        dq_ref[h] = nn(lk_ref[h], blocks[0]) + nn(lk_ref[h], blocks[1])
+        dk_ref[h] = nt(lq_ref[h], blocks[0]) + nt(lq_ref[h], blocks[1])
 
 
 def call(body, grid, ins, outs, scratch=(), flops=0, moved=0, exps=0, limit=40):
@@ -308,6 +450,16 @@
         scratch_shapes=list(scratch),
         compiler_params=pltpu.CompilerParams(vmem_limit_bytes=limit << 20),
         cost_estimate=pl.CostEstimate(flops=flops, bytes_accessed=moved, transcendentals=exps),
+    )
+
+
+def plain(body, outs, scratch=(), flops=0, moved=0, limit=40):
+    return pl.pallas_call(
+        body,
+        out_shape=list(outs),
+        scratch_shapes=list(scratch),
+        compiler_params=pltpu.CompilerParams(vmem_limit_bytes=limit << 20),
+        cost_estimate=pl.CostEstimate(flops=flops, bytes_accessed=moved, transcendentals=0),
     )
 
 
@@ -359,11 +511,13 @@
     bat = lax.axis_index("batch")
     core = me & 1
 
-    def swap(value, bit):
-        return lax.ppermute(value, "head", [(i, i ^ bit) for i in range(groups)])
-
-    def swap_batch(value, bit):
-        return lax.ppermute(value, "batch", [(i, i ^ bit) for i in range(batch_size)])
+    def swap(value, bit, name="swap"):
+        with jax.named_scope(name):
+            return lax.ppermute(value, "head", [(i, i ^ bit) for i in range(groups)])
+
+    def swap_batch(value, bit, name="swap"):
+        with jax.named_scope(name):
+            return lax.ppermute(value, "batch", [(i, i ^ bit) for i in range(batch_size)])
 
     def spread(value):
         two = swap(value, 2)
@@ -371,36 +525,32 @@
 
     def add_low(a, b):
         return (a.astype(F32) + b.astype(F32)).astype(BF)
+
+    def gate(*values):
+        return lax.optimization_barrier(values)
 
     def ordered(low_bit, mine, other):
         first = jnp.where(low_bit == 0, mine, other)
         second = jnp.where(low_bit == 0, other, mine)
         return jnp.concatenate([first, second], axis=0)
 
+    def halves(value, flag):
+        half = value.shape[0] // 2
+        mine = lax.dynamic_slice_in_dim(value, flag * half, half, 0)
+        return mine, lax.dynamic_slice_in_dim(value, (1 - flag) * half, half, 0)
+
     def head_sum(value):
-        half = value.shape[0] // 2
-        mine = lax.dynamic_slice_in_dim(value, core * half, half, 0)
-        other = lax.dynamic_slice_in_dim(value, (1 - core) * half, half, 0)
-        mine = add_low(mine, swap(other, 1))
-        mine = add_low(mine, swap(mine, 2))
+        mine, other = halves(value, core)
+        mine = mine + swap(other, 1)
+        mine = mine + swap(mine, 2)
         return ordered(core, mine, swap(mine, 1))
 
-    def batch_sum(value):
-        bits = [1 << b for b in range(batch_size.bit_length() - 1)]
-        for bit in bits:
-            half = value.shape[0] // 2
-            flag = jnp.where((bat & bit) != 0, 1, 0)
-            mine = lax.dynamic_slice_in_dim(value, flag * half, half, 0)
-            other = lax.dynamic_slice_in_dim(value, (1 - flag) * half, half, 0)
-            value = add_low(mine, swap_batch(other, bit))
-        for bit in reversed(bits):
-            flag = jnp.where((bat & bit) != 0, 1, 0)
-            value = ordered(flag, value, swap_batch(value, bit))
-        return value.astype(F32)
-
-    def slot_sum(keep, send):
-        got = add_low(keep, swap(send, 1))
-        return batch_sum(add_low(got[0], swap(got[1], 2)))
+    bits = [1 << b for b in range(batch_size.bit_length() - 1)]
+
+    def gather_heads(value):
+        got = lax.all_gather(value, "head", axis=0, tiled=False)
+        parts = [lax.dynamic_index_in_dim(got, me ^ slot, 0, False) for slot in range(groups)]
+        return [jnp.concatenate(parts[2 * half : 2 * half + 2], axis=0) for half in (0, 1)]
 
     code_row = jnp.where(pad_mask > 0, doc_ids, -1)
     outside = jnp.full((BLOCK - HALF,), -2, jnp.int32)
@@ -416,8 +566,8 @@
 
     packed = jnp.concatenate([w_query.T, w_key.T, w_value.T], axis=0)
     got = spread(packed)
-    taps = spread(conv_weight.astype(F32))
-    wo_parts = spread(w_output)
+    tap_pad = jnp.pad(conv_weight, ((0, 16 - own), (0, width - KW)))
+    out_parts = spread(jnp.concatenate([w_output, tap_pad], axis=0))
 
     def weight_half(half, index):
         return jnp.concatenate(
@@ -425,11 +575,17 @@
         )
 
     wq, wk, wv = ([weight_half(half, index) for half in (0, 1)] for index in range(3))
-    wo = [jnp.concatenate(wo_parts[2 * half : 2 * half + 2], axis=0) for half in (0, 1)]
-    tap_rows = [jnp.concatenate(taps[2 * half : 2 * half + 2], axis=0) for half in (0, 1)]
+    wo = [
+        jnp.concatenate([out_parts[2 * half + j][:local] for j in (0, 1)], axis=0)
+        for half in (0, 1)
+    ]
+    tap_rows = [
+        jnp.concatenate([out_parts[2 * half + j][local : local + own, :KW] for j in (0, 1)], axis=0)
+        for half in (0, 1)
+    ]
 
     def tap_lines(value):
-        value = jnp.pad(value, ((0, 0), (0, 2 * BLOCK - KW)))
+        value = jnp.pad(value.astype(F32), ((0, 0), (0, 2 * BLOCK - KW)))
         return value.reshape(side, 1, 2 * BLOCK)
 
     def with_edges(value):
@@ -441,7 +597,8 @@
     tokens_ext = with_edges(tokens_in)
 
     land_part = tn(member, tokens_in) / counts[:, None]
-    land_tokens = head_sum(land_part.astype(BF))
+    land_sum = head_sum(land_part)
+    land_tokens, land_rest = split_low(land_sum)
 
     queries, keys, values, land_q, land_k = [], [], [], [], []
     for half in (0, 1):
@@ -449,7 +606,8 @@
         keys.append((nt(tokens_in, wk[half]) * QK_SCALE).astype(BF))
         values.append(nt(tokens_ext, wv[half]).astype(BF))
         for weight, target in ((wq, land_q), (wk, land_k)):
-            mapped = (nt(weight[half], land_tokens) * QK_SCALE).astype(BF)
+            mapped = nt(weight[half], land_tokens) + nt(weight[half], land_rest)
+            mapped = (mapped * QK_SCALE).astype(BF)
             target.append(mapped.reshape(side, HEAD_DIM, SEGS))
 
     third_call = call(
@@ -457,8 +615,7 @@
         (pairs,),
         [whole((rows, 1)), column(rows, BLOCK), column(ext, BLOCK), heads_spec(HEAD_DIM, SEGS)],
         [
-            (heads_spec(HEAD_DIM, SEGS), shape_of((side, HEAD_DIM, SEGS), BF)),
-            (heads_spec(8, SEGS), shape_of((side, 8, SEGS), F32)),
+            (heads_spec(HEAD_DIM + 8, SEGS), shape_of((side, HEAD_DIM + 8, SEGS), F32)),
             (column(rows, WIDE), shape_of((rows, side * SEGS), BF)),
         ],
         [pltpu.VMEM((rows, WIDE), F32), pltpu.VMEM((BLOCK, WIDE), F32)],
@@ -466,51 +623,40 @@
         moved=2 * rows * (side_cols * 2 + side * SEGS),
         exps=rows * side * SEGS,
     )
-    carry_low, stats, third_exp = [], [], []
+    packs, third_exp = [], []
     for half in (0, 1):
-        c_out, st_out, e_out = third_call(code, keys[half], values[half], land_q[half])
-        carry_low.append(c_out)
-        stats.append(st_out[:, :2])
+        pack, e_out = third_call(code, keys[half], values[half], land_q[half])
+        packs.append(pack)
         third_exp.append(e_out)
 
-    def join(c_a, st_a, c_b, st_b):
-        top = jnp.maximum(st_a[..., 0, :], st_b[..., 0, :])
-        share_a = st_a[..., 1, :] * jnp.exp(st_a[..., 0, :] - top)
-        share_b = st_b[..., 1, :] * jnp.exp(st_b[..., 0, :] - top)
-        total = share_a + share_b
-        joined = (
-            c_a.astype(F32) * share_a[..., None, :] + c_b.astype(F32) * share_b[..., None, :]
-        ) / total[..., None, :]
-        return joined, jnp.stack([top, total], axis=-2)
-
-    c_keep = jnp.stack([carry_low[0][:own], carry_low[1][:own]])
-    c_send = jnp.stack([carry_low[0][own:], carry_low[1][own:]])
-    st_keep = jnp.stack([stats[0][:own], stats[1][:own]])
-    st_send = jnp.stack([stats[0][own:], stats[1][own:]])
-    c_join, st_join = join(c_keep, st_keep, swap(c_send, 1), swap(st_send, 1))
-    c_far, st_far = swap(c_join[1].astype(BF), 2), swap(st_join[1], 2)
-    carried, st_all = join(c_join[0], st_join[0], c_far, st_far)
-    third_lse = st_all[:, 0] + jnp.log(st_all[:, 1])
-
-    def small_kernel(q_t, k_t):
-        q_docs = q_t.reshape(own, HEAD_DIM, DOCS, LAND)
-        k_docs = k_t.reshape(own, HEAD_DIM, DOCS, LAND)
-        small_scores = jnp.einsum("hdai,hdaj->haij", q_docs, k_docs, precision=EXACT_PRECISION)
-        return newton_inverse(jax.nn.softmax(small_scores, axis=-1))
-
-    inverse, inverse_pull = jax.vjp(
-        small_kernel, land_q[0][:own].astype(F32), land_k[0][:own].astype(F32)
-    )
-    carried_docs = carried.reshape(own, HEAD_DIM, DOCS, LAND)
-    mixed_own = jnp.einsum("haij,hdaj->hdai", inverse, carried_docs, precision=EXACT_PRECISION)
-    mixed_own = mixed_own.reshape(own, HEAD_DIM, SEGS).astype(BF)
-
-    def spread_halves(value):
-        parts = spread(value)
-        return [jnp.concatenate(parts[2 * half : 2 * half + 2], axis=0) for half in (0, 1)]
-
-    mixed = spread_halves(mixed_own)
-    lse_all = spread_halves(third_lse)
+    docs_shape = shape_of((own, HEAD_DIM, SEGS), F32)
+    own_q, own_k = land_q[0][:own], land_k[0][:own]
+    inverse, small_t, saved = plain(
+        newton_kernel,
+        [docs_shape, docs_shape, shape_of((NEWTON, own, 4, HEAD_DIM, SEGS), F32)],
+        flops=own * NEWTON * 4 * 6 * LAND * SEGS * SEGS,
+        moved=4 * own * NEWTON * 4 * HEAD_DIM * SEGS,
+    )(own_q, own_k)
+
+    tall = HEAD_DIM + 8
+    pack_keep = jnp.concatenate([part[:own] for part in packs], axis=0)
+    pack_send = jnp.concatenate([part[own:] for part in packs], axis=0)
+    joined = plain(join_kernel, [shape_of((side, tall, SEGS), F32)], moved=12 * side * tall * SEGS)(
+        pack_keep, swap(pack_send, 1)
+    )[0]
+    mixed_own, carried = plain(
+        mix_kernel,
+        [shape_of((own, HEAD_DIM + 16, SEGS), BF), docs_shape],
+        flops=6 * own * LAND * SEGS * SEGS,
+        moved=16 * own * tall * SEGS,
+    )(joined[:own], swap(joined[own:], 2), inverse)
+    mixed = gather_heads(mixed_own)
+
+    def row_of(parts):
+        return [
+            jnp.sum(part[:, HEAD_DIM : HEAD_DIM + 3].astype(F32), axis=1, keepdims=True)
+            for part in parts
+        ]
 
     first_call = call(
         first_kernel,
@@ -535,7 +681,7 @@
     heads_call = call(
         heads_kernel,
         (pairs,),
-        [whole((rows, 1)), column(rows, WIDE), heads_spec(HEAD_DIM, SEGS), column(rows, BLOCK)],
+        [whole((rows, 1)), column(rows, WIDE), heads_spec(HEAD_DIM + 16, SEGS), column(rows, BLOCK)],
         [(column(rows, BLOCK), shape_of((rows, side_cols), BF))],
         flops=2 * rows * side_cols * SEGS,
         moved=2 * rows * (side_cols * 3 + side * SEGS),
@@ -618,22 +764,25 @@
         )(table, outer_low, norm_low, w_inner, w_outer, act, slope, previous)
 
     gi_send, go_send, first_grad = feed_back((1, 3), second_grad)
+    gi_core, go_core = swap(gi_send, 1, "inner_core"), swap(go_send, 1, "outer_core")
     gi_keep, go_keep, first_grad = feed_back((0, 2), first_grad)
-    grad_inner = slot_sum(gi_keep, gi_send)
-    grad_outer = slot_sum(go_keep, go_send)
-
+    first_grad, gi_core, go_core = gate(first_grad, gi_core, go_core)
+    inner_far = swap(add_low(gi_keep[1], gi_core[1]), 2, "inner_x")
+    outer_flags = [jnp.where((bat & bit) != 0, 1, 0) for bit in bits]
+
+    def split_rows(value, flag):
+        half = value.shape[1] // 2
+        mine = lax.dynamic_slice_in_dim(value, flag * half, half, 1)
+        return mine, lax.dynamic_slice_in_dim(value, (1 - flag) * half, half, 1)
+
+    own_keep, other_keep = split_rows(go_keep, outer_flags[0])
+    own_core, other_core = split_rows(go_core, outer_flags[0])
+    outer_near = swap_batch(add_low(other_keep, other_core), bits[0], "outer_y")
     first_in_grad, grad_first_gain, grad_first_bias = norm_backward(
         first_grad, first_normed, first_inv, first_gain
     )
     proj_low = first_in_grad.astype(BF)
 
-    def slots_of(parts):
-        cut_rows = parts[0].shape[0] // 2
-        keep = jnp.stack([part[:cut_rows] for part in parts])
-        send = jnp.stack([part[cut_rows:] for part in parts])
-        return keep, send
-
-    grad_output = slot_sum(*slots_of([tn(part, proj_low).astype(BF) for part in heads_out]))
     proj_ext = with_edges(proj_low)
     real_ext = line.reshape(ext, 1) >= 0
     heads_grad_ext = [
@@ -645,26 +794,30 @@
         mixed_grad_kernel,
         (pairs,),
         [column(rows, BLOCK), column(rows, WIDE)],
-        [(heads_spec(HEAD_DIM, SEGS), shape_of((side, HEAD_DIM, SEGS), BF))],
+        [(heads_spec(HEAD_DIM, SEGS), shape_of((side, HEAD_DIM, SEGS), F32))],
         flops=2 * rows * side_cols * SEGS,
         moved=2 * rows * (side_cols + side * SEGS),
     )
     mixed_part = [mixed_grad_call(heads_grad[half], first_low[half])[0] for half in (0, 1)]
 
-    def own_sum(parts):
-        keep = jnp.stack([part[:own] for part in parts])
-        send = jnp.stack([part[own:] for part in parts])
-        got = keep.astype(F32) + swap(send, 1).astype(F32)
-        return got[0] + swap(got[1].astype(BF), 2).astype(F32)
-
-    mixed_grad = own_sum(mixed_part).reshape(own, HEAD_DIM, DOCS, LAND)
-    inverse_grad = jnp.einsum("hdai,hdaj->haij", mixed_grad, carried_docs, precision=EXACT_PRECISION)
-    carried_low = jnp.einsum("haij,hdai->hdaj", inverse, mixed_grad, precision=EXACT_PRECISION)
-    carried_low = carried_low.reshape(own, HEAD_DIM, SEGS).astype(BF)
-    third_delta = jnp.sum(carried_low.astype(F32) * carried, axis=1)
-    carried_grad = spread_halves(carried_low)
-    delta_all = spread_halves(third_delta)
-    small_query, small_key = inverse_pull(inverse_grad)
+    mg_keep = jnp.concatenate([part[:own] for part in mixed_part], axis=0)
+    mg_send = jnp.concatenate([part[own:] for part in mixed_part], axis=0)
+    mg_sum = mg_keep + swap(mg_send, 1)
+    mixed_grad, carried_low = plain(
+        carry_back_kernel,
+        [docs_shape, shape_of((own, HEAD_DIM + 16, SEGS), BF)],
+        flops=6 * own * LAND * SEGS * SEGS,
+        moved=24 * own * tall * SEGS,
+    )(mg_sum[:own], swap(mg_sum[own:], 2), carried, inverse)
+    carried_grad = gather_heads(carried_low)
+    small_query, small_key = plain(
+        newton_back_kernel,
+        [docs_shape, docs_shape],
+        [pltpu.VMEM((own, SEGS, SEGS), F32)],
+        flops=own * NEWTON * 8 * 6 * LAND * SEGS * SEGS,
+        moved=4 * own * NEWTON * 4 * HEAD_DIM * SEGS,
+    )(mixed_grad, carried, small_t, saved, own_q, own_k)
+    delta_all, lse_all = row_of(carried_grad), row_of(mixed)
 
     first_back_call = call(
         first_back_kernel,
@@ -673,7 +826,7 @@
             column(rows, BLOCK),
             column(rows, WIDE),
             column(rows, BLOCK),
-            heads_spec(HEAD_DIM, SEGS),
+            heads_spec(HEAD_DIM + 16, SEGS),
             heads_spec(HEAD_DIM, SEGS),
         ],
         [
@@ -711,7 +864,7 @@
             column(rows, WIDE),
             heads_spec(1, SEGS),
             heads_spec(1, SEGS),
-            heads_spec(HEAD_DIM, SEGS),
+            heads_spec(HEAD_DIM + 16, SEGS),
             heads_spec(HEAD_DIM, SEGS),
             column(rows, BLOCK),
         ],
@@ -724,64 +877,151 @@
         flops=8 * rows * side_cols * SEGS,
         moved=2 * rows * (side_cols * 6 + side * SEGS),
     )
-    query_low, key_low, value_low, land_qg, land_kg, tap_grads = [], [], [], [], [], []
+    def hop_sum(value, got):
+        return (value.astype(F32) + got.astype(F32)).astype(BF)
+
+    def slot_parts(parts):
+        cut_rows = parts[0].shape[0] // 2
+        keep = [part[:cut_rows] for part in parts]
+        send = jnp.stack([part[cut_rows:] for part in parts])
+        return keep, send
+
+    out_keep, out_send = slot_parts([tn(part, proj_low).astype(BF) for part in heads_out])
+    out_core = swap(out_send, 1, "out_core")
+
+    dq_parts, lkg_parts, backs, tap_grads = [], [], [], []
     for half in (0, 1):
         dq, lkg = first_back_call(
             heads_grad[half], first_low[half], queries[half], mixed[half], land_k[half]
         )
+        dq_parts.append(dq)
+        lkg_parts.append(lkg)
+
+    conv_in, lkg_parts[1], inner_far, outer_near, out_core = gate(
+        heads_grad_ext[0], lkg_parts[1], inner_far, outer_near, out_core
+    )
+    inner = (gi_keep[0].astype(F32) + gi_core[0].astype(F32) + inner_far.astype(F32)).astype(BF)
+    inner, other = halves(inner, outer_flags[0])
+    inner_hop = swap_batch(other, bits[0], "inner_y")
+    outer = (own_keep.astype(F32) + own_core.astype(F32) + outer_near.astype(F32)).astype(BF)
+    outer, other = split_rows(outer, outer_flags[1])
+    outer_hop = swap_batch(other, bits[1], "outer_z")
+    out_far = swap(add_low(out_keep[1], out_core[1]), 2, "out_x")
+    for half in (0, 1):
         back, tap_out = conv_back_call(
-            code, line, heads_grad_ext[half], values[half], tap_lines(tap_rows[half][:, ::-1])
+            code, line, (conv_in, heads_grad_ext[1])[half], values[half],
+            tap_lines(tap_rows[half][:, ::-1]),
         )
-        factor = jnp.exp(stats[half][:, 0] - lse_all[half]).reshape(side, 1, SEGS)
+        backs.append(back)
+        tap_grads.append(tap_out[:, 0, :KW])
+
+    exp_in, small_query, inner_hop, outer_hop, out_far = gate(
+        third_exp[0], small_query, inner_hop, outer_hop, out_far
+    )
+    inner, other = halves(hop_sum(inner, inner_hop), outer_flags[1])
+    inner_hop = swap_batch(other, bits[1], "inner_z")
+    outer, other = split_rows(hop_sum(outer, outer_hop), outer_flags[2])
+    outer_hop = swap_batch(other, bits[2], "outer_w")
+    out_sum = out_keep[0].astype(F32) + out_core[0].astype(F32) + out_far.astype(F32)
+    out_sum = out_sum.astype(BF)
+    out_hop = swap_batch(out_sum, bits[0], "out_y")
+
+    dk_parts, dv_parts, lqg_parts = [], [], []
+    for half in (0, 1):
+        factor = jnp.exp(packs[half][:, HEAD_DIM : HEAD_DIM + 1] - lse_all[half])
         dk, dv, lqg = third_back_call(
             keys[half],
             values[half],
-            third_exp[half],
+            (exp_in, third_exp[1])[half],
             factor,
-            delta_all[half].reshape(side, 1, SEGS),
+            delta_all[half],
             carried_grad[half],
             land_q[half],
-            back,
+            backs[half],
         )
-        if half == 0:
-            lqg = jnp.concatenate([lqg[:own] + small_query, lqg[own:]], axis=0)
-            lkg = jnp.concatenate([lkg[:own] + small_key, lkg[own:]], axis=0)
-        query_low.append(dq)
-        key_low.append(dk)
-        value_low.append(dv)
-        land_qg.append(lqg.reshape(side_cols, SEGS).astype(BF))
-        land_kg.append(lkg.reshape(side_cols, SEGS).astype(BF))
-        tap_grads.append(tap_out[:, 0, :KW])
-
-    def weight_grad(lows, lands, factor):
+        dk_parts.append(dk)
+        dv_parts.append(dv)
+        lqg_parts.append(lqg)
+    lqg_parts[0] = jnp.concatenate([lqg_parts[0][:own] + small_query, lqg_parts[0][own:]], axis=0)
+    lkg_parts[0] = jnp.concatenate([lkg_parts[0][:own] + small_key, lkg_parts[0][own:]], axis=0)
+    land_qg = [part.reshape(side_cols, SEGS).astype(BF) for part in lqg_parts]
+    land_kg = [part.reshape(side_cols, SEGS).astype(BF) for part in lkg_parts]
+
+    def weight_parts(lows, lands, factor):
         parts = []
         for half in (0, 1):
             part = tn(lows[half], tokens_in)
             if lands is not None:
                 part = part + nn(lands[half], land_tokens)
             parts.append((part * factor).astype(BF))
-        return slot_sum(*slots_of(parts)).T
-
-    grad_value = weight_grad(value_low, None, 1.0)
-    grad_key = weight_grad(key_low, land_kg, QK_SCALE)
-    grad_query = weight_grad(query_low, land_qg, QK_SCALE)
-
+        return slot_parts(parts)
+
+    val_keep, val_send = weight_parts(dv_parts, None, 1.0)
+    val_core = swap(val_send, 1, "val_core")
+    dk_parts[1], inner_hop, outer_hop, out_hop = gate(dk_parts[1], inner_hop, outer_hop, out_hop)
+    inner, other = halves(hop_sum(inner, inner_hop), outer_flags[2])
+    inner_hop = swap_batch(other, bits[2], "inner_w")
+    outer = hop_sum(outer, outer_hop)
+    outer_hop = swap(outer[1], 2, "outer_x")
+    out_sum = hop_sum(out_sum, out_hop)
+    out_hop = swap_batch(out_sum, bits[1], "out_z")
+
+    key_keep, key_send = weight_parts(dk_parts, land_kg, QK_SCALE)
+    key_core = swap(key_send, 1, "key_core")
+    val_far = swap(add_low(val_keep[1], val_core[1]), 2, "val_x")
+    que_keep, que_send = weight_parts(dq_parts, land_qg, QK_SCALE)
+    que_core = swap(que_send, 1, "que_core")
+    key_far = swap(add_low(key_keep[1], key_core[1]), 2, "key_x")
+
+    que_core, inner_hop, outer_hop, out_hop = gate(que_core, inner_hop, outer_hop, out_hop)
+    que_far = swap(add_low(que_keep[1], que_core[1]), 2, "que_x")
+    inner = hop_sum(inner, inner_hop)
+    outer = hop_sum(outer[0], outer_hop)
+    out_sum = hop_sum(out_sum, out_hop)
+    inner_hop = swap_batch(inner, bits[2], "inner_w2")
+    outer_hop = swap_batch(outer, bits[2], "outer_w2")
+    out_hop = swap_batch(out_sum, bits[2], "out_w")
     land_back = sum(tn(land_qg[half], wq[half]) + tn(land_kg[half], wk[half]) for half in (0, 1))
-    land_back = head_sum((QK_SCALE * land_back / counts[:, None]).astype(BF))
-    scaled = sum(nn(query_low[half], wq[half]) + nn(key_low[half], wk[half]) for half in (0, 1))
-    plain = sum(nn(value_low[half], wv[half]) for half in (0, 1))
-    input_grad = (first_in_grad + QK_SCALE * scaled + plain + nn(member, land_back)).astype(BF)
-
-    tap_keep = jnp.stack([part[:own] for part in tap_grads])
-    tap_send = jnp.stack([part[own:] for part in tap_grads])
-    tap_got = tap_keep + swap(tap_send, 1)
-    tap_own = tap_got[0] + swap(tap_got[1], 2)
+    land_back = head_sum(QK_SCALE * land_back / counts[:, None]).astype(BF)
+    scaled = sum(nn(dq_parts[half], wq[half]) + nn(dk_parts[half], wk[half]) for half in (0, 1))
+    direct = sum(nn(dv_parts[half], wv[half]) for half in (0, 1))
+    input_grad = (first_in_grad + QK_SCALE * scaled + direct + nn(member, land_back)).astype(BF)
+
+    tails = []
+    for keep, near, far, order, name in (
+        (val_keep, val_core, val_far, (0, 1, 2), "val"),
+        (key_keep, key_core, key_far, (1, 2, 0), "key"),
+        (que_keep, que_core, que_far, (2, 0, 1), "que"),
+    ):
+        total = keep[0].astype(F32) + near[0].astype(F32) + far.astype(F32)
+        tails.append((total.astype(BF), order, name))
+    inner = ordered(outer_flags[2], inner, inner_hop)
+    outer = ordered(outer_flags[2], outer, outer_hop)
+    out_sum = hop_sum(out_sum, out_hop)
+    for bit in bits[3:]:
+        inner = hop_sum(inner, swap_batch(inner, bit, "inner_more"))
+        outer = hop_sum(outer, swap_batch(outer, bit, "outer_more"))
+        out_sum = hop_sum(out_sum, swap_batch(out_sum, bit, "out_more"))
+    grad_output = out_sum.astype(F32)
+    inner = ordered(outer_flags[1], inner, swap_batch(inner, bits[1], "inner_z2"))
+    outer = ordered(outer_flags[1], outer, swap_batch(outer, bits[1], "outer_z2"))
+    grad_inner = ordered(outer_flags[0], inner, swap_batch(inner, bits[0], "inner_y2")).astype(F32)
+    grad_outer = ordered(outer_flags[0], outer, swap_batch(outer, bits[0], "outer_y2")).astype(F32)
+    sums = []
+    for total, order, name in tails:
+        for index in order + tuple(range(3, len(bits))):
+            total = hop_sum(total, swap_batch(total, bits[index], name))
+        sums.append(total.astype(F32).T)
+    grad_value, grad_key, grad_query = sums
+
     norms = jnp.stack([grad_first_gain, grad_first_bias, grad_second_gain, grad_second_bias])
-    for bit in (1, 2):
-        norms = norms + swap(norms, bit)
-    small = jnp.concatenate([norms, jnp.pad(tap_own, ((0, 0), (0, width - KW)))], axis=0)
-    for b in range(batch_size.bit_length() - 1):
-        small = small + swap_batch(small, 1 << b)
+    tap_lines_own = [jnp.pad(part, ((0, 0), (0, width - KW))) for part in tap_grads]
+    keep = jnp.concatenate([norms] + [part[:own] for part in tap_lines_own], axis=0)
+    send = jnp.concatenate([norms] + [part[own:] for part in tap_lines_own], axis=0)
+    keep = keep + swap(send, 1)
+    small = keep[: 4 + own] + swap(jnp.concatenate([keep[:4], keep[4 + own :]], axis=0), 2)
+    for bit in bits:
+        small = small + swap_batch(small, bit)
     return (
         layer_out,
         input_grad,

time: 644 us -> 444 us (0.69)
  matrix products: 113 us -> 42.4 us
  waiting for transfers between devices: 162 us -> 101 us
  Pallas kernels: 162 us -> 130 us
  local copies, waits for them, and re-layouts: 56.9 us -> 33.1 us
  starting transfers between devices: 86.1 us -> 63.5 us
  blocking collectives: 0 us -> 14.2 us
    ppermute x49 -> x30, waiting for transfers between devices: 91.1 us -> 21.3 us  [swap(): return lax.ppermute(value, 'head', [(i, i ^ bit) for i in range(groups)])]
    dot_general x78 -> x0, matrix products: 66.2 us -> none  [the longest x36 27.1 us: newton_inverse(): jnp.matmul(product, factor_term, precision=EXACT_PRECISION)]
    all_gather x0 -> x2, blocking collectives: none -> 14.2 us  [gather_heads(): got = lax.all_gather(value, 'head', axis=0, tiled=False)]
    pallas_call x2, Pallas kernels: 25.3 us -> 11.1 us  [shards(): first_call(code, line, queries[half], values[half], land_k[half], tap_lin...]
    ppermute x39 -> x27, starting transfers between devices: 50 us -> 35.9 us  [swap_batch(): lax.ppermute(value, 'batch', [(i, i ^ bit) for i in range(batch_size)])]
    unnamed x417 -> x299, local copies, waits for them, and re-layouts: 30.1 us -> 19.9 us
    convert_element_type x6 -> x26, other arithmetic: 4.74 us -> 13.4 us  [the longest x1 3.43 us: shards(): (own_keep.astype(F32) + own_core.astype(F32) + outer_near.astype(F32)).as...]
    ppermute x39 -> x27, waiting for transfers between devices: 71 us -> 79.7 us  [swap_batch(): lax.ppermute(value, 'batch', [(i, i ^ bit) for i in range(batch_size)])]
  transfers between devices with their start and end apart: 92 -> 61, of which waited for: 42 -> 18; matrix products, arithmetic and copies ran while one was open for 25% -> 17% of each run, Pallas kernels for 13% -> 18%
where the time goes in v2:
time: 444 us; the launch traced here: 438 us
  Pallas kernels  130 us (29%)
  waiting for transfers between devices  101 us (23%)
  starting transfers between devices  63.5 us (14%)
  other arithmetic  49.2 us (11%)
  matrix products  42.4 us (10%)
  local copies, waits for them, and re-layouts  33.1 us (7%)
  blocking collectives  14.2 us (3%)
    ppermute x27, waiting for transfers between devices, swap_batch(): lax.ppermute(value, 'batch', [(i, i ^ bit) for i in range(batch_size)])  79.7 us
    pallas_call x2, Pallas kernels, feed_back(): pl.pallas_call(feed_back_kernel, grid_spec=grid_spec, out_shape=[shape_of...  40.3 us
    ppermute x27, starting transfers between devices, swap_batch(): lax.ppermute(value, 'batch', [(i, i ^ bit) for i in range(batch_size)])  35.9 us
    ppermute x30, starting transfers between devices, swap(): return lax.ppermute(value, 'head', [(i, i ^ bit) for i in range(groups)])  21.3 us
    ppermute x30, waiting for transfers between devices, swap(): return lax.ppermute(value, 'head', [(i, i ^ bit) for i in range(groups)])  21.3 us
    unnamed x299, local copies, waits for them, and re-layouts  19.9 us
    dot_general x13, matrix products, nn(): lax.dot_general(a, b, (((1,), (0,)), ((), ())), preferred_element_type=F32)  18.3 us
    pallas_call x1, Pallas kernels, shards(): call(feed_kernel, (ff // block,), [whole((rows, width)), column(width, bl...  16.2 us
  transfers between devices with their start and end apart: 61, of which 18 were waited for; matrix products, arithmetic and copies ran while one was open for 17% of the time, Pallas kernels for 18%

profile of v2, /device:TPU:0, one launch (start us, length us, event | category | flops | bytes accessed | tf_op | source)
XLA Modules:
  0.0 437.5 jit_solution(10788152527273642784)
XLA Ops:
  24.4 16.2 %collective-permute-done.4 = f32[128,768]{1,0:T(8,128)S(1)} collective-permute-done((f32[128,768]{1,0:T(8,128)S(1)}, f32[128,768]{1,0:T(8,128)S(1)}, u32[]{:S(2)}, u32[]{:S(2)}) %collective-permute-start.4) | collective-permute-done | bytes 393248 | tf_op jit(solution)/shard_map/swap/ppermute | solution.py:516
  49.1 4.5 %shard_map.256 = (f32[6,72,256]{2,1,0:T(8,128)S(1)}, bf16[1024,1536]{1,0:T(8,128)(2,1)S(1)}) custom-call(s32[1024,1]{1,0:T(8,128)S(1)} %copy.76.code_ref, bf16[1024,384]{1,0:T(8,128)(2,1)S(1)} %fusion.24.k_ref, bf16[1152,384]{1,0:T(8,128)(2,1)S(1)} %convolution_convert_fusion.1.v_ref, bf16[6,64,256]{2,1,0:T(8,128)(2,1)S(1)} %bitcast.178), custom_call_target="tpu_custom_call" | custom-call | flops 402653184 | bytes 4718592 | tf_op jit(solution)/shard_map/pallas_call | solution.py:628
  55.3 5.5 %shard_map.255 = (bf16[1024,1536]{1,0:T(8,128)(2,1)S(1)}, f32[1024,384]{1,0:T(8,128)S(1)}) custom-call(s32[1024,1]{1,0:T(8,128)S(1)} %copy.76.code_ref, s32[1,1152]{1,0:T(1,128)S(1)} %reshape.149.line_ref, bf16[1024,384]{1,0:T(8,128)(2,1)S(1)} %fusion.23.q_ref, bf16[1152,384]{1,0:T(8,128)(2,1)S(1)} %convolution_convert_fusion.1.v_ref, ...), custom_call_target="tpu_custom_call" | custom-call | flops 402653184 | bytes 6291456 | tf_op jit(solution)/shard_map/pallas_call | solution.py:691
  60.9 5.4 %shard_map.259 = (f32[3,64,256]{2,1,0:T(8,128)S(1)}, f32[3,64,256]{2,1,0:T(8,128)S(1)}, f32[6,3,4,64,256]{4,3,2,1,0:T(8,128)S(1)}) custom-call(bf16[3,64,256]{2,1,0:T(8,128)(2,1)S(1)} %bitcast.186, bf16[3,64,256]{2,1,0:T(8,128)(2,1)S(1)} %bitcast.188), custom_call_target="tpu_custom_call" | custom-call | flops 1811939328 | bytes 4718592 | tf_op jit(solution)/shard_map/pallas_call | solution.py:634
  72.0 4.2 shard_map.257
  81.6 5.5 %shard_map.262 = (bf16[1024,1536]{1,0:T(8,128)(2,1)S(1)}, f32[1024,384]{1,0:T(8,128)S(1)}) custom-call(s32[1024,1]{1,0:T(8,128)S(1)} %copy-done.3, s32[1,1152]{1,0:T(1,128)S(1)} %reshape.149.line_ref, bf16[1024,384]{1,0:T(8,128)(2,1)S(1)} %fusion.26.q_ref, bf16[1152,384]{1,0:T(8,128)(2,1)S(1)} %convolution_convert_fusion.v_ref, ...), custom_call_target="tpu_custom_call" | custom-call | flops 402653184 | bytes 6291456 | tf_op jit(solution)/shard_map/pallas_call | solution.py:691
  87.5 6.9 %all-gather = bf16[12,80,256]{2,1,0:T(8,128)(2,1)S(1)} all-gather(bf16[3,80,256]{2,1,0:T(8,128)(2,1)S(1)} %get-tuple-element.78), channel_id=2, replica_groups=mesh['batch'=8,'head'=4] {'head'}, dimensions={0}, use_global_device_ids=true | all-gather | bytes 614400 | tf_op jit(solution)/shard_map/all_gather | solution.py:551
  104.0 16.2 %shard_map.264 = (bf16[1024,3072]{1,0:T(8,128)(2,1)}, bf16[1024,3072]{1,0:T(8,128)(2,1)}, f32[1024,768]{1,0:T(8,128)S(1)}) custom-call(bf16[1024,768]{1,0:T(8,128)(2,1)S(1)} %fusion.10.x_ref, bf16[768,3072]{1,0:T(8,128)(2,1)S(1)} %bitcast.191, bf16[3072,768]{1,0:T(8,128)(2,1)S(1)} %bitcast.193), custom_call_target="tpu_custom_call" | custom-call | flops 9663676416 | bytes 26738688 | tf_op jit(solution)/shard_map/pallas_call | solution.py:704
  127.2 19.8 %shard_map.265 = (bf16[2,768,768]{2,1,0:T(8,128)(2,1)}, bf16[2,768,768]{2,1,0:T(8,128)(2,1)}, f32[1024,768]{1,0:T(8,128)}) custom-call(s32[4]{0:T(128)S(1)} %get-tuple-element.216.table, bf16[1024,768]{1,0:T(8,128)(2,1)S(1)} %get-tuple-element.149.og_ref, bf16[1024,768]{1,0:T(8,128)(2,1)S(1)} %fusion.10.x_ref, bf16[768,3072]{1,0:T(8,128)(2,1)} %wi_ref.5, ...), custom_call_target="tpu_custom_call" | custom-call | flops 9663676416 | bytes 25165824 | tf_op jit(solution)/shard_map/pallas_call | solution.py:750
  153.8 20.5 %shard_map.266 = (bf16[2,768,768]{2,1,0:T(8,128)(2,1)S(1)}, bf16[2,768,768]{2,1,0:T(8,128)(2,1)}, f32[1024,768]{1,0:T(8,128)}) custom-call(s32[4]{0:T(128)S(1)} %get-tuple-element.215.table, bf16[1024,768]{1,0:T(8,128)(2,1)S(1)} %copy-done.20, bf16[1024,768]{1,0:T(8,128)(2,1)S(1)} %copy-done.22, bf16[768,3072]{1,0:T(8,128)(2,1)} %wi_ref.5, ...), custom_call_target="tpu_custom_call" | custom-call | flops 9663676416 | bytes 25165824 | tf_op jit(solution)/shard_map/pallas_call | solution.py:750
  174.3 3.2 multiply_reduce_fusion
  198.9 5.2 %shard_map.272 = (bf16[1024,384]{1,0:T(8,128)(2,1)S(1)}, f32[6,64,256]{2,1,0:T(8,128)S(1)}) custom-call(bf16[1024,384]{1,0:T(8,128)(2,1)S(1)} %slice.394.hg_ref, bf16[1024,1536]{1,0:T(8,128)(2,1)S(1)} %get-tuple-element.80.p_ref, bf16[1024,384]{1,0:T(8,128)(2,1)S(1)} %copy-done.32, bf16[6,80,256]{2,1,0:T(8,128)(2,1)S(1)} %copy-done.18, ...), custom_call_target="tpu_custom_call" | custom-call | flops 603979776 | bytes 5505024 | tf_op jit(solution)/shard_map/pallas_call | solution.py:894
  214.4 4.8 %shard_map.267 = (bf16[1024,384]{1,0:T(8,128)(2,1)S(1)}, f32[6,64,256]{2,1,0:T(8,128)S(1)}) custom-call(bf16[1024,384]{1,0:T(8,128)(2,1)S(1)} %slice.392.hg_ref, bf16[1024,1536]{1,0:T(8,128)(2,1)S(1)} %copy-done.1, bf16[1024,384]{1,0:T(8,128)(2,1)S(1)} %copy-done.30, bf16[6,80,256]{2,1,0:T(8,128)(2,1)S(1)} %pad_maximum_fusion.29.mix_ref, ...), custom_call_target="tpu_custom_call" | custom-call | flops 603979776 | bytes 5505024 | tf_op jit(solution)/shard_map/pallas_call | solution.py:894
  224.3 5.6 %shard_map.275 = (f32[1024,384]{1,0:T(8,128)S(1)}, f32[6,8,256]{2,1,0:T(8,128)S(1)}) custom-call(s32[1024,1]{1,0:T(8,128)S(1)} %copy-done.4, s32[1,1152]{1,0:T(1,128)S(1)} %reshape.149.line_ref, bf16[1152,384]{1,0:T(8,128)(2,1)S(1)} %fusion.8.hgx_ref, bf16[1152,384]{1,0:T(8,128)(2,1)S(1)} %copy-done.12, f32[6,1,256]{2,1,0:T(1,128)S(1)} %reshape.170.w_ref), custom_call_target="tpu_custom_call" | custom-call | flops 402653184 | bytes 3145728 | tf_op jit(solution)/shard_map/pallas_call | solution.py:911
  230.5 7.3 %all-gather.1 = bf16[12,80,256]{2,1,0:T(8,128)(2,1)S(1)} all-gather(bf16[3,80,256]{2,1,0:T(8,128)(2,1)S(1)} %get-tuple-element.106), channel_id=3, replica_groups=mesh['batch'=8,'head'=4] {'head'}, dimensions={0}, use_global_device_ids=true | all-gather | bytes 614400 | tf_op jit(solution)/shard_map/all_gather | solution.py:551
  238.0 10.1 %shard_map.271 = (f32[3,64,256]{2,1,0:T(8,128)S(1)}, f32[3,64,256]{2,1,0:T(8,128)S(1)}) custom-call(f32[3,64,256]{2,1,0:T(8,128)S(1)} %get-tuple-element.93.mg_ref, f32[3,64,256]{2,1,0:T(8,128)S(1)} %copy-done.48, f32[3,64,256]{2,1,0:T(8,128)S(1)} %copy-done.53, f32[6,3,4,64,256]{4,3,2,1,0:T(8,128)S(1)} %bitcast.195, bf16[3,64,256]{2,1,0:T(8,128)(2,1)S(1)} %bitcast.187, ...), custom_call_target="tpu_custom_call" | custom-call | flops 3623878656 | bytes 4718592 | tf_op jit(solution)/shard_map/pallas_call | solution.py:813
  248.1 5.0 %shard_map.276 = (bf16[1024,384]{1,0:T(8,128)(2,1)S(1)}, bf16[1024,384]{1,0:T(8,128)(2,1)S(1)}, f32[6,64,256]{2,1,0:T(8,128)S(1)}) custom-call(bf16[1024,384]{1,0:T(8,128)(2,1)S(1)} %copy-done.28, bf16[1152,384]{1,0:T(8,128)(2,1)S(1)} %copy-done.12, bf16[1024,1536]{1,0:T(8,128)(2,1)S(1)} %copy-done.16, f32[6,1,256]{2,1,0:T(1,128)S(1)} %subtract_exponential_fusion.f_ref, ...), custom_call_target="tpu_custom_call" | custom-call | flops 805306368 | bytes 7864320 | tf_op jit(solution)/shard_map/pallas_call | solution.py:932
  260.0 3.1 fusion.11
  264.0 5.6 %shard_map.273 = (f32[1024,384]{1,0:T(8,128)S(1)}, f32[6,8,256]{2,1,0:T(8,128)S(1)}) custom-call(s32[1024,1]{1,0:T(8,128)S(1)} %copy-done.4, s32[1,1152]{1,0:T(1,128)S(1)} %reshape.149.line_ref, bf16[1152,384]{1,0:T(8,128)(2,1)S(1)} %fusion.7.hgx_ref, bf16[1152,384]{1,0:T(8,128)(2,1)S(1)} %copy-done.10, f32[6,1,256]{2,1,0:T(1,128)S(1)} %copy.82.w_ref), custom_call_target="tpu_custom_call" | custom-call | flops 402653184 | bytes 3145728 | tf_op jit(solution)/shard_map/pallas_call | solution.py:911
  271.2 3.4 add_convert_fusion.2
  284.7 10.6 %collective-permute-done.53 = f32[7,768]{1,0:T(8,128)S(1)} collective-permute-done((f32[7,768]{1,0:T(8,128)S(1)}, f32[7,768]{1,0:T(8,128)S(1)}, u32[]{:S(2)}, u32[]{:S(2)}) %collective-permute-start.53) | collective-permute-done | bytes 21536 | tf_op jit(solution)/shard_map/swap/ppermute | solution.py:520
  301.3 5.0 %shard_map.274 = (bf16[1024,384]{1,0:T(8,128)(2,1)S(1)}, bf16[1024,384]{1,0:T(8,128)(2,1)S(1)}, f32[6,64,256]{2,1,0:T(8,128)S(1)}) custom-call(bf16[1024,384]{1,0:T(8,128)(2,1)S(1)} %copy-done.26, bf16[1152,384]{1,0:T(8,128)(2,1)S(1)} %copy-done.10, bf16[1024,1536]{1,0:T(8,128)(2,1)S(1)} %copy-done.14, f32[6,1,256]{2,1,0:T(1,128)S(1)} %subtract_exponential_fusion.1.f_ref, ...), custom_call_target="tpu_custom_call" | custom-call | flops 805306368 | bytes 7864320 | tf_op jit(solution)/shard_map/pallas_call | solution.py:932
  332.1 3.0 collective-permute-done.32
  336.1 4.3 collective-permute-done.34
  343.6 9.1 %collective-permute-done.55 = bf16[96,768]{1,0:T(8,128)(2,1)S(1)} collective-permute-done((bf16[96,768]{1,0:T(8,128)(2,1)S(1)}, bf16[96,768]{1,0:T(8,128)(2,1)S(1)}, u32[]{:S(2)}, u32[]{:S(2)}) %collective-permute-start.55) | collective-permute-done | bytes 147488 | tf_op jit(solution)/shard_map/inner_w2/ppermute | solution.py:520
  352.7 9.4 %collective-permute-done.58 = bf16[96,768]{1,0:T(8,128)(2,1)S(1)} collective-permute-done((bf16[96,768]{1,0:T(8,128)(2,1)S(1)}, bf16[96,768]{1,0:T(8,128)(2,1)S(1)}, u32[]{:S(2)}, u32[]{:S(2)}) %collective-permute-start.58) | collective-permute-done | bytes 147488 | tf_op jit(solution)/shard_map/outer_w2/ppermute | solution.py:520
  376.5 4.4 %add_convert_fusion = bf16[1024,768]{1,0:T(8,128)(2,1)} fusion(f32[1024,768]{1,0:T(8,128)} %fusion.36, f32[1024,768]{1,0:T(8,128)S(1)} %fusion.57, f32[1024,768]{1,0:T(8,128)S(1)} %copy-done.62, f32[1024,768]{1,0:T(8,128)S(1)} %copy-done.60, f32[1024,768]{1,0:T(8,128)S(1)} %fusion.77, f32[1024,768]{1,0:T(8,128)S(1)} %copy-done.61, ...), kind=kOutput, calls=%fused_computation.15 | convolution fusion | flops 612237312 | bytes 24969216 | tf_op jit(solution)/shard_map/dot_general | solution.py:46
  384.4 4.7 %collective-permute-start.60 = (bf16[384,768]{1,0:T(8,128)(2,1)S(1)}, bf16[384,768]{1,0:T(8,128)(2,1)S(1)}, u32[]{:S(2)}, u32[]{:S(2)}) collective-permute-start(bf16[384,768]{1,0:T(8,128)(2,1)S(1)} %pad_maximum_fusion.15), channel_id=1, source_target_pairs={{0,4},{4,0},{8,12},{12,8},{16,20},{20,16},{24,28},{28,24},{1,5},{5... | collective-permute-start | bytes 1769480 | tf_op jit(solution)/shard_map/outer_y2/ppermute | solution.py:520
  391.6 7.5 %collective-permute-done.47 = bf16[192,768]{1,0:T(8,128)(2,1)S(1)} collective-permute-done((bf16[192,768]{1,0:T(8,128)(2,1)S(1)}, bf16[192,768]{1,0:T(8,128)(2,1)S(1)}, u32[]{:S(2)}, u32[]{:S(2)}) %collective-permute-start.47) | collective-permute-done | bytes 294944 | tf_op jit(solution)/shard_map/val/ppermute | solution.py:520
  399.5 14.4 %collective-permute-done.37 = bf16[192,768]{1,0:T(8,128)(2,1)S(1)} collective-permute-done((bf16[192,768]{1,0:T(8,128)(2,1)S(1)}, bf16[192,768]{1,0:T(8,128)(2,1)S(1)}, u32[]{:S(2)}, u32[]{:S(2)}) %collective-permute-start.37) | collective-permute-done | bytes 294944 | tf_op jit(solution)/shard_map/que/ppermute | solution.py:520
  420.4 9.0 %collective-permute-done.42 = bf16[192,768]{1,0:T(8,128)(2,1)S(1)} collective-permute-done((bf16[192,768]{1,0:T(8,128)(2,1)S(1)}, bf16[192,768]{1,0:T(8,128)(2,1)S(1)}, u32[]{:S(2)}, u32[]{:S(2)}) %collective-permute-start.42) | collective-permute-done | bytes 294944 | tf_op jit(solution)/shard_map/key/ppermute | solution.py:520
  431.8 4.4 %collective-permute-done.43 = bf16[192,768]{1,0:T(8,128)(2,1)S(1)} collective-permute-done((bf16[192,768]{1,0:T(8,128)(2,1)S(1)}, bf16[192,768]{1,0:T(8,128)(2,1)S(1)}, u32[]{:S(2)}, u32[]{:S(2)}) %collective-permute-start.43) | collective-permute-done | bytes 294944 | tf_op jit(solution)/shard_map/key/ppermute | solution.py:520
  (638 shorter events, 189.4 us)
Async XLA Ops:
  7.6 36.6 %collective-permute-start.7 = (bf16[576,768]{1,0:T(8,128)(2,1)}, bf16[576,768]{1,0:T(8,128)(2,1)}, u32[]{:S(2)}, u32[]{:S(2)}) collective-permute-start(bf16[576,768]{1,0:T(8,128)(2,1)} %pad_maximum_fusion), channel_id=1, source_target_pairs={{0,2},{1,3},{2,0},{3,1},{4,6},{5,7},{6,4},{7,5},{8,10},{9,11},{10,... | collective-permute-start | bytes 2654216 | tf_op jit(solution)/shard_map/swap/ppermute | solution.py:516
  7.6 33.1 %collective-permute-start = (bf16[576,768]{1,0:T(8,128)(2,1)}, bf16[576,768]{1,0:T(8,128)(2,1)}, u32[]{:S(2)}, u32[]{:S(2)}) collective-permute-start(bf16[576,768]{1,0:T(8,128)(2,1)} %pad_maximum_fusion), channel_id=1, source_target_pairs={{0,1},{1,0},{2,3},{3,2},{4,5},{5,4},{6,7},{7,6},{8,9},{9,8},{10,11... | collective-permute-start | bytes 2654216 | tf_op jit(solution)/shard_map/swap/ppermute | solution.py:516
  14.1 32.1 %collective-permute-start.1 = (bf16[16,768]{1,0:T(8,128)(2,1)S(1)}, bf16[16,768]{1,0:T(8,128)(2,1)S(1)}, u32[]{:S(2)}, u32[]{:S(2)}) collective-permute-start(bf16[16,768]{1,0:T(8,128)(2,1)S(1)} %get-tuple-element.162), channel_id=1, source_target_pairs={{0,1},{1,2},{2,3},{4,5},{5,6},{6,7},{8,9},{9,10},{10,11},{12,13},{... | collective-permute-start | bytes 73736 | tf_op jit(solution)/shard_map/ppermute | solution.py:592
  20.0 20.6 %collective-permute-start.4 = (f32[128,768]{1,0:T(8,128)S(1)}, f32[128,768]{1,0:T(8,128)S(1)}, u32[]{:S(2)}, u32[]{:S(2)}) collective-permute-start(f32[128,768]{1,0:T(8,128)S(1)} %dynamic-slice_add_fusion.1), channel_id=1, source_target_pairs={{0,2},{1,3},{2,0},{3,1},{4,6},{5,7},{6,4},{7,5},{8,10},{9,11},{10,... | collective-permute-start | bytes 1179656 | tf_op jit(solution)/shard_map/swap/ppermute | solution.py:516
  23.0 23.3 %collective-permute-start.2 = (bf16[16,768]{1,0:T(8,128)(2,1)S(1)}, bf16[16,768]{1,0:T(8,128)(2,1)S(1)}, u32[]{:S(2)}, u32[]{:S(2)}) collective-permute-start(bf16[16,768]{1,0:T(8,128)(2,1)S(1)} %get-tuple-element.163), channel_id=1, source_target_pairs={{1,0},{2,1},{3,2},{5,4},{6,5},{7,6},{9,8},{10,9},{11,10},{13,12},{... | collective-permute-start | bytes 73736 | tf_op jit(solution)/shard_map/ppermute | solution.py:593
  45.7 22.6 %collective-permute-start.8 = (bf16[576,768]{1,0:T(8,128)(2,1)}, bf16[576,768]{1,0:T(8,128)(2,1)S(1)}, u32[]{:S(2)}, u32[]{:S(2)}) collective-permute-start(bf16[576,768]{1,0:T(8,128)(2,1)} %collective-permute-done.7), channel_id=1, source_target_pairs={{0,1},{1,0},{2,3},{3,2},{4,5},{5,4},{6,7},{7,6},{8,9},{9,8},{10,11... | collective-permute-start | bytes 2654216 | tf_op jit(solution)/shard_map/swap/ppermute | solution.py:516
  147.0 27.3 %collective-permute-start.13 = (bf16[2,768,768]{2,1,0:T(8,128)(2,1)}, bf16[2,768,768]{2,1,0:T(8,128)(2,1)}, u32[]{:S(2)}, u32[]{:S(2)}) collective-permute-start(bf16[2,768,768]{2,1,0:T(8,128)(2,1)} %get-tuple-element.87), channel_id=1, source_target_pairs={{0,1},{1,0},{2,3},{3,2},{4,5},{5,4},{6,7},{7,6},{8,9},{9,8},{10,11... | collective-permute-start | bytes 7077896 | tf_op jit(solution)/shard_map/inner_core/ppermute | solution.py:516
  147.4 26.9 %collective-permute-start.14 = (bf16[2,768,768]{2,1,0:T(8,128)(2,1)}, bf16[2,768,768]{2,1,0:T(8,128)(2,1)}, u32[]{:S(2)}, u32[]{:S(2)}) collective-permute-start(bf16[2,768,768]{2,1,0:T(8,128)(2,1)} %get-tuple-element.88), channel_id=1, source_target_pairs={{0,1},{1,0},{2,3},{3,2},{4,5},{5,4},{6,7},{7,6},{8,9},{9,8},{10,11... | collective-permute-start | bytes 7077896 | tf_op jit(solution)/shard_map/outer_core/ppermute | solution.py:516
  181.9 14.5 %collective-permute-start.15 = (bf16[16,768]{1,0:T(8,128)(2,1)S(1)}, bf16[16,768]{1,0:T(8,128)(2,1)S(1)}, u32[]{:S(2)}, u32[]{:S(2)}) collective-permute-start(bf16[16,768]{1,0:T(8,128)(2,1)S(1)} %get-tuple-element.160), channel_id=1, source_target_pairs={{0,1},{1,2},{2,3},{4,5},{5,6},{6,7},{8,9},{9,10},{10,11},{12,13},{... | collective-permute-start | bytes 73736 | tf_op jit(solution)/shard_map/ppermute | solution.py:592
  186.6 71.6 %collective-permute-start.21 = (bf16[2,192,768]{2,1,0:T(8,128)(2,1)}, bf16[2,192,768]{2,1,0:T(8,128)(2,1)}, u32[]{:S(2)}, u32[]{:S(2)}) collective-permute-start(bf16[2,192,768]{2,1,0:T(8,128)(2,1)} %pad_maximum_fusion.10), channel_id=1, source_target_pairs={{0,1},{1,0},{2,3},{3,2},{4,5},{5,4},{6,7},{7,6},{8,9},{9,8},{10,11... | collective-permute-start | bytes 1769480 | tf_op jit(solution)/shard_map/out_core/ppermute | solution.py:516
  190.6 67.6 %collective-permute-start.20 = (bf16[2,384,768]{2,1,0:T(8,128)(2,1)}, bf16[2,384,768]{2,1,0:T(8,128)(2,1)}, u32[]{:S(2)}, u32[]{:S(2)}) collective-permute-start(bf16[2,384,768]{2,1,0:T(8,128)(2,1)} %add_convert_fusion.3), channel_id=1, source_target_pairs={{0,4},{4,0},{8,12},{12,8},{16,20},{20,16},{24,28},{28,24},{1,5},{5... | collective-permute-start | bytes 3538952 | tf_op jit(solution)/shard_map/outer_y/ppermute | solution.py:520
  194.8 63.4 %collective-permute-start.19 = (bf16[768,768]{1,0:T(8,128)(2,1)}, bf16[768,768]{1,0:T(8,128)(2,1)}, u32[]{:S(2)}, u32[]{:S(2)}) collective-permute-start(bf16[768,768]{1,0:T(8,128)(2,1)} %fusion.31), channel_id=1, source_target_pairs={{0,2},{1,3},{2,0},{3,1},{4,6},{5,7},{6,4},{7,5},{8,10},{9,11},{10,... | collective-permute-start | bytes 3538952 | tf_op jit(solution)/shard_map/inner_x/ppermute | solution.py:516
  263.1 38.1 %collective-permute-start.24 = (bf16[192,768]{1,0:T(8,128)(2,1)}, bf16[192,768]{1,0:T(8,128)(2,1)}, u32[]{:S(2)}, u32[]{:S(2)}) collective-permute-start(bf16[192,768]{1,0:T(8,128)(2,1)} %fusion.50), channel_id=1, source_target_pairs={{0,2},{1,3},{2,0},{3,1},{4,6},{5,7},{6,4},{7,5},{8,10},{9,11},{10,... | collective-permute-start | bytes 884744 | tf_op jit(solution)/shard_map/out_x/ppermute | solution.py:516
  280.5 20.8 %collective-permute-start.23 = (bf16[2,192,768]{2,1,0:T(8,128)(2,1)S(1)}, bf16[2,192,768]{2,1,0:T(8,128)(2,1)S(1)}, u32[]{:S(2)}, u32[]{:S(2)}) collective-permute-start(bf16[2,192,768]{2,1,0:T(8,128)(2,1)S(1)} %constant_dynamic-slice_fusion.4), channel_id=1, source_target_pairs={{0,8},{4,12},{8,0},{12,4},{16,24},{20,28},{24,16},{28,20},{1,9},{5... | collective-permute-start | bytes 1769480 | tf_op jit(solution)/shard_map/outer_z/ppermute | solution.py:520
  282.1 19.2 %collective-permute-start.22 = (bf16[384,768]{1,0:T(8,128)(2,1)S(1)}, bf16[384,768]{1,0:T(8,128)(2,1)S(1)}, u32[]{:S(2)}, u32[]{:S(2)}) collective-permute-start(bf16[384,768]{1,0:T(8,128)(2,1)S(1)} %constant_dynamic-slice_fusion.5), channel_id=1, source_target_pairs={{0,4},{4,0},{8,12},{12,8},{16,20},{20,16},{24,28},{28,24},{1,5},{5... | collective-permute-start | bytes 1769480 | tf_op jit(solution)/shard_map/inner_y/ppermute | solution.py:520
  323.5 16.8 %collective-permute-start.31 = (bf16[2,192,768]{2,1,0:T(8,128)(2,1)S(1)}, bf16[2,192,768]{2,1,0:T(8,128)(2,1)S(1)}, u32[]{:S(2)}, u32[]{:S(2)}) collective-permute-start(bf16[2,192,768]{2,1,0:T(8,128)(2,1)S(1)} %pad_maximum_fusion.11), channel_id=1, source_target_pairs={{0,1},{1,0},{2,3},{3,2},{4,5},{5,4},{6,7},{7,6},{8,9},{9,8},{10,11... | collective-permute-start | bytes 1769480 | tf_op jit(solution)/shard_map/que_core/ppermute | solution.py:516
  330.9 41.7 %collective-permute-start.39 = (bf16[2,192,768]{2,1,0:T(8,128)(2,1)S(1)}, bf16[2,192,768]{2,1,0:T(8,128)(2,1)S(1)}, u32[]{:S(2)}, u32[]{:S(2)}) collective-permute-start(bf16[2,192,768]{2,1,0:T(8,128)(2,1)S(1)} %pad_maximum_fusion.12), channel_id=1, source_target_pairs={{0,1},{1,0},{2,3},{3,2},{4,5},{5,4},{6,7},{7,6},{8,9},{9,8},{10,11... | collective-permute-start | bytes 1769480 | tf_op jit(solution)/shard_map/key_core/ppermute | solution.py:516
  331.1 32.1 %collective-permute-start.29 = (f32[128,768]{1,0:T(8,128)S(1)}, f32[128,768]{1,0:T(8,128)S(1)}, u32[]{:S(2)}, u32[]{:S(2)}) collective-permute-start(f32[128,768]{1,0:T(8,128)S(1)} %dynamic-slice_add_fusion), channel_id=1, source_target_pairs={{0,2},{1,3},{2,0},{3,1},{4,6},{5,7},{6,4},{7,5},{8,10},{9,11},{10,... | collective-permute-start | bytes 1179656 | tf_op jit(solution)/shard_map/swap/ppermute | solution.py:516
  335.1 28.2 %collective-permute-start.45 = (bf16[192,768]{1,0:T(8,128)(2,1)S(1)}, bf16[192,768]{1,0:T(8,128)(2,1)S(1)}, u32[]{:S(2)}, u32[]{:S(2)}) collective-permute-start(bf16[192,768]{1,0:T(8,128)(2,1)S(1)} %fusion.39), channel_id=1, source_target_pairs={{0,2},{1,3},{2,0},{3,1},{4,6},{5,7},{6,4},{7,5},{8,10},{9,11},{10,... | collective-permute-start | bytes 884744 | tf_op jit(solution)/shard_map/val_x/ppermute | solution.py:516
  340.8 21.4 %collective-permute-start.58 = (bf16[96,768]{1,0:T(8,128)(2,1)S(1)}, bf16[96,768]{1,0:T(8,128)(2,1)S(1)}, u32[]{:S(2)}, u32[]{:S(2)}) collective-permute-start(bf16[96,768]{1,0:T(8,128)(2,1)S(1)} %fusion.60), channel_id=1, source_target_pairs={{0,16},{4,20},{8,24},{12,28},{16,0},{20,4},{24,8},{28,12},{1,17},{... | collective-permute-start | bytes 442376 | tf_op jit(solution)/shard_map/outer_w2/ppermute | solution.py:520
  352.7 15.8 %collective-permute-start.49 = (bf16[192,768]{1,0:T(8,128)(2,1)S(1)}, bf16[192,768]{1,0:T(8,128)(2,1)S(1)}, u32[]{:S(2)}, u32[]{:S(2)}) collective-permute-start(bf16[192,768]{1,0:T(8,128)(2,1)S(1)} %add_convert_fusion.8), channel_id=1, source_target_pairs={{0,16},{4,20},{8,24},{12,28},{16,0},{20,4},{24,8},{28,12},{1,17},{... | collective-permute-start | bytes 884744 | tf_op jit(solution)/shard_map/out_w/ppermute | solution.py:520
  363.2 17.8 %collective-permute-start.56 = (bf16[192,768]{1,0:T(8,128)(2,1)S(1)}, bf16[192,768]{1,0:T(8,128)(2,1)S(1)}, u32[]{:S(2)}, u32[]{:S(2)}) collective-permute-start(bf16[192,768]{1,0:T(8,128)(2,1)S(1)} %pad_maximum_fusion.27), channel_id=1, source_target_pairs={{0,8},{4,12},{8,0},{12,4},{16,24},{20,28},{24,16},{28,20},{1,9},{5... | collective-permute-start | bytes 884744 | tf_op jit(solution)/shard_map/inner_z2/ppermute | solution.py:520
  363.4 20.9 %collective-permute-start.59 = (bf16[192,768]{1,0:T(8,128)(2,1)S(1)}, bf16[192,768]{1,0:T(8,128)(2,1)S(1)}, u32[]{:S(2)}, u32[]{:S(2)}) collective-permute-start(bf16[192,768]{1,0:T(8,128)(2,1)S(1)} %pad_maximum_fusion.28), channel_id=1, source_target_pairs={{0,8},{4,12},{8,0},{12,4},{16,24},{20,28},{24,16},{28,20},{1,9},{5... | collective-permute-start | bytes 884744 | tf_op jit(solution)/shard_map/outer_z2/ppermute | solution.py:520
  371.0 18.1 %collective-permute-start.46 = (bf16[192,768]{1,0:T(8,128)(2,1)S(1)}, bf16[192,768]{1,0:T(8,128)(2,1)S(1)}, u32[]{:S(2)}, u32[]{:S(2)}) collective-permute-start(bf16[192,768]{1,0:T(8,128)(2,1)S(1)} %fusion.41), channel_id=1, source_target_pairs={{0,4},{4,0},{8,12},{12,8},{16,20},{20,16},{24,28},{28,24},{1,5},{5... | collective-permute-start | bytes 884744 | tf_op jit(solution)/shard_map/val/ppermute | solution.py:520
  372.7 16.6 %collective-permute-start.36 = (bf16[192,768]{1,0:T(8,128)(2,1)S(1)}, bf16[192,768]{1,0:T(8,128)(2,1)S(1)}, u32[]{:S(2)}, u32[]{:S(2)}) collective-permute-start(bf16[192,768]{1,0:T(8,128)(2,1)S(1)} %fusion.47), channel_id=1, source_target_pairs={{0,16},{4,20},{8,24},{12,28},{16,0},{20,4},{24,8},{28,12},{1,17},{... | collective-permute-start | bytes 884744 | tf_op jit(solution)/shard_map/que/ppermute | solution.py:520
  372.8 16.6 %collective-permute-start.40 = (bf16[192,768]{1,0:T(8,128)(2,1)S(1)}, bf16[192,768]{1,0:T(8,128)(2,1)S(1)}, u32[]{:S(2)}, u32[]{:S(2)}) collective-permute-start(bf16[192,768]{1,0:T(8,128)(2,1)S(1)} %fusion.42), channel_id=1, source_target_pairs={{0,2},{1,3},{2,0},{3,1},{4,6},{5,7},{6,4},{7,5},{8,10},{9,11},{10,... | collective-permute-start | bytes 884744 | tf_op jit(solution)/shard_map/key_x/ppermute | solution.py:516
  381.1 35.7 %collective-permute-start.57 = (bf16[384,768]{1,0:T(8,128)(2,1)S(1)}, bf16[384,768]{1,0:T(8,128)(2,1)S(1)}, u32[]{:S(2)}, u32[]{:S(2)}) collective-permute-start(bf16[384,768]{1,0:T(8,128)(2,1)S(1)} %pad_maximum_fusion.14), channel_id=1, source_target_pairs={{0,4},{4,0},{8,12},{12,8},{16,20},{20,16},{24,28},{28,24},{1,5},{5... | collective-permute-start | bytes 1769480 | tf_op jit(solution)/shard_map/inner_y2/ppermute | solution.py:520
  384.4 32.6 %collective-permute-start.60 = (bf16[384,768]{1,0:T(8,128)(2,1)S(1)}, bf16[384,768]{1,0:T(8,128)(2,1)S(1)}, u32[]{:S(2)}, u32[]{:S(2)}) collective-permute-start(bf16[384,768]{1,0:T(8,128)(2,1)S(1)} %pad_maximum_fusion.15), channel_id=1, source_target_pairs={{0,4},{4,0},{8,12},{12,8},{16,20},{20,16},{24,28},{28,24},{1,5},{5... | collective-permute-start | bytes 1769480 | tf_op jit(solution)/shard_map/outer_y2/ppermute | solution.py:520
  389.3 24.6 %collective-permute-start.37 = (bf16[192,768]{1,0:T(8,128)(2,1)S(1)}, bf16[192,768]{1,0:T(8,128)(2,1)S(1)}, u32[]{:S(2)}, u32[]{:S(2)}) collective-permute-start(bf16[192,768]{1,0:T(8,128)(2,1)S(1)} %add_convert_fusion.17), channel_id=1, source_target_pairs={{0,4},{4,0},{8,12},{12,8},{16,20},{20,16},{24,28},{28,24},{1,5},{5... | collective-permute-start | bytes 884744 | tf_op jit(solution)/shard_map/que/ppermute | solution.py:520
  389.5 26.5 %collective-permute-start.41 = (bf16[192,768]{1,0:T(8,128)(2,1)S(1)}, bf16[192,768]{1,0:T(8,128)(2,1)S(1)}, u32[]{:S(2)}, u32[]{:S(2)}) collective-permute-start(bf16[192,768]{1,0:T(8,128)(2,1)S(1)} %fusion.44), channel_id=1, source_target_pairs={{0,8},{4,12},{8,0},{12,4},{16,24},{20,28},{24,16},{28,20},{1,9},{5... | collective-permute-start | bytes 884744 | tf_op jit(solution)/shard_map/key/ppermute | solution.py:520
  399.2 30.8 %collective-permute-start.48 = (bf16[192,768]{1,0:T(8,128)(2,1)S(1)}, bf16[192,768]{1,0:T(8,128)(2,1)S(1)}, u32[]{:S(2)}, u32[]{:S(2)}) collective-permute-start(bf16[192,768]{1,0:T(8,128)(2,1)S(1)} %add_convert_fusion.10), channel_id=1, source_target_pairs={{0,16},{4,20},{8,24},{12,28},{16,0},{20,4},{24,8},{28,12},{1,17},{... | collective-permute-start | bytes 884744 | tf_op jit(solution)/shard_map/val/ppermute | solution.py:520
  414.0 16.9 %collective-permute-start.38 = (bf16[192,768]{1,0:T(8,128)(2,1)S(1)}, bf16[192,768]{1,0:T(8,128)(2,1)S(1)}, u32[]{:S(2)}, u32[]{:S(2)}) collective-permute-start(bf16[192,768]{1,0:T(8,128)(2,1)S(1)} %add_convert_fusion.16), channel_id=1, source_target_pairs={{0,8},{4,12},{8,0},{12,4},{16,24},{20,28},{24,16},{28,20},{1,9},{5... | collective-permute-start | bytes 884744 | tf_op jit(solution)/shard_map/que/ppermute | solution.py:520
  (178 other events, 1530.1 us)

commit v3 on v2

--- a/solution.py
+++ b/solution.py
@@ -18,6 +18,7 @@
 BLOCK = 128
 CHUNK = 256
 QK_SCALE = HEAD_DIM ** (-0.25)
+FAR_TYPE = jnp.bfloat16
 
 NEG_FILL = -1e30
 NORM_EPS = 1e-05
@@ -125,8 +126,7 @@
     return code_ref[rows_of(i, BLOCK), :] == line
 
 
-def first_kernel(code_ref, line_ref, q_ref, v_ref, lk_ref, w_ref, p_ref, conv_ref, t_scr):
-    lk2 = pair_block(lk_ref)
+def conv_kernel(code_ref, line_ref, v_ref, w_ref, conv_ref, t_scr):
     t_scr[0] = band(w_ref, 0)
     t_scr[1] = band(w_ref, 1)
     left_lane = lax.broadcasted_iota(jnp.int32, (BLOCK, BLOCK), 1) < HEAD_DIM
@@ -141,7 +141,11 @@
         conv_ref[rows_of(i, BLOCK), :] = jnp.where(left_lane, one, two)
         return carry
 
-    lax.fori_loop(0, q_ref.shape[0] // BLOCK, convolve, 0, unroll=True)
+    lax.fori_loop(0, conv_ref.shape[0] // BLOCK, convolve, 0, unroll=True)
+
+
+def first_kernel(code_ref, q_ref, lk_ref, p_ref):
+    lk2 = pair_block(lk_ref)
 
     def weigh(i, carry):
         r = rows_of(i, CHUNK)
@@ -196,7 +200,14 @@
     put_pair(lkg_ref, acc[...])
 
 
-def conv_back_kernel(code_ref, line_ref, hgx_ref, v_ref, w_ref, back_ref, tap_ref, t_scr, acc):
+def conv_back_kernel(
+    code_ref, line_ref, hg_ref, edge_ref, v_ref, w_ref, part_ref, dv_ref, tap_ref, t_scr, acc, hgx
+):
+    rows = hg_ref.shape[0]
+    hgx[:HALF, :] = edge_ref[:HALF, :]
+    hgx[HALF : HALF + rows, :] = hg_ref[...]
+    hgx[HALF + rows : 2 * HALF + rows, :] = edge_ref[HALF:, :]
+    hgx[2 * HALF + rows :, :] = jnp.zeros((BLOCK - 2 * HALF, BLOCK), BF)
     t_scr[0] = band(w_ref, 0)
     t_scr[1] = band(w_ref, 1)
     acc[...] = jnp.zeros_like(acc)
@@ -204,27 +215,28 @@
 
     def body(i, carry):
         mask = band_mask(code_ref, line_ref, i)
-        grads = hgx_ref[rows_of(i, BLOCK), :], hgx_ref[rows_of(i + 1, BLOCK), :]
+        grads = hgx[rows_of(i, BLOCK), :], hgx[rows_of(i + 1, BLOCK), :]
         grads = jnp.concatenate(grads, axis=0)
         vals = v_ref[rows_of(i, BLOCK), :], v_ref[rows_of(i + 1, BLOCK), :]
         vals = jnp.concatenate(vals, axis=0)
         zero = jnp.zeros((BLOCK, 2 * BLOCK), BF)
         one = nn(jnp.where(mask, t_scr[0], zero), grads)
         two = nn(jnp.where(mask, t_scr[1], zero), grads)
-        back_ref[rows_of(i, BLOCK), :] = jnp.where(left_lane, one, two)
-        here = hgx_ref[rows_of(i, BLOCK, HALF), :]
+        r = rows_of(i, BLOCK)
+        dv_ref[r, :] = (part_ref[r, :] + jnp.where(left_lane, one, two)).astype(BF)
+        here = hg_ref[r, :]
         none = jnp.zeros_like(here)
         acc[0] += jnp.where(mask, nt(jnp.where(left_lane, here, none), vals), 0.0)
         acc[1] += jnp.where(mask, nt(jnp.where(left_lane, none, here), vals), 0.0)
         return carry
 
-    lax.fori_loop(0, back_ref.shape[0] // BLOCK, body, 0, unroll=True)
+    lax.fori_loop(0, rows // BLOCK, body, 0, unroll=True)
     for side in (0, 1):
         tap_ref[side, 0:1, :] = jnp.sum(skew(acc[side], True), axis=0, keepdims=True)
 
 
 def third_back_kernel(
-    k_ref, v_ref, e_ref, f_ref, d_ref, cg_ref, lq_ref, back_ref, dk_ref, dv_ref, lqg_ref, acc
+    k_ref, v_ref, e_ref, f_ref, d_ref, cg_ref, lq_ref, dk_ref, dv_ref, lqg_ref, acc
 ):
     cg2 = pair_block(cg_ref)
     lq2 = pair_block(lq_ref)
@@ -238,7 +250,7 @@
         p = e_ref[r, :].astype(F32) * factor
         ds = (p * (h - delta)).astype(BF)
         dk_ref[r, :] = nt(ds, lq2).astype(BF)
-        dv_ref[r, :] = (nt(p.astype(BF), cg2) + back_ref[r, :]).astype(BF)
+        dv_ref[r, :] = nt(p.astype(BF), cg2)
         acc[...] += tn(k_ref[r, :], ds)
         return carry
 
@@ -440,7 +452,72 @@
         dk_ref[h] = nt(lq_ref[h], blocks[0]) + nt(lq_ref[h], blocks[1])
 
 
-def call(body, grid, ins, outs, scratch=(), flops=0, moved=0, exps=0, limit=40):
+def project_kernel(x_ref, one_ref, two_ref, q_ref, k_ref, v_ref):
+    local = one_ref.shape[0] // 3
+    rows = q_ref.shape[0]
+    weights = []
+    for kind in range(3):
+        cut = slice(kind * local, (kind + 1) * local)
+        weights.append(jnp.concatenate([one_ref[cut, :], two_ref[cut, :]], axis=0))
+    size = 2 * BLOCK
+    for i in range(rows // size):
+        x = x_ref[HALF + i * size : HALF + (i + 1) * size, :]
+        r = slice(i * size, (i + 1) * size)
+        q_ref[r, :] = (nt(x, weights[0]) * QK_SCALE).astype(BF)
+        k_ref[r, :] = (nt(x, weights[1]) * QK_SCALE).astype(BF)
+        v_ref[HALF + i * size : HALF + (i + 1) * size, :] = nt(x, weights[2]).astype(BF)
+    ends = jnp.concatenate([x_ref[:HALF, :], x_ref[HALF + rows :, :]], axis=0)
+    ends = nt(ends, weights[2]).astype(BF)
+    v_ref[:HALF, :] = ends[:HALF]
+    v_ref[HALF + rows :, :] = ends[HALF:]
+
+
+def landmark_kernel(land_ref, one_ref, two_ref, lq_ref, lk_ref):
+    local = one_ref.shape[0] // 3
+    high, low = split_low(land_ref[...])
+    for kind, out in ((0, lq_ref), (1, lk_ref)):
+        for index, part in enumerate((one_ref, two_ref)):
+            weight = part[kind * local : (kind + 1) * local, :]
+            mapped = ((nt(weight, high) + nt(weight, low)) * QK_SCALE).astype(BF)
+            for h in range(local // HEAD_DIM):
+                head = index * (local // HEAD_DIM) + h
+                out[head] = mapped[h * HEAD_DIM : (h + 1) * HEAD_DIM]
+
+
+def weight_grad_kernel(count, with_land, x_ref, *refs):
+    keep_ref, send_ref = refs[-2:]
+    lows, rest = refs[: 2 * count], refs[2 * count : -2]
+    x = x_ref[...]
+    for index in range(count):
+        for half in (0, 1):
+            total = tn(lows[2 * index + half][...], x)
+            if with_land:
+                land = rest[1 + 2 * index + half]
+                flat = [land[h].astype(BF) for h in range(land.shape[0])]
+                total = total + nn(jnp.concatenate(flat, axis=0), rest[0][...])
+                total = total * QK_SCALE
+            local = total.shape[0] // 2
+            cut = slice(index * local, (index + 1) * local)
+            keep_ref[half, cut, :] = total[:local].astype(BF)
+            send_ref[half, cut, :] = total[local:].astype(BF)
+
+
+def input_grad_kernel(base_ref, *refs):
+    out_ref = refs[-1]
+    lows, pieces = refs[:6], refs[6:10]
+    local = pieces[0].shape[0] // 3
+    weights = []
+    for kind in range(3):
+        cut = slice(kind * local, (kind + 1) * local)
+        for half in (0, 1):
+            parts = [pieces[2 * half][cut, :], pieces[2 * half + 1][cut, :]]
+            weights.append(jnp.concatenate(parts, axis=0))
+    scaled = sum(nn(lows[j][...], weights[j]) for j in range(4))
+    direct = nn(lows[4][...], weights[4]) + nn(lows[5][...], weights[5])
+    out_ref[...] = base_ref[...] + QK_SCALE * scaled + direct
+
+
+def call(body, grid, ins, outs, scratch=(), flops=0, moved=0, limit=20):
     return pl.pallas_call(
         body,
         grid=grid,
@@ -449,17 +526,17 @@
         out_shape=[shape for _, shape in outs],
         scratch_shapes=list(scratch),
         compiler_params=pltpu.CompilerParams(vmem_limit_bytes=limit << 20),
-        cost_estimate=pl.CostEstimate(flops=flops, bytes_accessed=moved, transcendentals=exps),
-    )
-
-
-def plain(body, outs, scratch=(), flops=0, moved=0, limit=40):
+        cost_estimate=pl.CostEstimate(flops=flops // 50, bytes_accessed=moved // 50, transcendentals=0),
+    )
+
+
+def plain(body, outs, scratch=(), flops=0, moved=0, limit=20):
     return pl.pallas_call(
         body,
         out_shape=list(outs),
         scratch_shapes=list(scratch),
         compiler_params=pltpu.CompilerParams(vmem_limit_bytes=limit << 20),
-        cost_estimate=pl.CostEstimate(flops=flops, bytes_accessed=moved, transcendentals=0),
+        cost_estimate=pl.CostEstimate(flops=flops // 50, bytes_accessed=moved // 50, transcendentals=0),
     )
 
 
@@ -519,9 +596,9 @@
         with jax.named_scope(name):
             return lax.ppermute(value, "batch", [(i, i ^ bit) for i in range(batch_size)])
 
-    def spread(value):
-        two = swap(value, 2)
-        return value, swap(value, 1), two, swap(two, 1)
+    def spread(value, name):
+        two = swap(value, 2, name)
+        return value, swap(value, 1, name), two, swap(two, 1, name)
 
     def add_low(a, b):
         return (a.astype(F32) + b.astype(F32)).astype(BF)
@@ -539,18 +616,21 @@
         mine = lax.dynamic_slice_in_dim(value, flag * half, half, 0)
         return mine, lax.dynamic_slice_in_dim(value, (1 - flag) * half, half, 0)
 
-    def head_sum(value):
+    def head_sum(value, name, far=F32):
         mine, other = halves(value, core)
-        mine = mine + swap(other, 1)
-        mine = mine + swap(mine, 2)
-        return ordered(core, mine, swap(mine, 1))
+        mine = mine + swap(other, 1, name)
+        mine = mine.astype(far)
+        mine = mine.astype(F32) + swap(mine, 2, name).astype(F32)
+        return ordered(core, mine, swap(mine, 1, name))
 
     bits = [1 << b for b in range(batch_size.bit_length() - 1)]
 
-    def gather_heads(value):
-        got = lax.all_gather(value, "head", axis=0, tiled=False)
-        parts = [lax.dynamic_index_in_dim(got, me ^ slot, 0, False) for slot in range(groups)]
+    def gather_heads(value, name):
+        parts = value, swap(value, 1, name), swap(value, 2, name), swap(value, 3, name)
         return [jnp.concatenate(parts[2 * half : 2 * half + 2], axis=0) for half in (0, 1)]
+
+    def hop_sum(value, got):
+        return (value.astype(F32) + got.astype(F32)).astype(BF)
 
     code_row = jnp.where(pad_mask > 0, doc_ids, -1)
     outside = jnp.full((BLOCK - HALF,), -2, jnp.int32)
@@ -565,16 +645,17 @@
     member = (segment[:, None] == columns[None, :]).astype(BF)
 
     packed = jnp.concatenate([w_query.T, w_key.T, w_value.T], axis=0)
-    got = spread(packed)
+    got = spread(packed, "weights")
     tap_pad = jnp.pad(conv_weight, ((0, 16 - own), (0, width - KW)))
-    out_parts = spread(jnp.concatenate([w_output, tap_pad], axis=0))
-
-    def weight_half(half, index):
-        return jnp.concatenate(
-            [got[2 * half + j][index * local : (index + 1) * local] for j in (0, 1)], axis=0
-        )
-
-    wq, wk, wv = ([weight_half(half, index) for half in (0, 1)] for index in range(3))
+    out_packed, far_weights = gate(
+        jnp.concatenate([w_output, tap_pad], axis=0), got[2]
+    )
+    got = got[:2] + (far_weights,) + got[3:]
+    out_far = swap(out_packed, 2, "w_output")
+    out_parts = (
+        out_packed, swap(out_packed, 1, "w_output"), out_far, swap(out_far, 1, "w_output")
+    )
+
     wo = [
         jnp.concatenate([out_parts[2 * half + j][:local] for j in (0, 1)], axis=0)
         for half in (0, 1)
@@ -597,18 +678,25 @@
     tokens_ext = with_edges(tokens_in)
 
     land_part = tn(member, tokens_in) / counts[:, None]
-    land_sum = head_sum(land_part)
-    land_tokens, land_rest = split_low(land_sum)
+    land_sum = head_sum(land_part, "land", FAR_TYPE)
+    land_tokens = land_sum.astype(BF)
 
     queries, keys, values, land_q, land_k = [], [], [], [], []
+    low_shape = shape_of((rows, side_cols), BF)
+    land_shape = shape_of((side, HEAD_DIM, SEGS), BF)
     for half in (0, 1):
-        queries.append((nt(tokens_in, wq[half]) * QK_SCALE).astype(BF))
-        keys.append((nt(tokens_in, wk[half]) * QK_SCALE).astype(BF))
-        values.append(nt(tokens_ext, wv[half]).astype(BF))
-        for weight, target in ((wq, land_q), (wk, land_k)):
-            mapped = nt(weight[half], land_tokens) + nt(weight[half], land_rest)
-            mapped = (mapped * QK_SCALE).astype(BF)
-            target.append(mapped.reshape(side, HEAD_DIM, SEGS))
+        one, two = got[2 * half : 2 * half + 2]
+        projected = plain(
+            project_kernel, [low_shape, low_shape, shape_of((ext, side_cols), BF)]
+        )(tokens_ext, one, two)
+        for target, value in zip((queries, keys, values), projected):
+            target.append(value)
+    for half in (0, 1):
+        one, two = got[2 * half : 2 * half + 2]
+        for target, value in zip(
+            (land_q, land_k), plain(landmark_kernel, [land_shape, land_shape])(land_sum, one, two)
+        ):
+            target.append(value)
 
     third_call = call(
         third_kernel,
@@ -621,7 +709,6 @@
         [pltpu.VMEM((rows, WIDE), F32), pltpu.VMEM((BLOCK, WIDE), F32)],
         flops=4 * rows * side_cols * SEGS,
         moved=2 * rows * (side_cols * 2 + side * SEGS),
-        exps=rows * side * SEGS,
     )
     packs, third_exp = [], []
     for half in (0, 1):
@@ -629,28 +716,68 @@
         packs.append(pack)
         third_exp.append(e_out)
 
+    tall = HEAD_DIM + 8
+    pack_keep = jnp.concatenate([part[:own] for part in packs], axis=0)
+    pack_send = jnp.concatenate([part[own:] for part in packs], axis=0)
     docs_shape = shape_of((own, HEAD_DIM, SEGS), F32)
-    own_q, own_k = land_q[0][:own], land_k[0][:own]
+    own_q, own_k, pack_send = gate(land_q[0][:own], land_k[0][:own], pack_send)
+    pack_core = swap(pack_send, 1, "pack")
     inverse, small_t, saved = plain(
         newton_kernel,
         [docs_shape, docs_shape, shape_of((NEWTON, own, 4, HEAD_DIM, SEGS), F32)],
         flops=own * NEWTON * 4 * 6 * LAND * SEGS * SEGS,
         moved=4 * own * NEWTON * 4 * HEAD_DIM * SEGS,
     )(own_q, own_k)
-
-    tall = HEAD_DIM + 8
-    pack_keep = jnp.concatenate([part[:own] for part in packs], axis=0)
-    pack_send = jnp.concatenate([part[own:] for part in packs], axis=0)
+    pack_core, inverse = gate(pack_core, inverse)
     joined = plain(join_kernel, [shape_of((side, tall, SEGS), F32)], moved=12 * side * tall * SEGS)(
-        pack_keep, swap(pack_send, 1)
+        pack_keep, pack_core
     )[0]
+
+    first_call = call(
+        first_kernel,
+        (pairs,),
+        [whole((rows, 1)), column(rows, BLOCK), heads_spec(HEAD_DIM, SEGS)],
+        [(column(rows, WIDE), shape_of((rows, side * SEGS), BF))],
+        flops=2 * rows * side_cols * SEGS,
+        moved=2 * rows * (side_cols + side * SEGS),
+    )
+    conv_call = call(
+        conv_kernel,
+        (pairs,),
+        [whole((rows, 1)), whole((1, ext)), column(ext, BLOCK), heads_spec(1, 2 * BLOCK)],
+        [(column(rows, BLOCK), shape_of((rows, side_cols), F32))],
+        [pltpu.VMEM((2, BLOCK, 2 * BLOCK), BF)],
+        flops=2 * rows * side_cols * SEGS,
+        moved=2 * rows * (side_cols * 3),
+    )
+    heads_call = call(
+        heads_kernel,
+        (pairs,),
+        [
+            whole((rows, 1)),
+            column(rows, WIDE),
+            heads_spec(HEAD_DIM + 16, SEGS),
+            column(rows, BLOCK),
+        ],
+        [(column(rows, BLOCK), shape_of((rows, side_cols), BF))],
+        flops=2 * rows * side_cols * SEGS,
+        moved=2 * rows * (side_cols * 3 + side * SEGS),
+    )
+    wait_in, far_send = gate((queries, values), joined[own:])
+    pack_far = swap(far_send, 2, "pack_x")
+    queries, values = wait_in
+    conv_outs = [
+        conv_call(code, line, values[half], tap_lines(tap_rows[half]))[0] for half in (0, 1)
+    ]
+    first_low = [first_call(code, queries[half], land_k[half])[0] for half in (0, 1)]
+    pack_far, first_low, conv_outs = gate(pack_far, first_low, conv_outs)
     mixed_own, carried = plain(
         mix_kernel,
         [shape_of((own, HEAD_DIM + 16, SEGS), BF), docs_shape],
         flops=6 * own * LAND * SEGS * SEGS,
         moved=16 * own * tall * SEGS,
-    )(joined[:own], swap(joined[own:], 2), inverse)
-    mixed = gather_heads(mixed_own)
+    )(joined[:own], pack_far, inverse)
+    mixed = gather_heads(mixed_own, "mixed")
 
     def row_of(parts):
         return [
@@ -658,42 +785,9 @@
             for part in parts
         ]
 
-    first_call = call(
-        first_kernel,
-        (pairs,),
-        [
-            whole((rows, 1)),
-            whole((1, ext)),
-            column(rows, BLOCK),
-            column(ext, BLOCK),
-            heads_spec(HEAD_DIM, SEGS),
-            heads_spec(1, 2 * BLOCK),
-        ],
-        [
-            (column(rows, WIDE), shape_of((rows, side * SEGS), BF)),
-            (column(rows, BLOCK), shape_of((rows, side_cols), F32)),
-        ],
-        [pltpu.VMEM((2, BLOCK, 2 * BLOCK), BF)],
-        flops=4 * rows * side_cols * SEGS,
-        moved=2 * rows * (side_cols * 4 + side * SEGS),
-        exps=rows * side * SEGS,
-    )
-    heads_call = call(
-        heads_kernel,
-        (pairs,),
-        [whole((rows, 1)), column(rows, WIDE), heads_spec(HEAD_DIM + 16, SEGS), column(rows, BLOCK)],
-        [(column(rows, BLOCK), shape_of((rows, side_cols), BF))],
-        flops=2 * rows * side_cols * SEGS,
-        moved=2 * rows * (side_cols * 3 + side * SEGS),
-    )
-    first_low, heads_out = [], []
-    for half in (0, 1):
-        p_out, conv_out = first_call(
-            code, line, queries[half], values[half], land_k[half], tap_lines(tap_rows[half])
-        )
-        first_low.append(p_out)
-        heads_out.append(heads_call(code, p_out, mixed[half], conv_out)[0])
-
+    heads_out = [
+        heads_call(code, first_low[half], mixed[half], conv_outs[half])[0] for half in (0, 1)
+    ]
     projected = nn(heads_out[0], wo[0]) + nn(heads_out[1], wo[1])
     first_out, first_normed, first_inv = norm_forward(
         tokens_in.astype(F32) + projected, first_gain, first_bias
@@ -712,7 +806,7 @@
         ],
         flops=4 * rows * width * ff,
         moved=2 * (2 * width * ff + 2 * rows * ff + 3 * rows * width),
-        exps=2 * rows * ff,
+        limit=30,
     )(norm_low, w_inner, w_outer)
     second_out, second_normed, second_inv = norm_forward(
         first_out + outer_out, second_gain, second_bias
@@ -755,7 +849,7 @@
                 shape_of((len(slots), share, width), BF),
                 shape_of((rows, width), F32),
             ],
-            compiler_params=pltpu.CompilerParams(vmem_limit_bytes=48 << 20),
+            compiler_params=pltpu.CompilerParams(vmem_limit_bytes=36 << 20),
             cost_estimate=pl.CostEstimate(
                 flops=8 * rows * width * share * len(slots),
                 bytes_accessed=2 * len(slots) * share * (4 * width + 2 * rows) + 12 * rows * width,
@@ -767,7 +861,6 @@
     gi_core, go_core = swap(gi_send, 1, "inner_core"), swap(go_send, 1, "outer_core")
     gi_keep, go_keep, first_grad = feed_back((0, 2), first_grad)
     first_grad, gi_core, go_core = gate(first_grad, gi_core, go_core)
-    inner_far = swap(add_low(gi_keep[1], gi_core[1]), 2, "inner_x")
     outer_flags = [jnp.where((bat & bit) != 0, 1, 0) for bit in bits]
 
     def split_rows(value, flag):
@@ -777,18 +870,27 @@
 
     own_keep, other_keep = split_rows(go_keep, outer_flags[0])
     own_core, other_core = split_rows(go_core, outer_flags[0])
-    outer_near = swap_batch(add_low(other_keep, other_core), bits[0], "outer_y")
+    first_grad, near_send, far_send = gate(
+        first_grad, add_low(other_keep, other_core), add_low(gi_keep[1], gi_core[1])
+    )
+    outer_near = swap_batch(near_send, bits[0], "outer_y")
+    inner_far = swap(far_send, 2, "inner_x")
     first_in_grad, grad_first_gain, grad_first_bias = norm_backward(
         first_grad, first_normed, first_inv, first_gain
     )
     proj_low = first_in_grad.astype(BF)
 
-    proj_ext = with_edges(proj_low)
-    real_ext = line.reshape(ext, 1) >= 0
-    heads_grad_ext = [
-        jnp.where(real_ext, nt(proj_ext, wo[half]), 0.0).astype(BF) for half in (0, 1)
+    def edge_rows(value, name):
+        with jax.named_scope(name):
+            down = [(i, i + 1) for i in range(groups - 1)]
+            up = [(i + 1, i) for i in range(groups - 1)]
+            before = lax.ppermute(value[-HALF:], "head", down)
+            after = lax.ppermute(value[:HALF], "head", up)
+        return jnp.concatenate([before, after], axis=0)
+
+    heads_grad = [
+        jnp.where(code >= 0, nt(proj_low, wo[half]), 0.0).astype(BF) for half in (0, 1)
     ]
-    heads_grad = [part[HALF : HALF + rows] for part in heads_grad_ext]
 
     mixed_grad_call = call(
         mixed_grad_kernel,
@@ -802,22 +904,8 @@
 
     mg_keep = jnp.concatenate([part[:own] for part in mixed_part], axis=0)
     mg_send = jnp.concatenate([part[own:] for part in mixed_part], axis=0)
-    mg_sum = mg_keep + swap(mg_send, 1)
-    mixed_grad, carried_low = plain(
-        carry_back_kernel,
-        [docs_shape, shape_of((own, HEAD_DIM + 16, SEGS), BF)],
-        flops=6 * own * LAND * SEGS * SEGS,
-        moved=24 * own * tall * SEGS,
-    )(mg_sum[:own], swap(mg_sum[own:], 2), carried, inverse)
-    carried_grad = gather_heads(carried_low)
-    small_query, small_key = plain(
-        newton_back_kernel,
-        [docs_shape, docs_shape],
-        [pltpu.VMEM((own, SEGS, SEGS), F32)],
-        flops=own * NEWTON * 8 * 6 * LAND * SEGS * SEGS,
-        moved=4 * own * NEWTON * 4 * HEAD_DIM * SEGS,
-    )(mixed_grad, carried, small_t, saved, own_q, own_k)
-    delta_all, lse_all = row_of(carried_grad), row_of(mixed)
+    heads_grad, mg_keep, mg_send = gate(heads_grad, mg_keep, mg_send)
+    mg_core = swap(mg_send, 1, "mixed_grad")
 
     first_back_call = call(
         first_back_kernel,
@@ -843,17 +931,23 @@
         [
             whole((rows, 1)),
             whole((1, ext)),
-            column(ext, BLOCK),
+            column(rows, BLOCK),
+            column(2 * HALF, BLOCK),
             column(ext, BLOCK),
             heads_spec(1, 2 * BLOCK),
+            column(rows, BLOCK),
         ],
         [
-            (column(rows, BLOCK), shape_of((rows, side_cols), F32)),
+            (column(rows, BLOCK), shape_of((rows, side_cols), BF)),
             (heads_spec(8, 2 * BLOCK), shape_of((side, 8, 2 * BLOCK), F32)),
         ],
-        [pltpu.VMEM((2, BLOCK, 2 * BLOCK), BF), pltpu.VMEM((2, BLOCK, 2 * BLOCK), F32)],
+        [
+            pltpu.VMEM((2, BLOCK, 2 * BLOCK), BF),
+            pltpu.VMEM((2, BLOCK, 2 * BLOCK), F32),
+            pltpu.VMEM((ext, BLOCK), BF),
+        ],
         flops=4 * rows * side_cols * SEGS,
-        moved=2 * rows * side_cols * 4,
+        moved=2 * rows * side_cols * 5,
     )
     third_back_call = call(
         third_back_kernel,
@@ -866,162 +960,231 @@
             heads_spec(1, SEGS),
             heads_spec(HEAD_DIM + 16, SEGS),
             heads_spec(HEAD_DIM, SEGS),
-            column(rows, BLOCK),
         ],
         [
             (column(rows, BLOCK), shape_of((rows, side_cols), BF)),
-            (column(rows, BLOCK), shape_of((rows, side_cols), BF)),
+            (column(rows, BLOCK), shape_of((rows, side_cols), F32)),
             (heads_spec(HEAD_DIM, SEGS), shape_of((side, HEAD_DIM, SEGS), F32)),
         ],
         [pltpu.VMEM((BLOCK, WIDE), F32)],
         flops=8 * rows * side_cols * SEGS,
         moved=2 * rows * (side_cols * 6 + side * SEGS),
     )
-    def hop_sum(value, got):
-        return (value.astype(F32) + got.astype(F32)).astype(BF)
-
     def slot_parts(parts):
         cut_rows = parts[0].shape[0] // 2
         keep = [part[:cut_rows] for part in parts]
         send = jnp.stack([part[cut_rows:] for part in parts])
         return keep, send
 
-    out_keep, out_send = slot_parts([tn(part, proj_low).astype(BF) for part in heads_out])
-    out_core = swap(out_send, 1, "out_core")
-
-    dq_parts, lkg_parts, backs, tap_grads = [], [], [], []
+    def grads_call(count, with_land, *args):
+        shape = shape_of((2, count * local, width), BF)
+        return plain(
+            functools.partial(weight_grad_kernel, count, with_land), [shape, shape], limit=28
+        )(*args)
+
+    def spread_sum(keep, near, far):
+        return (keep[0].astype(F32) + near[0].astype(F32) + far.astype(F32)).astype(BF)
+
+    dq_parts, lkg_parts = [], []
     for half in (0, 1):
         dq, lkg = first_back_call(
             heads_grad[half], first_low[half], queries[half], mixed[half], land_k[half]
         )
         dq_parts.append(dq)
         lkg_parts.append(lkg)
-
-    conv_in, lkg_parts[1], inner_far, outer_near, out_core = gate(
-        heads_grad_ext[0], lkg_parts[1], inner_far, outer_near, out_core
-    )
+        if half == 0:
+            mg_core, lkg_parts, dq_parts = gate(mg_core, lkg_parts, dq_parts)
+            mg_sum = mg_keep + mg_core
+            heads_grad, mg_sum = gate(heads_grad, mg_sum)
+            mg_far = swap(mg_sum[own:], 2, "mixed_grad_x")
+            edges = edge_rows(proj_low, "grad_edges")
+    heads_out, dq_parts, lkg_parts, edges = gate(heads_out, dq_parts, lkg_parts, edges)
+    out_keep, out_send = grads_call(1, False, proj_low, *heads_out)
+    out_core = swap(out_send, 1, "out_core")
+
+    mg_sum, mg_far, out_core = gate(mg_sum, mg_far, out_core)
+    mixed_grad, carried_low = plain(
+        carry_back_kernel, [docs_shape, shape_of((own, HEAD_DIM + 16, SEGS), BF)]
+    )(mg_sum[:own], mg_far, carried, inverse)
+    carried_low, mixed_grad, outer_near, inner_far = gate(
+        carried_low, mixed_grad, outer_near, inner_far
+    )
+    carried_grad = gather_heads(carried_low, "carried_grad")
     inner = (gi_keep[0].astype(F32) + gi_core[0].astype(F32) + inner_far.astype(F32)).astype(BF)
-    inner, other = halves(inner, outer_flags[0])
-    inner_hop = swap_batch(other, bits[0], "inner_y")
+    inner, inner_send = halves(inner, outer_flags[0])
     outer = (own_keep.astype(F32) + own_core.astype(F32) + outer_near.astype(F32)).astype(BF)
-    outer, other = split_rows(outer, outer_flags[1])
-    outer_hop = swap_batch(other, bits[1], "outer_z")
-    out_far = swap(add_low(out_keep[1], out_core[1]), 2, "out_x")
-    for half in (0, 1):
-        back, tap_out = conv_back_call(
-            code, line, (conv_in, heads_grad_ext[1])[half], values[half],
-            tap_lines(tap_rows[half][:, ::-1]),
-        )
-        backs.append(back)
-        tap_grads.append(tap_out[:, 0, :KW])
-
-    exp_in, small_query, inner_hop, outer_hop, out_far = gate(
-        third_exp[0], small_query, inner_hop, outer_hop, out_far
-    )
-    inner, other = halves(hop_sum(inner, inner_hop), outer_flags[1])
-    inner_hop = swap_batch(other, bits[1], "inner_z")
-    outer, other = split_rows(hop_sum(outer, outer_hop), outer_flags[2])
-    outer_hop = swap_batch(other, bits[2], "outer_w")
-    out_sum = out_keep[0].astype(F32) + out_core[0].astype(F32) + out_far.astype(F32)
-    out_sum = out_sum.astype(BF)
-    out_hop = swap_batch(out_sum, bits[0], "out_y")
-
+    outer, outer_send = split_rows(outer, outer_flags[1])
+    mixed_grad, inner_send, outer_send = gate(mixed_grad, inner_send, outer_send)
+    inner_hop = swap_batch(inner_send, bits[0], "inner_y")
+    outer_hop = swap_batch(outer_send, bits[1], "outer_z")
+    small_query, small_key = plain(
+        newton_back_kernel, [docs_shape, docs_shape], [pltpu.VMEM((own, SEGS, SEGS), F32)]
+    )(mixed_grad, carried, small_t, saved, own_q, own_k)
+
+    small_query, small_key, carried_grad = gate(small_query, small_key, carried_grad)
+    delta_all, lse_all = row_of(carried_grad), row_of(mixed)
     dk_parts, dv_parts, lqg_parts = [], [], []
     for half in (0, 1):
         factor = jnp.exp(packs[half][:, HEAD_DIM : HEAD_DIM + 1] - lse_all[half])
+        third_in = third_exp[half]
+        if half == 1:
+            third_in, lqg_parts, inner_hop, outer_hop = gate(
+                third_in, lqg_parts, inner_hop, outer_hop
+            )
+            inner = hop_sum(inner, inner_hop)
+            outer = hop_sum(outer, outer_hop)
+            third_in, inner, outer, out_send = gate(
+                third_in, inner, outer, add_low(out_keep[1], out_core[1])
+            )
+            outer_hop = swap_batch(outer, bits[2], "outer_w")
+            inner_hop = swap_batch(inner, bits[1], "inner_z")
+            out_far = swap(out_send, 2, "out_x")
         dk, dv, lqg = third_back_call(
-            keys[half],
-            values[half],
-            (exp_in, third_exp[1])[half],
-            factor,
-            delta_all[half],
-            carried_grad[half],
+            keys[half], values[half], third_in, factor, delta_all[half], carried_grad[half],
             land_q[half],
-            backs[half],
         )
         dk_parts.append(dk)
         dv_parts.append(dv)
         lqg_parts.append(lqg)
     lqg_parts[0] = jnp.concatenate([lqg_parts[0][:own] + small_query, lqg_parts[0][own:]], axis=0)
     lkg_parts[0] = jnp.concatenate([lkg_parts[0][:own] + small_key, lkg_parts[0][own:]], axis=0)
-    land_qg = [part.reshape(side_cols, SEGS).astype(BF) for part in lqg_parts]
-    land_kg = [part.reshape(side_cols, SEGS).astype(BF) for part in lkg_parts]
-
-    def weight_parts(lows, lands, factor):
-        parts = []
-        for half in (0, 1):
-            part = tn(lows[half], tokens_in)
-            if lands is not None:
-                part = part + nn(lands[half], land_tokens)
-            parts.append((part * factor).astype(BF))
-        return slot_parts(parts)
-
-    val_keep, val_send = weight_parts(dv_parts, None, 1.0)
+
+    dk_parts, lqg_parts, lkg_parts = gate(dk_parts, lqg_parts, lkg_parts)
+    pair_keep, pair_send = grads_call(
+        2, True, tokens_in, *dk_parts, *dq_parts, land_tokens, *lkg_parts, *lqg_parts
+    )
+    def flat(parts):
+        return [part.reshape(side_cols, SEGS).astype(BF) for part in parts]
+
+    def weight_rows(half, kind):
+        cut = slice(kind * local, (kind + 1) * local)
+        return jnp.concatenate([got[2 * half][cut], got[2 * half + 1][cut]], axis=0)
+
+    land_back = sum(
+        tn(land, weight_rows(half, kind))
+        for kind, lands in ((0, flat(lqg_parts)), (1, flat(lkg_parts)))
+        for half, land in enumerate(lands)
+    )
+    land_mine, land_send = halves(QK_SCALE * land_back / counts[:, None], core)
+    dv_parts, pair_send, land_send = gate(dv_parts, pair_send, land_send)
+    pair_core = swap(pair_send, 1, "pair_core")
+    land_hop = swap(land_send, 1, "land_core")
+    edge_code = jnp.concatenate([line[0, :HALF], line[0, HALF + rows : 2 * HALF + rows]])
+    edge_real = edge_code.reshape(2 * HALF, 1) >= 0
+    edge_parts = [
+        jnp.where(edge_real, nt(edges, wo[half]), 0.0).astype(BF) for half in (0, 1)
+    ]
+    tap_grads = []
+    for half in (0, 1):
+        if half == 1:
+            pair_core, land_hop, tap_grads, dv_parts = gate(
+                pair_core, land_hop, tap_grads, dv_parts
+            )
+            land_mine = (land_mine + land_hop).astype(BF)
+            dv_parts, pair_far_send, land_mine = gate(
+                dv_parts, add_low(pair_keep[1], pair_core[1]), land_mine
+            )
+            pair_far = swap(pair_far_send, 2, "pair_x")
+            land_hop = swap(land_mine, 2, "land_x")
+        dv_parts[half], tap_out = conv_back_call(
+            code, line, heads_grad[half], edge_parts[half], values[half],
+            tap_lines(tap_rows[half][:, ::-1]), dv_parts[half],
+        )
+        tap_grads.append(tap_out[:, 0, :KW])
+    dv_parts, tap_grads, inner_hop, outer_hop, out_far, land_hop = gate(
+        dv_parts, tap_grads, inner_hop, outer_hop, out_far, land_hop
+    )
+    inner = hop_sum(inner, inner_hop)
+    outer = hop_sum(outer, outer_hop)
+    out_sum = spread_sum(out_keep, out_core, out_far)
+    land_mine = land_mine.astype(F32) + land_hop.astype(F32)
+    dv_parts, inner, outer, out_sum, land_mine = gate(dv_parts, inner, outer, out_sum, land_mine)
+    outer_hop = swap(outer[1], 2, "outer_x")
+    inner_hop = swap_batch(inner, bits[2], "inner_w")
+    out_hop = swap_batch(out_sum, bits[0], "out_y")
+    land_hop = swap(land_mine, 1, "land_core")
+    val_keep, val_send = grads_call(1, False, tokens_in, *dv_parts)
+    norms = jnp.stack([grad_first_gain, grad_first_bias, grad_second_gain, grad_second_bias])
+
+    def small_rows(first):
+        lines = [
+            jnp.concatenate([norms, jnp.pad(part[first : first + own], ((0, 0), (0, width - KW)))])
+            for part in tap_grads
+        ]
+        return jnp.pad(jnp.stack(lines), ((0, 0), (0, 16 - 4 - own), (0, 0))).astype(BF)
+
+    val_keep = jnp.concatenate([val_keep, small_rows(0)], axis=1)
+    val_send = jnp.concatenate([val_send, small_rows(own)], axis=1)
+    val_send, pair_far, land_hop = gate(val_send, pair_far, land_hop)
+    land_back = ordered(core, land_mine, land_hop).astype(BF)
+    pair_sum = spread_sum(pair_keep, pair_core, pair_far)
+    pair_sum, pair_other = halves(pair_sum, outer_flags[0])
+    val_send, pair_other = gate(val_send, pair_other)
+    pair_hop = swap_batch(pair_other, bits[0], "pair_y")
     val_core = swap(val_send, 1, "val_core")
-    dk_parts[1], inner_hop, outer_hop, out_hop = gate(dk_parts[1], inner_hop, outer_hop, out_hop)
-    inner, other = halves(hop_sum(inner, inner_hop), outer_flags[2])
-    inner_hop = swap_batch(other, bits[2], "inner_w")
-    outer = hop_sum(outer, outer_hop)
-    outer_hop = swap(outer[1], 2, "outer_x")
-    out_sum = hop_sum(out_sum, out_hop)
-    out_hop = swap_batch(out_sum, bits[1], "out_z")
-
-    key_keep, key_send = weight_parts(dk_parts, land_kg, QK_SCALE)
-    key_core = swap(key_send, 1, "key_core")
-    val_far = swap(add_low(val_keep[1], val_core[1]), 2, "val_x")
-    que_keep, que_send = weight_parts(dq_parts, land_qg, QK_SCALE)
-    que_core = swap(que_send, 1, "que_core")
-    key_far = swap(add_low(key_keep[1], key_core[1]), 2, "key_x")
-
-    que_core, inner_hop, outer_hop, out_hop = gate(que_core, inner_hop, outer_hop, out_hop)
-    que_far = swap(add_low(que_keep[1], que_core[1]), 2, "que_x")
-    inner = hop_sum(inner, inner_hop)
+    val_core, dv_parts = gate(val_core, dv_parts)
+    dv_parts, val_far_send = gate(dv_parts, add_low(val_keep[1], val_core[1]))
+    val_far = swap(val_far_send, 2, "val_x")
+    row_block = 2 * BLOCK
+    rows_spec = pl.BlockSpec((row_block, side_cols), lambda p: (p, 0))
+    full_spec = pl.BlockSpec((row_block, width), lambda p: (p, 0))
+    input_part = call(
+        input_grad_kernel,
+        (rows // row_block,),
+        [full_spec] + [rows_spec] * 6 + [whole((3 * local, width))] * 4,
+        [(full_spec, shape_of((rows, width), F32))],
+    )(first_in_grad, *dq_parts, *dk_parts, *dv_parts, *got)[0]
+
+    input_part, outer_hop, pair_hop, val_far, out_hop = gate(
+        input_part, outer_hop, pair_hop, val_far, out_hop
+    )
+    val_sum = spread_sum(val_keep, val_core, val_far)
+    pair_sum = hop_sum(pair_sum, pair_hop)
     outer = hop_sum(outer[0], outer_hop)
     out_sum = hop_sum(out_sum, out_hop)
-    inner_hop = swap_batch(inner, bits[2], "inner_w2")
-    outer_hop = swap_batch(outer, bits[2], "outer_w2")
-    out_hop = swap_batch(out_sum, bits[2], "out_w")
-    land_back = sum(tn(land_qg[half], wq[half]) + tn(land_kg[half], wk[half]) for half in (0, 1))
-    land_back = head_sum(QK_SCALE * land_back / counts[:, None]).astype(BF)
-    scaled = sum(nn(dq_parts[half], wq[half]) + nn(dk_parts[half], wk[half]) for half in (0, 1))
-    direct = sum(nn(dv_parts[half], wv[half]) for half in (0, 1))
-    input_grad = (first_in_grad + QK_SCALE * scaled + direct + nn(member, land_back)).astype(BF)
-
-    tails = []
-    for keep, near, far, order, name in (
-        (val_keep, val_core, val_far, (0, 1, 2), "val"),
-        (key_keep, key_core, key_far, (1, 2, 0), "key"),
-        (que_keep, que_core, que_far, (2, 0, 1), "que"),
-    ):
-        total = keep[0].astype(F32) + near[0].astype(F32) + far.astype(F32)
-        tails.append((total.astype(BF), order, name))
-    inner = ordered(outer_flags[2], inner, inner_hop)
-    outer = ordered(outer_flags[2], outer, outer_hop)
+    val_hop = swap_batch(val_sum, bits[0], "val_y")
+    pair_hop = swap_batch(pair_sum, bits[2], "pair_w")
+    outer_hop = swap_batch(outer, bits[1], "outer_z2")
+    out_hop = swap_batch(out_sum, bits[1], "out_z")
+    input_grad = (input_part + nn(member, land_back)).astype(BF)
+
+    input_grad, pair_hop, val_hop, outer_hop = gate(input_grad, pair_hop, val_hop, outer_hop)
+    pair_sum = hop_sum(pair_sum, pair_hop)
+    val_sum = hop_sum(val_sum, val_hop)
+    outer = ordered(outer_flags[1], outer, outer_hop)
+    for bit in bits[3:]:
+        outer = hop_sum(outer, swap_batch(outer, bit, "outer_more"))
+    pair_hop = swap_batch(pair_sum, bits[1], "pair_z")
+    val_hop = swap_batch(val_sum, bits[2], "val_w")
+    outer_hop = swap_batch(outer, bits[0], "outer_y2")
+    inner_hop, out_hop, pair_sum = gate(inner_hop, out_hop, pair_sum)
+    inner = hop_sum(inner, inner_hop)
     out_sum = hop_sum(out_sum, out_hop)
     for bit in bits[3:]:
         inner = hop_sum(inner, swap_batch(inner, bit, "inner_more"))
-        outer = hop_sum(outer, swap_batch(outer, bit, "outer_more"))
         out_sum = hop_sum(out_sum, swap_batch(out_sum, bit, "out_more"))
-    grad_output = out_sum.astype(F32)
-    inner = ordered(outer_flags[1], inner, swap_batch(inner, bits[1], "inner_z2"))
-    outer = ordered(outer_flags[1], outer, swap_batch(outer, bits[1], "outer_z2"))
-    grad_inner = ordered(outer_flags[0], inner, swap_batch(inner, bits[0], "inner_y2")).astype(F32)
-    grad_outer = ordered(outer_flags[0], outer, swap_batch(outer, bits[0], "outer_y2")).astype(F32)
-    sums = []
-    for total, order, name in tails:
-        for index in order + tuple(range(3, len(bits))):
-            total = hop_sum(total, swap_batch(total, bits[index], name))
-        sums.append(total.astype(F32).T)
-    grad_value, grad_key, grad_query = sums
-
-    norms = jnp.stack([grad_first_gain, grad_first_bias, grad_second_gain, grad_second_bias])
-    tap_lines_own = [jnp.pad(part, ((0, 0), (0, width - KW))) for part in tap_grads]
-    keep = jnp.concatenate([norms] + [part[:own] for part in tap_lines_own], axis=0)
-    send = jnp.concatenate([norms] + [part[own:] for part in tap_lines_own], axis=0)
-    keep = keep + swap(send, 1)
-    small = keep[: 4 + own] + swap(jnp.concatenate([keep[:4], keep[4 + own :]], axis=0), 2)
-    for bit in bits:
-        small = small + swap_batch(small, bit)
+    inner_hop = swap_batch(inner, bits[0], "inner_y2")
+    out_hop = swap_batch(out_sum, bits[2], "out_w")
+
+    pair_hop, val_hop, inner = gate(pair_hop, val_hop, inner)
+    pair_sum = hop_sum(pair_sum, pair_hop)
+    val_sum = hop_sum(val_sum, val_hop)
+    for bit in bits[3:]:
+        pair_sum = hop_sum(pair_sum, swap_batch(pair_sum, bit, "pair_more"))
+        val_sum = hop_sum(val_sum, swap_batch(val_sum, bit, "val_more"))
+    pair_hop = swap_batch(pair_sum, bits[0], "pair_y2")
+    val_hop = swap_batch(val_sum, bits[1], "val_z")
+    outer_hop, out_hop, pair_sum = gate(outer_hop, out_hop, pair_sum)
+    grad_outer = ordered(outer_flags[0], outer, outer_hop).astype(F32)
+    grad_output = hop_sum(out_sum, out_hop).astype(F32)
+    inner_hop, grad_outer = gate(inner_hop, grad_outer)
+    grad_inner = ordered(outer_flags[0], inner, inner_hop).astype(F32)
+    pair_sum = ordered(outer_flags[0], pair_sum, pair_hop)
+    val_sum = hop_sum(val_sum, val_hop)
+    grad_key, grad_query, grad_value = (
+        part.astype(F32).T for part in (pair_sum[:local], pair_sum[local:], val_sum[:local])
+    )
+    small = val_sum[local:].astype(F32)
     return (
         layer_out,
         input_grad,

time: 444 us -> 428 us (0.964)
  matrix products: 42.4 us -> 11.3 us
  Pallas kernels: 130 us -> 158 us
  local copies, waits for them, and re-layouts: 33.1 us -> 47.9 us
  blocking collectives: 14.2 us -> 0 us
  starting transfers between devices: 63.5 us -> 52.1 us
  waiting for transfers between devices: 101 us -> 94.2 us
  other arithmetic: 49.2 us -> 54.5 us
    pallas_call x8 -> x18, Pallas kernels: 35.9 us -> 67.6 us  [the longest x2 11.8 us: shards(): conv_back_call(code, line, heads_grad[half], edge_parts[half], values[hal...]
    dot_general x13 -> x3, matrix products: 18.3 us -> 2.76 us  [nn(): lax.dot_general(a, b, (((1,), (0,)), ((), ())), preferred_element_type=F32)]
    ppermute x27 -> x19, starting transfers between devices: 35.9 us -> 20.5 us  [swap_batch(): lax.ppermute(value, 'batch', [(i, i ^ bit) for i in range(batch_size)])]
    ppermute x27 -> x19, waiting for transfers between devices: 79.7 us -> 64.6 us  [swap_batch(): lax.ppermute(value, 'batch', [(i, i ^ bit) for i in range(batch_size)])]
    all_gather x2 -> x0, blocking collectives: 14.2 us -> none  [gather_heads(): got = lax.all_gather(value, 'head', axis=0, tiled=False)]
    unnamed x299 -> x288, local copies, waits for them, and re-layouts: 19.9 us -> 32.2 us
    dot_general x13 -> x5, matrix products: 12.8 us -> 3.88 us  [tn(): lax.dot_general(a, b, (((0,), (0,)), ((), ())), preferred_element_type=F32)]
    ppermute x30 -> x32, waiting for transfers between devices: 21.3 us -> 29.6 us  [swap(): return lax.ppermute(value, 'head', [(i, i ^ bit) for i in range(groups)])]
  transfers between devices with their start and end apart: 61 -> 55, of which waited for: 18 -> 11; matrix products, arithmetic and copies ran while one was open for 17% -> 13% of each run, Pallas kernels for 18% -> 26%
where the time goes in v3:
time: 428 us; the launch traced here: 422 us
  Pallas kernels  158 us (37%)
  waiting for transfers between devices  94.2 us (22%)
  other arithmetic  54.5 us (13%)
  starting transfers between devices  52.1 us (12%)
  local copies, waits for them, and re-layouts  47.9 us (11%)
  matrix products  11.3 us (3%)
    ppermute x19, waiting for transfers between devices, swap_batch(): lax.ppermute(value, 'batch', [(i, i ^ bit) for i in range(batch_size)])  64.6 us
    pallas_call x2, Pallas kernels, feed_back(): pl.pallas_call(feed_back_kernel, grid_spec=grid_spec, out_shape=[shape_of...  35.8 us
    unnamed x288, local copies, waits for them, and re-layouts  32.2 us
    ppermute x32, waiting for transfers between devices, swap(): return lax.ppermute(value, 'head', [(i, i ^ bit) for i in range(groups)])  29.6 us
    ppermute x32, starting transfers between devices, swap(): return lax.ppermute(value, 'head', [(i, i ^ bit) for i in range(groups)])  22.8 us
    ppermute x19, starting transfers between devices, swap_batch(): lax.ppermute(value, 'batch', [(i, i ^ bit) for i in range(batch_size)])  20.5 us
    pallas_call x1, Pallas kernels, shards(): call(feed_kernel, (ff // block,), [whole((rows, width)), column(width, bl...  16.8 us
    pallas_call x2, Pallas kernels, shards(): conv_back_call(code, line, heads_grad[half], edge_parts[half], values[hal...  11.8 us
  transfers between devices with their start and end apart: 55, of which 11 were waited for; matrix products, arithmetic and copies ran while one was open for 13% of the time, Pallas kernels for 26%

profile of v3, /device:TPU:0, one launch (start us, length us, event | category | flops | bytes accessed | tf_op | source)
XLA Modules:
  0.0 422.0 jit_solution(7858036919576358919)
XLA Ops:
  12.4 3.0 collective-permute-start
  20.8 8.8 %collective-permute-done.6 = bf16[128,768]{1,0:T(8,128)(2,1)S(1)} collective-permute-done((bf16[128,768]{1,0:T(8,128)(2,1)S(1)}, bf16[128,768]{1,0:T(8,128)(2,1)S(1)}, u32[]{:S(2)}, u32[]{:S(2)}) %collective-permute-start.6) | collective-permute-done | bytes 196640 | tf_op jit(solution)/shard_map/land/ppermute | solution.py:593
  32.5 4.0 shard_map.255
  40.8 4.3 %shard_map.258 = (f32[6,72,256]{2,1,0:T(8,128)S(1)}, bf16[1024,1536]{1,0:T(8,128)(2,1)S(1)}) custom-call(s32[1024,1]{1,0:T(8,128)S(1)} %copy.57.code_ref, bf16[1024,384]{1,0:T(8,128)(2,1)S(1)} %get-tuple-element.196.k_ref, bf16[1152,384]{1,0:T(8,128)(2,1)S(1)} %get-tuple-element.212.v_ref, bf16[6,64,256]{2,1,0:T(8,128)(2,1)S(1)} %get-tuple-element.197.lq_ref), custom_call_target="tpu_custom_call" | custom-call | flops 8053063 | bytes 94371 | tf_op jit(solution)/shard_map/pallas_call | solution.py:715
  46.8 4.4 %shard_map.256 = (bf16[1024,384]{1,0:T(8,128)(2,1)S(1)}, bf16[1024,384]{1,0:T(8,128)(2,1)S(1)}, bf16[1152,384]{1,0:T(8,128)(2,1)S(1)}) custom-call(bf16[1152,768]{1,0:T(8,128)(2,1)S(1)} %maximum_maximum_fusion.x_ref, bf16[576,768]{1,0:T(8,128)(2,1)} %collective-permute-done.3.one_ref.refs_8_, bf16[576,768]{1,0:T(8,128)(2,1)S(1)} %collective-permute-done.4.two_ref.refs_9_), custom_call_target="tpu_custom_call" | custom-call | tf_op jit(solution)/shard_map/pallas_call | solution.py:689
  51.2 3.0 shard_map.259
  55.0 4.0 shard_map.260
  67.2 5.4 %shard_map.261 = (f32[3,64,256]{2,1,0:T(8,128)S(1)}, f32[3,64,256]{2,1,0:T(8,128)S(1)}, f32[6,3,4,64,256]{4,3,2,1,0:T(8,128)S(1)}) custom-call(bf16[3,64,256]{2,1,0:T(8,128)(2,1)S(1)} %slice.237.lq_ref, bf16[3,64,256]{2,1,0:T(8,128)(2,1)S(1)} %copy-done.74), custom_call_target="tpu_custom_call" | custom-call | flops 36238784 | bytes 94371 | tf_op jit(solution)/shard_map/pallas_call | solution.py:725
  77.0 4.1 shard_map.263.p_ref
  81.2 4.7 %shard_map.264.p_ref = bf16[1024,1536]{1,0:T(8,128)(2,1)S(1)} custom-call(s32[1024,1]{1,0:T(8,128)S(1)} %copy.57.code_ref, bf16[1024,384]{1,0:T(8,128)(2,1)S(1)} %copy-done.46, bf16[6,64,256]{2,1,0:T(8,128)(2,1)S(1)} %copy-done.77), custom_call_target="tpu_custom_call" | custom-call | flops 4026531 | bytes 78643 | tf_op jit(solution)/shard_map/pallas_call | solution.py:772
  88.9 3.0 shard_map.266.conv_ref
  99.0 4.9 %collective-permute-done.15 = bf16[3,80,256]{2,1,0:T(8,128)(2,1)S(1)} collective-permute-done((bf16[3,80,256]{2,1,0:T(8,128)(2,1)S(1)}, bf16[3,80,256]{2,1,0:T(8,128)(2,1)S(1)}, u32[]{:S(2)}, u32[]{:S(2)}) %collective-permute-start.15) | collective-permute-done | bytes 122912 | tf_op jit(solution)/shard_map/mixed/ppermute | solution.py:593
  111.3 16.8 %shard_map.270 = (bf16[1024,3072]{1,0:T(8,128)(2,1)S(1)}, bf16[1024,3072]{1,0:T(8,128)(2,1)}, f32[1024,768]{1,0:T(8,128)S(1)}) custom-call(bf16[1024,768]{1,0:T(8,128)(2,1)S(1)} %fusion.8.x_ref, bf16[768,3072]{1,0:T(8,128)(2,1)S(1)} %bitcast.86, bf16[3072,768]{1,0:T(8,128)(2,1)S(1)} %bitcast.88), custom_call_target="tpu_custom_call" | custom-call | flops 193273536 | bytes 534773 | tf_op jit(solution)/shard_map/pallas_call | solution.py:798
  136.6 18.1 %shard_map.271 = (bf16[2,768,768]{2,1,0:T(8,128)(2,1)}, bf16[2,768,768]{2,1,0:T(8,128)(2,1)}, f32[1024,768]{1,0:T(8,128)S(1)}) custom-call(s32[4]{0:T(128)S(1)} %get-tuple-element.436.table, bf16[1024,768]{1,0:T(8,128)(2,1)S(1)} %get-tuple-element.384.og_ref, bf16[1024,768]{1,0:T(8,128)(2,1)S(1)} %fusion.8.x_ref, bf16[768,3072]{1,0:T(8,128)(2,1)} %wi_ref.5, ...), custom_call_target="tpu_custom_call" | custom-call | flops 9663676416 | bytes 25165824 | tf_op jit(solution)/shard_map/pallas_call | solution.py:844
  164.0 17.7 %shard_map.272 = (bf16[2,768,768]{2,1,0:T(8,128)(2,1)S(1)}, bf16[2,768,768]{2,1,0:T(8,128)(2,1)S(1)}, f32[1024,768]{1,0:T(8,128)S(1)}) custom-call(s32[4]{0:T(128)S(1)} %get-tuple-element.435.table, bf16[1024,768]{1,0:T(8,128)(2,1)S(1)} %copy-done.63, bf16[1024,768]{1,0:T(8,128)(2,1)S(1)} %copy-done.26, bf16[768,3072]{1,0:T(8,128)(2,1)} %wi_ref.5, ...), custom_call_target="tpu_custom_call" | custom-call | flops 9663676416 | bytes 25165824 | tf_op jit(solution)/shard_map/pallas_call | solution.py:844
  198.8 3.0 collective-permute-start.19
  205.0 4.8 %shard_map.275 = (bf16[1024,384]{1,0:T(8,128)(2,1)S(1)}, f32[6,64,256]{2,1,0:T(8,128)S(1)}) custom-call(bf16[1024,384]{1,0:T(8,128)(2,1)S(1)} %select_convert_fusion.1.hg_ref, bf16[1024,1536]{1,0:T(8,128)(2,1)S(1)} %copy-done.3, bf16[1024,384]{1,0:T(8,128)(2,1)S(1)} %copy-done.44, bf16[6,80,256]{2,1,0:T(8,128)(2,1)S(1)} %constant_dynamic-update-slice_fusion.mix_ref, ...), custom_call_target="tpu_custom_call" | custom-call | flops 12079595 | bytes 110100 | tf_op jit(solution)/shard_map/pallas_call | solution.py:990
  210.1 5.2 %shard_map.276 = (bf16[1024,384]{1,0:T(8,128)(2,1)S(1)}, f32[6,64,256]{2,1,0:T(8,128)S(1)}) custom-call(bf16[1024,384]{1,0:T(8,128)(2,1)S(1)} %select_convert_fusion.hg_ref, bf16[1024,1536]{1,0:T(8,128)(2,1)S(1)} %copy-done.1, bf16[1024,384]{1,0:T(8,128)(2,1)S(1)} %copy-done.47, bf16[6,80,256]{2,1,0:T(8,128)(2,1)S(1)} %constant_dynamic-update-slice_fusion.2.mix_ref, ...), custom_call_target="tpu_custom_call" | custom-call | flops 12079595 | bytes 110100 | tf_op jit(solution)/shard_map/pallas_call | solution.py:990
  220.4 15.8 %collective-permute-done.21.b_ref = f32[3,64,256]{2,1,0:T(8,128)S(1)} collective-permute-done((f32[3,64,256]{2,1,0:T(8,128)S(1)}, f32[3,64,256]{2,1,0:T(8,128)S(1)}, u32[]{:S(2)}, u32[]{:S(2)}) %collective-permute-start.21) | collective-permute-done | bytes 196640 | tf_op jit(solution)/shard_map/mixed_grad_x/ppermute | solution.py:593
  245.7 9.9 %shard_map.279 = (f32[3,64,256]{2,1,0:T(8,128)S(1)}, f32[3,64,256]{2,1,0:T(8,128)S(1)}) custom-call(f32[3,64,256]{2,1,0:T(8,128)S(1)} %get-tuple-element.264.mg_ref, f32[3,64,256]{2,1,0:T(8,128)S(1)} %copy-done.82, f32[3,64,256]{2,1,0:T(8,128)S(1)} %copy-done.90, f32[6,3,4,64,256]{4,3,2,1,0:T(8,128)S(1)} %bitcast.84, bf16[3,64,256]{2,1,0:T(8,128)(2,1)S(1)} %copy-done.73, ...), custom_call_target="tpu_custom_call" | custom-call | tf_op jit(solution)/shard_map/pallas_call | solution.py:1020
  255.9 4.8 %shard_map.280 = (bf16[1024,384]{1,0:T(8,128)(2,1)S(1)}, f32[1024,384]{1,0:T(8,128)S(1)}, f32[6,64,256]{2,1,0:T(8,128)S(1)}) custom-call(bf16[1024,384]{1,0:T(8,128)(2,1)S(1)} %copy-done.55, bf16[1152,384]{1,0:T(8,128)(2,1)S(1)} %copy-done.11, bf16[1024,1536]{1,0:T(8,128)(2,1)S(1)} %copy-done.51, f32[6,1,256]{2,1,0:T(1,128)S(1)} %subtract_exponential_fusion.1.f_ref, ...), custom_call_target="tpu_custom_call" | custom-call | flops 16106127 | bytes 157286 | tf_op jit(solution)/shard_map/pallas_call | solution.py:1042
  264.4 4.6 %shard_map.281 = (bf16[1024,384]{1,0:T(8,128)(2,1)S(1)}, f32[1024,384]{1,0:T(8,128)S(1)}, f32[6,64,256]{2,1,0:T(8,128)S(1)}) custom-call(bf16[1024,384]{1,0:T(8,128)(2,1)S(1)} %copy-done.53, bf16[1152,384]{1,0:T(8,128)(2,1)S(1)} %copy-done.7, bf16[1024,1536]{1,0:T(8,128)(2,1)S(1)} %copy-done.49, f32[6,1,256]{2,1,0:T(1,128)S(1)} %subtract_exponential_fusion.f_ref, ...), custom_call_target="tpu_custom_call" | custom-call | flops 16106127 | bytes 157286 | tf_op jit(solution)/shard_map/pallas_call | solution.py:1042
  273.6 4.3 %shard_map.282 = (bf16[2,384,768]{2,1,0:T(8,128)(2,1)S(1)}, bf16[2,384,768]{2,1,0:T(8,128)(2,1)}) custom-call(bf16[1024,768]{1,0:T(8,128)(2,1)S(1)} %copy-done.4, bf16[1024,384]{1,0:T(8,128)(2,1)S(1)} %get-tuple-element.290.refs_0_.refs_2_, bf16[1024,384]{1,0:T(8,128)(2,1)S(1)} %get-tuple-element.291.refs_1_.refs_3_, ...), custom_call_target="tpu_custom_call" | custom-call | tf_op jit(solution)/shard_map/pallas_call | solution.py:981
  284.1 5.8 %shard_map.283 = (bf16[1024,384]{1,0:T(8,128)(2,1)S(1)}, f32[6,8,256]{2,1,0:T(8,128)S(1)}) custom-call(s32[1024,1]{1,0:T(8,128)S(1)} %copy.57.code_ref, s32[1,1152]{1,0:T(1,128)S(1)} %reshape.159.line_ref, bf16[1024,384]{1,0:T(8,128)(2,1)S(1)} %copy-done.24, bf16[32,384]{1,0:T(8,128)(2,1)S(1)} %fusion.15.edge_ref, bf16[1152,384]{1,0:T(8,128)(2,1)S(1)} %copy-done.12, ...), custom_call_target="tpu_custom_call" | custom-call | flops 8053063 | bytes 78643 | tf_op jit(solution)/shard_map/pallas_call | solution.py:1089
  297.0 6.0 %shard_map.284 = (bf16[1024,384]{1,0:T(8,128)(2,1)S(1)}, f32[6,8,256]{2,1,0:T(8,128)S(1)}) custom-call(s32[1024,1]{1,0:T(8,128)S(1)} %copy.57.code_ref, s32[1,1152]{1,0:T(1,128)S(1)} %reshape.159.line_ref, bf16[1024,384]{1,0:T(8,128)(2,1)S(1)} %copy-done.22, bf16[32,384]{1,0:T(8,128)(2,1)S(1)} %fusion.16.edge_ref, bf16[1152,384]{1,0:T(8,128)(2,1)S(1)} %copy-done.8, ...), custom_call_target="tpu_custom_call" | custom-call | flops 8053063 | bytes 78643 | tf_op jit(solution)/shard_map/pallas_call | solution.py:1089
  306.0 12.9 %collective-permute-done.32 = bf16[384,768]{1,0:T(8,128)(2,1)S(1)} collective-permute-done((bf16[384,768]{1,0:T(8,128)(2,1)}, bf16[384,768]{1,0:T(8,128)(2,1)S(1)}, u32[]{:S(2)}, u32[]{:S(2)}) %collective-permute-start.32) | collective-permute-done | bytes 589856 | tf_op jit(solution)/shard_map/inner_z/ppermute | solution.py:597
  341.6 7.1 %shard_map.286 = f32[1024,768]{1,0:T(8,128)S(1)} custom-call(f32[1024,768]{1,0:T(8,128)S(1)} %copy-done.13, bf16[1024,384]{1,0:T(8,128)(2,1)S(1)} %copy-done.29, bf16[1024,384]{1,0:T(8,128)(2,1)S(1)} %copy-done.31, bf16[1024,384]{1,0:T(8,128)(2,1)S(1)} %copy-done.33, bf16[1024,384]{1,0:T(8,128)(2,1)S(1)} %copy-done.35, bf16[1024,384]{1,0:T(8,128)(2,1)S(1)} %copy-done.38, ...), custom_call_target="tpu_custom_call" | custom-call | tf_op jit(solution)/shard_map/pallas_call | solution.py:1131
  357.5 17.6 %collective-permute-done.43 = bf16[192,768]{1,0:T(8,128)(2,1)S(1)} collective-permute-done((bf16[192,768]{1,0:T(8,128)(2,1)S(1)}, bf16[192,768]{1,0:T(8,128)(2,1)S(1)}, u32[]{:S(2)}, u32[]{:S(2)}) %collective-permute-start.43) | collective-permute-done | bytes 294944 | tf_op jit(solution)/shard_map/pair_w/ppermute | solution.py:597
  378.3 6.0 %collective-permute-done.47 = bf16[192,768]{1,0:T(8,128)(2,1)S(1)} collective-permute-done((bf16[192,768]{1,0:T(8,128)(2,1)S(1)}, bf16[192,768]{1,0:T(8,128)(2,1)S(1)}, u32[]{:S(2)}, u32[]{:S(2)}) %collective-permute-start.47) | collective-permute-done | bytes 294944 | tf_op jit(solution)/shard_map/out_z/ppermute | solution.py:597
  384.3 3.8 collective-permute-start.49
  390.5 18.4 %collective-permute-done.49 = bf16[208,768]{1,0:T(8,128)(2,1)S(1)} collective-permute-done((bf16[208,768]{1,0:T(8,128)(2,1)S(1)}, bf16[208,768]{1,0:T(8,128)(2,1)S(1)}, u32[]{:S(2)}, u32[]{:S(2)}) %collective-permute-start.49) | collective-permute-done | bytes 319520 | tf_op jit(solution)/shard_map/val_w/ppermute | solution.py:597
  409.2 3.7 collective-permute-done.52
  (580 shorter events, 178.4 us)
Async XLA Ops:
  1.8 30.7 %collective-permute-start.2 = (bf16[576,768]{1,0:T(8,128)(2,1)S(1)}, bf16[576,768]{1,0:T(8,128)(2,1)}, u32[]{:S(2)}, u32[]{:S(2)}) collective-permute-start(bf16[576,768]{1,0:T(8,128)(2,1)S(1)} %pad_maximum_fusion.one_ref.refs_6_), channel_id=1, source_target_pairs={{0,1},{1,0},{2,3},{3,2},{4,5},{5,4},{6,7},{7,6},{8,9},{9,8},{10,11... | collective-permute-start | bytes 2654216 | tf_op jit(solution)/shard_map/weights/ppermute | solution.py:593
  2.4 27.4 %collective-permute-start.3 = (bf16[576,768]{1,0:T(8,128)(2,1)S(1)}, bf16[576,768]{1,0:T(8,128)(2,1)}, u32[]{:S(2)}, u32[]{:S(2)}) collective-permute-start(bf16[576,768]{1,0:T(8,128)(2,1)S(1)} %pad_maximum_fusion.one_ref.refs_6_), channel_id=1, source_target_pairs={{0,2},{1,3},{2,0},{3,1},{4,6},{5,7},{6,4},{7,5},{8,10},{9,11},{10,... | collective-permute-start | bytes 2654216 | tf_op jit(solution)/shard_map/weights/ppermute | solution.py:593
  11.1 19.2 %collective-permute-start.1 = (bf16[16,768]{1,0:T(8,128)(2,1)S(1)}, bf16[16,768]{1,0:T(8,128)(2,1)S(1)}, u32[]{:S(2)}, u32[]{:S(2)}) collective-permute-start(bf16[16,768]{1,0:T(8,128)(2,1)S(1)} %get-tuple-element.394), channel_id=1, source_target_pairs={{1,0},{2,1},{3,2},{5,4},{6,5},{7,6},{9,8},{10,9},{11,10},{13,12},{... | collective-permute-start | bytes 73736 | tf_op jit(solution)/shard_map/ppermute | solution.py:674
  12.4 17.9 %collective-permute-start = (bf16[16,768]{1,0:T(8,128)(2,1)S(1)}, bf16[16,768]{1,0:T(8,128)(2,1)S(1)}, u32[]{:S(2)}, u32[]{:S(2)}) collective-permute-start(bf16[16,768]{1,0:T(8,128)(2,1)S(1)} %get-tuple-element.393), channel_id=1, source_target_pairs={{0,1},{1,2},{2,3},{4,5},{5,6},{6,7},{8,9},{9,10},{10,11},{12,13},{... | collective-permute-start | bytes 73736 | tf_op jit(solution)/shard_map/ppermute | solution.py:673
  29.8 17.0 %collective-permute-start.4 = (bf16[576,768]{1,0:T(8,128)(2,1)}, bf16[576,768]{1,0:T(8,128)(2,1)S(1)}, u32[]{:S(2)}, u32[]{:S(2)}) collective-permute-start(bf16[576,768]{1,0:T(8,128)(2,1)} %collective-permute-done.3.one_ref.refs_8_), channel_id=1, source_target_pairs={{0,1},{1,0},{2,3},{3,2},{4,5},{5,4},{6,7},{7,6},{8,9},{9,8},{10,11... | collective-permute-start | bytes 2654216 | tf_op jit(solution)/shard_map/weights/ppermute | solution.py:593
  30.6 33.6 %collective-permute-start.10 = (bf16[208,768]{1,0:T(8,128)(2,1)}, bf16[208,768]{1,0:T(8,128)(2,1)}, u32[]{:S(2)}, u32[]{:S(2)}) collective-permute-start(bf16[208,768]{1,0:T(8,128)(2,1)} %fusion.42), channel_id=1, source_target_pairs={{0,1},{1,0},{2,3},{3,2},{4,5},{5,4},{6,7},{7,6},{8,9},{9,8},{10,11... | collective-permute-start | bytes 958472 | tf_op jit(solution)/shard_map/w_output/ppermute | solution.py:593
  30.8 31.0 %collective-permute-start.11 = (bf16[208,768]{1,0:T(8,128)(2,1)}, bf16[208,768]{1,0:T(8,128)(2,1)}, u32[]{:S(2)}, u32[]{:S(2)}) collective-permute-start(bf16[208,768]{1,0:T(8,128)(2,1)} %fusion.42), channel_id=1, source_target_pairs={{0,2},{1,3},{2,0},{3,1},{4,6},{5,7},{6,4},{7,5},{8,10},{9,11},{10,... | collective-permute-start | bytes 958472 | tf_op jit(solution)/shard_map/w_output/ppermute | solution.py:593
  156.3 25.4 %collective-permute-start.16 = (bf16[2,768,768]{2,1,0:T(8,128)(2,1)}, bf16[2,768,768]{2,1,0:T(8,128)(2,1)}, u32[]{:S(2)}, u32[]{:S(2)}) collective-permute-start(bf16[2,768,768]{2,1,0:T(8,128)(2,1)} %get-tuple-element.227), channel_id=1, source_target_pairs={{0,1},{1,0},{2,3},{3,2},{4,5},{5,4},{6,7},{7,6},{8,9},{9,8},{10,11... | collective-permute-start | bytes 7077896 | tf_op jit(solution)/shard_map/inner_core/ppermute | solution.py:593
  156.3 25.4 %collective-permute-start.17 = (bf16[2,768,768]{2,1,0:T(8,128)(2,1)}, bf16[2,768,768]{2,1,0:T(8,128)(2,1)}, u32[]{:S(2)}, u32[]{:S(2)}) collective-permute-start(bf16[2,768,768]{2,1,0:T(8,128)(2,1)} %get-tuple-element.228), channel_id=1, source_target_pairs={{0,1},{1,0},{2,3},{3,2},{4,5},{5,4},{6,7},{7,6},{8,9},{9,8},{10,11... | collective-permute-start | bytes 7077896 | tf_op jit(solution)/shard_map/outer_core/ppermute | solution.py:593
  201.9 35.6 %collective-permute-start.23 = (bf16[2,384,768]{2,1,0:T(8,128)(2,1)S(1)}, bf16[2,384,768]{2,1,0:T(8,128)(2,1)S(1)}, u32[]{:S(2)}, u32[]{:S(2)}) collective-permute-start(bf16[2,384,768]{2,1,0:T(8,128)(2,1)S(1)} %add_convert_fusion.4), channel_id=1, source_target_pairs={{0,4},{4,0},{8,12},{12,8},{16,20},{20,16},{24,28},{28,24},{1,5},{5... | collective-permute-start | bytes 3538952 | tf_op jit(solution)/shard_map/outer_y/ppermute | solution.py:597
  203.5 34.0 %collective-permute-start.24 = (bf16[768,768]{1,0:T(8,128)(2,1)S(1)}, bf16[768,768]{1,0:T(8,128)(2,1)S(1)}, u32[]{:S(2)}, u32[]{:S(2)}) collective-permute-start(bf16[768,768]{1,0:T(8,128)(2,1)S(1)} %fusion.13), channel_id=1, source_target_pairs={{0,2},{1,3},{2,0},{3,1},{4,6},{5,7},{6,4},{7,5},{8,10},{9,11},{10,... | collective-permute-start | bytes 3538952 | tf_op jit(solution)/shard_map/inner_x/ppermute | solution.py:593
  216.8 19.4 %collective-permute-start.22 = (bf16[2,192,768]{2,1,0:T(8,128)(2,1)S(1)}, bf16[2,192,768]{2,1,0:T(8,128)(2,1)S(1)}, u32[]{:S(2)}, u32[]{:S(2)}) collective-permute-start(bf16[2,192,768]{2,1,0:T(8,128)(2,1)S(1)} %get-tuple-element.253), channel_id=1, source_target_pairs={{0,1},{1,0},{2,3},{3,2},{4,5},{5,4},{6,7},{7,6},{8,9},{9,8},{10,11... | collective-permute-start | bytes 1769480 | tf_op jit(solution)/shard_map/out_core/ppermute | solution.py:593
  217.9 18.3 %collective-permute-start.21 = (f32[3,64,256]{2,1,0:T(8,128)S(1)}, f32[3,64,256]{2,1,0:T(8,128)S(1)}, u32[]{:S(2)}, u32[]{:S(2)}) collective-permute-start(f32[3,64,256]{2,1,0:T(8,128)S(1)} %slice.261), channel_id=1, source_target_pairs={{0,2},{1,3},{2,0},{3,1},{4,6},{5,7},{6,4},{7,5},{8,10},{9,11},{10,... | collective-permute-start | bytes 589832 | tf_op jit(solution)/shard_map/mixed_grad_x/ppermute | solution.py:593
  237.4 18.2 %collective-permute-start.25 = (bf16[3,80,256]{2,1,0:T(8,128)(2,1)S(1)}, bf16[3,80,256]{2,1,0:T(8,128)(2,1)S(1)}, u32[]{:S(2)}, u32[]{:S(2)}) collective-permute-start(bf16[3,80,256]{2,1,0:T(8,128)(2,1)S(1)} %get-tuple-element.269), channel_id=1, source_target_pairs={{0,1},{1,0},{2,3},{3,2},{4,5},{5,4},{6,7},{7,6},{8,9},{9,8},{10,11... | collective-permute-start | bytes 368648 | tf_op jit(solution)/shard_map/carried_grad/ppermute | solution.py:593
  237.7 18.1 %collective-permute-start.27 = (bf16[3,80,256]{2,1,0:T(8,128)(2,1)S(1)}, bf16[3,80,256]{2,1,0:T(8,128)(2,1)S(1)}, u32[]{:S(2)}, u32[]{:S(2)}) collective-permute-start(bf16[3,80,256]{2,1,0:T(8,128)(2,1)S(1)} %get-tuple-element.269), channel_id=1, source_target_pairs={{0,3},{1,2},{2,1},{3,0},{4,7},{5,6},{6,5},{7,4},{8,11},{9,10},{10,... | collective-permute-start | bytes 368648 | tf_op jit(solution)/shard_map/carried_grad/ppermute | solution.py:593
  238.6 17.1 %collective-permute-start.26 = (bf16[3,80,256]{2,1,0:T(8,128)(2,1)S(1)}, bf16[3,80,256]{2,1,0:T(8,128)(2,1)S(1)}, u32[]{:S(2)}, u32[]{:S(2)}) collective-permute-start(bf16[3,80,256]{2,1,0:T(8,128)(2,1)S(1)} %get-tuple-element.269), channel_id=1, source_target_pairs={{0,2},{1,3},{2,0},{3,1},{4,6},{5,7},{6,4},{7,5},{8,10},{9,11},{10,... | collective-permute-start | bytes 368648 | tf_op jit(solution)/shard_map/carried_grad/ppermute | solution.py:593
  243.5 17.3 %collective-permute-start.28 = (bf16[384,768]{1,0:T(8,128)(2,1)S(1)}, bf16[384,768]{1,0:T(8,128)(2,1)S(1)}, u32[]{:S(2)}, u32[]{:S(2)}) collective-permute-start(bf16[384,768]{1,0:T(8,128)(2,1)S(1)} %constant_dynamic-slice_fusion.3), channel_id=1, source_target_pairs={{0,4},{4,0},{8,12},{12,8},{16,20},{20,16},{24,28},{28,24},{1,5},{5... | collective-permute-start | bytes 1769480 | tf_op jit(solution)/shard_map/inner_y/ppermute | solution.py:597
  244.1 16.7 %collective-permute-start.29 = (bf16[2,192,768]{2,1,0:T(8,128)(2,1)S(1)}, bf16[2,192,768]{2,1,0:T(8,128)(2,1)S(1)}, u32[]{:S(2)}, u32[]{:S(2)}) collective-permute-start(bf16[2,192,768]{2,1,0:T(8,128)(2,1)S(1)} %constant_dynamic-slice_fusion.2), channel_id=1, source_target_pairs={{0,8},{4,12},{8,0},{12,4},{16,24},{20,28},{24,16},{28,20},{1,9},{5... | collective-permute-start | bytes 1769480 | tf_op jit(solution)/shard_map/outer_z/ppermute | solution.py:597
  290.8 28.2 %collective-permute-start.32 = (bf16[384,768]{1,0:T(8,128)(2,1)}, bf16[384,768]{1,0:T(8,128)(2,1)S(1)}, u32[]{:S(2)}, u32[]{:S(2)}) collective-permute-start(bf16[384,768]{1,0:T(8,128)(2,1)} %add_convert_fusion.10), channel_id=1, source_target_pairs={{0,8},{4,12},{8,0},{12,4},{16,24},{20,28},{24,16},{28,20},{1,9},{5... | collective-permute-start | bytes 1769480 | tf_op jit(solution)/shard_map/inner_z/ppermute | solution.py:597
  291.3 27.7 %collective-permute-start.33 = (bf16[2,192,768]{2,1,0:T(8,128)(2,1)S(1)}, bf16[2,192,768]{2,1,0:T(8,128)(2,1)S(1)}, u32[]{:S(2)}, u32[]{:S(2)}) collective-permute-start(bf16[2,192,768]{2,1,0:T(8,128)(2,1)S(1)} %copy-done.101), channel_id=1, source_target_pairs={{0,16},{4,20},{8,24},{12,28},{16,0},{20,4},{24,8},{28,12},{1,17},{... | collective-permute-start | bytes 1769480 | tf_op jit(solution)/shard_map/outer_w/ppermute | solution.py:597
  305.1 22.1 %collective-permute-start.36 = (bf16[384,768]{1,0:T(8,128)(2,1)}, bf16[384,768]{1,0:T(8,128)(2,1)}, u32[]{:S(2)}, u32[]{:S(2)}) collective-permute-start(bf16[384,768]{1,0:T(8,128)(2,1)} %fusion.20), channel_id=1, source_target_pairs={{0,2},{1,3},{2,0},{3,1},{4,6},{5,7},{6,4},{7,5},{8,10},{9,11},{10,... | collective-permute-start | bytes 1769480 | tf_op jit(solution)/shard_map/pair_x/ppermute | solution.py:593
  331.3 17.5 %collective-permute-start.39 = (bf16[192,768]{1,0:T(8,128)(2,1)S(1)}, bf16[192,768]{1,0:T(8,128)(2,1)S(1)}, u32[]{:S(2)}, u32[]{:S(2)}) collective-permute-start(bf16[192,768]{1,0:T(8,128)(2,1)S(1)} %slice_bitcast_fusion), channel_id=1, source_target_pairs={{0,2},{1,3},{2,0},{3,1},{4,6},{5,7},{6,4},{7,5},{8,10},{9,11},{10,... | collective-permute-start | bytes 884744 | tf_op jit(solution)/shard_map/outer_x/ppermute | solution.py:593
  332.3 16.5 %collective-permute-start.42 = (bf16[192,768]{1,0:T(8,128)(2,1)S(1)}, bf16[192,768]{1,0:T(8,128)(2,1)S(1)}, u32[]{:S(2)}, u32[]{:S(2)}) collective-permute-start(bf16[192,768]{1,0:T(8,128)(2,1)S(1)} %fusion.36), channel_id=1, source_target_pairs={{0,4},{4,0},{8,12},{12,8},{16,20},{20,16},{24,28},{28,24},{1,5},{5... | collective-permute-start | bytes 884744 | tf_op jit(solution)/shard_map/out_y/ppermute | solution.py:597
  333.9 44.4 %collective-permute-start.46 = (bf16[384,768]{1,0:T(8,128)(2,1)}, bf16[384,768]{1,0:T(8,128)(2,1)S(1)}, u32[]{:S(2)}, u32[]{:S(2)}) collective-permute-start(bf16[384,768]{1,0:T(8,128)(2,1)} %add_convert_fusion.7), channel_id=1, source_target_pairs={{0,16},{4,20},{8,24},{12,28},{16,0},{20,4},{24,8},{28,12},{1,17},{... | collective-permute-start | bytes 1769480 | tf_op jit(solution)/shard_map/inner_w/ppermute | solution.py:597
  348.9 26.2 %collective-permute-start.43 = (bf16[192,768]{1,0:T(8,128)(2,1)S(1)}, bf16[192,768]{1,0:T(8,128)(2,1)S(1)}, u32[]{:S(2)}, u32[]{:S(2)}) collective-permute-start(bf16[192,768]{1,0:T(8,128)(2,1)S(1)} %add_convert_fusion.20), channel_id=1, source_target_pairs={{0,16},{4,20},{8,24},{12,28},{16,0},{20,4},{24,8},{28,12},{1,17},{... | collective-permute-start | bytes 884744 | tf_op jit(solution)/shard_map/pair_w/ppermute | solution.py:597
  351.6 26.3 %collective-permute-start.44 = (bf16[208,768]{1,0:T(8,128)(2,1)S(1)}, bf16[208,768]{1,0:T(8,128)(2,1)S(1)}, u32[]{:S(2)}, u32[]{:S(2)}) collective-permute-start(bf16[208,768]{1,0:T(8,128)(2,1)S(1)} %fusion.18), channel_id=1, source_target_pairs={{0,4},{4,0},{8,12},{12,8},{16,20},{20,16},{24,28},{28,24},{1,5},{5... | collective-permute-start | bytes 958472 | tf_op jit(solution)/shard_map/val_y/ppermute | solution.py:597
  353.2 24.7 %collective-permute-start.45 = (bf16[192,768]{1,0:T(8,128)(2,1)S(1)}, bf16[192,768]{1,0:T(8,128)(2,1)S(1)}, u32[]{:S(2)}, u32[]{:S(2)}) collective-permute-start(bf16[192,768]{1,0:T(8,128)(2,1)S(1)} %fusion.35), channel_id=1, source_target_pairs={{0,8},{4,12},{8,0},{12,4},{16,24},{20,28},{24,16},{28,20},{1,9},{5... | collective-permute-start | bytes 884744 | tf_op jit(solution)/shard_map/outer_z2/ppermute | solution.py:597
  356.0 28.3 %collective-permute-start.47 = (bf16[192,768]{1,0:T(8,128)(2,1)S(1)}, bf16[192,768]{1,0:T(8,128)(2,1)S(1)}, u32[]{:S(2)}, u32[]{:S(2)}) collective-permute-start(bf16[192,768]{1,0:T(8,128)(2,1)S(1)} %add_convert_fusion.19), channel_id=1, source_target_pairs={{0,8},{4,12},{8,0},{12,4},{16,24},{20,28},{24,16},{28,20},{1,9},{5... | collective-permute-start | bytes 884744 | tf_op jit(solution)/shard_map/out_z/ppermute | solution.py:597
  378.0 34.8 %collective-permute-start.51 = (bf16[384,768]{1,0:T(8,128)(2,1)S(1)}, bf16[384,768]{1,0:T(8,128)(2,1)S(1)}, u32[]{:S(2)}, u32[]{:S(2)}) collective-permute-start(bf16[384,768]{1,0:T(8,128)(2,1)S(1)} %pad_maximum_fusion.5), channel_id=1, source_target_pairs={{0,4},{4,0},{8,12},{12,8},{16,20},{20,16},{24,28},{28,24},{1,5},{5... | collective-permute-start | bytes 1769480 | tf_op jit(solution)/shard_map/outer_y2/ppermute | solution.py:597
  384.3 24.6 %collective-permute-start.49 = (bf16[208,768]{1,0:T(8,128)(2,1)S(1)}, bf16[208,768]{1,0:T(8,128)(2,1)S(1)}, u32[]{:S(2)}, u32[]{:S(2)}) collective-permute-start(bf16[208,768]{1,0:T(8,128)(2,1)S(1)} %add_convert_fusion.13), channel_id=1, source_target_pairs={{0,16},{4,20},{8,24},{12,28},{16,0},{20,4},{24,8},{28,12},{1,17},{... | collective-permute-start | bytes 958472 | tf_op jit(solution)/shard_map/val_w/ppermute | solution.py:597
  388.2 24.6 %collective-permute-start.52 = (bf16[192,768]{1,0:T(8,128)(2,1)S(1)}, bf16[192,768]{1,0:T(8,128)(2,1)S(1)}, u32[]{:S(2)}, u32[]{:S(2)}) collective-permute-start(bf16[192,768]{1,0:T(8,128)(2,1)S(1)} %add_convert_fusion.16), channel_id=1, source_target_pairs={{0,16},{4,20},{8,24},{12,28},{16,0},{20,4},{24,8},{28,12},{1,17},{... | collective-permute-start | bytes 884744 | tf_op jit(solution)/shard_map/out_w/ppermute | solution.py:597
  388.5 26.2 %collective-permute-start.54 = (bf16[384,768]{1,0:T(8,128)(2,1)S(1)}, bf16[384,768]{1,0:T(8,128)(2,1)S(1)}, u32[]{:S(2)}, u32[]{:S(2)}) collective-permute-start(bf16[384,768]{1,0:T(8,128)(2,1)S(1)} %add_convert_fusion.5), channel_id=1, source_target_pairs={{0,4},{4,0},{8,12},{12,8},{16,20},{20,16},{24,28},{28,24},{1,5},{5... | collective-permute-start | bytes 1769480 | tf_op jit(solution)/shard_map/inner_y2/ppermute | solution.py:597
  (166 other events, 1312.6 us)

commit v4 on v3

--- a/solution.py
+++ b/solution.py
@@ -19,6 +19,7 @@
 CHUNK = 256
 QK_SCALE = HEAD_DIM ** (-0.25)
 FAR_TYPE = jnp.bfloat16
+TAP_ROWS = 16
 
 NEG_FILL = -1e30
 NORM_EPS = 1e-05
@@ -453,7 +454,7 @@
 
 
 def project_kernel(x_ref, one_ref, two_ref, q_ref, k_ref, v_ref):
-    local = one_ref.shape[0] // 3
+    local = (one_ref.shape[0] - TAP_ROWS) // 3
     rows = q_ref.shape[0]
     weights = []
     for kind in range(3):
@@ -473,7 +474,7 @@
 
 
 def landmark_kernel(land_ref, one_ref, two_ref, lq_ref, lk_ref):
-    local = one_ref.shape[0] // 3
+    local = (one_ref.shape[0] - TAP_ROWS) // 3
     high, low = split_low(land_ref[...])
     for kind, out in ((0, lq_ref), (1, lk_ref)):
         for index, part in enumerate((one_ref, two_ref)):
@@ -505,7 +506,7 @@
 def input_grad_kernel(base_ref, *refs):
     out_ref = refs[-1]
     lows, pieces = refs[:6], refs[6:10]
-    local = pieces[0].shape[0] // 3
+    local = (pieces[0].shape[0] - TAP_ROWS) // 3
     weights = []
     for kind in range(3):
         cut = slice(kind * local, (kind + 1) * local)
@@ -644,12 +645,11 @@
     segment = lax.dynamic_slice_in_dim(segment_row, me * rows, rows, 0)
     member = (segment[:, None] == columns[None, :]).astype(BF)
 
-    packed = jnp.concatenate([w_query.T, w_key.T, w_value.T], axis=0)
+    tap_pad = jnp.pad(conv_weight, ((0, TAP_ROWS - own), (0, width - KW)))
+    packed = jnp.concatenate([w_query.T, w_key.T, w_value.T, tap_pad], axis=0)
+    packed, member_in = gate(packed, member)
     got = spread(packed, "weights")
-    tap_pad = jnp.pad(conv_weight, ((0, 16 - own), (0, width - KW)))
-    out_packed, far_weights = gate(
-        jnp.concatenate([w_output, tap_pad], axis=0), got[2]
-    )
+    out_packed, far_weights = gate(w_output, got[2])
     got = got[:2] + (far_weights,) + got[3:]
     out_far = swap(out_packed, 2, "w_output")
     out_parts = (
@@ -657,11 +657,13 @@
     )
 
     wo = [
-        jnp.concatenate([out_parts[2 * half + j][:local] for j in (0, 1)], axis=0)
+        jnp.concatenate([out_parts[2 * half + j] for j in (0, 1)], axis=0)
         for half in (0, 1)
     ]
     tap_rows = [
-        jnp.concatenate([out_parts[2 * half + j][local : local + own, :KW] for j in (0, 1)], axis=0)
+        jnp.concatenate(
+            [got[2 * half + j][3 * local : 3 * local + own, :KW] for j in (0, 1)], axis=0
+        )
         for half in (0, 1)
     ]
 
@@ -677,7 +679,7 @@
 
     tokens_ext = with_edges(tokens_in)
 
-    land_part = tn(member, tokens_in) / counts[:, None]
+    land_part = tn(member_in, tokens_in) / counts[:, None]
     land_sum = head_sum(land_part, "land", FAR_TYPE)
     land_tokens = land_sum.astype(BF)
 
@@ -712,7 +714,10 @@
     )
     packs, third_exp = [], []
     for half in (0, 1):
-        pack, e_out = third_call(code, keys[half], values[half], land_q[half])
+        third_land = land_q[half]
+        if half == 1:
+            third_land, wo, tap_rows = gate(third_land, wo, tap_rows)
+        pack, e_out = third_call(code, keys[half], values[half], third_land)
         packs.append(pack)
         third_exp.append(e_out)
 
@@ -766,18 +771,20 @@
     wait_in, far_send = gate((queries, values), joined[own:])
     pack_far = swap(far_send, 2, "pack_x")
     queries, values = wait_in
-    conv_outs = [
-        conv_call(code, line, values[half], tap_lines(tap_rows[half]))[0] for half in (0, 1)
-    ]
     first_low = [first_call(code, queries[half], land_k[half])[0] for half in (0, 1)]
-    pack_far, first_low, conv_outs = gate(pack_far, first_low, conv_outs)
+    pack_far, first_low = gate(pack_far, first_low)
     mixed_own, carried = plain(
         mix_kernel,
         [shape_of((own, HEAD_DIM + 16, SEGS), BF), docs_shape],
         flops=6 * own * LAND * SEGS * SEGS,
         moved=16 * own * tall * SEGS,
     )(joined[:own], pack_far, inverse)
+    values_in, mixed_own = gate(values, mixed_own)
     mixed = gather_heads(mixed_own, "mixed")
+    conv_outs = [
+        conv_call(code, line, values_in[half], tap_lines(tap_rows[half]))[0] for half in (0, 1)
+    ]
+    mixed, conv_outs = gate(mixed, conv_outs)
 
     def row_of(parts):
         return [
@@ -1131,7 +1138,7 @@
     input_part = call(
         input_grad_kernel,
         (rows // row_block,),
-        [full_spec] + [rows_spec] * 6 + [whole((3 * local, width))] * 4,
+        [full_spec] + [rows_spec] * 6 + [whole((3 * local + TAP_ROWS, width))] * 4,
         [(full_spec, shape_of((rows, width), F32))],
     )(first_in_grad, *dq_parts, *dk_parts, *dv_parts, *got)[0]
 

time: 428 us -> 424 us (level)
  local copies, waits for them, and re-layouts: 47.9 us -> 42.7 us
    slice x8 -> x4, local copies, waits for them, and re-layouts: 7.03 us -> 1.35 us  [shards(): got[2 * half + j][3 * local:3 * local + own, :KW]]
    ppermute x32, waiting for transfers between devices: 29.6 us -> 34.2 us  [swap(): return lax.ppermute(value, 'head', [(i, i ^ bit) for i in range(groups)])]
    unnamed x288 -> x282, local copies, waits for them, and re-layouts: 32.2 us -> 32.4 us
  transfers between devices with their start and end apart: 55 -> 55, of which waited for: 11 -> 11; matrix products, arithmetic and copies ran while one was open for 13% -> 10% of each run, Pallas kernels for 26% -> 23%
where the time goes in v4:
time: 424 us; the launch traced here: 418 us
  Pallas kernels  157 us (37%)
  waiting for transfers between devices  97.7 us (23%)
  other arithmetic  54.7 us (13%)
  starting transfers between devices  52.4 us (12%)
  local copies, waits for them, and re-layouts  42.7 us (10%)
  matrix products  9.65 us (2%)
    ppermute x19, waiting for transfers between devices, swap_batch(): lax.ppermute(value, 'batch', [(i, i ^ bit) for i in range(batch_size)])  63.5 us
    pallas_call x2, Pallas kernels, feed_back(): pl.pallas_call(feed_back_kernel, grid_spec=grid_spec, out_shape=[shape_of...  35.1 us
    ppermute x32, waiting for transfers between devices, swap(): return lax.ppermute(value, 'head', [(i, i ^ bit) for i in range(groups)])  34.2 us
    unnamed x282, local copies, waits for them, and re-layouts  32.4 us
    ppermute x32, starting transfers between devices, swap(): return lax.ppermute(value, 'head', [(i, i ^ bit) for i in range(groups)])  22.6 us
    ppermute x19, starting transfers between devices, swap_batch(): lax.ppermute(value, 'batch', [(i, i ^ bit) for i in range(batch_size)])  21.1 us
    pallas_call x1, Pallas kernels, shards(): call(feed_kernel, (ff // block,), [whole((rows, width)), column(width, bl...  16.5 us
    pallas_call x2, Pallas kernels, shards(): conv_back_call(code, line, heads_grad[half], edge_parts[half], values[hal...  11.8 us
  transfers between devices with their start and end apart: 55, of which 11 were waited for; matrix products, arithmetic and copies ran while one was open for 10% of the time, Pallas kernels for 23%

profile of v4, /device:TPU:0, one launch (start us, length us, event | category | flops | bytes accessed | tf_op | source)
XLA Modules:
  0.0 417.5 jit_solution(17636261237175988020)
XLA Ops:
  11.0 3.0 collective-permute-start
  17.1 18.0 %collective-permute-done.6 = bf16[128,768]{1,0:T(8,128)(2,1)S(1)} collective-permute-done((bf16[128,768]{1,0:T(8,128)(2,1)S(1)}, bf16[128,768]{1,0:T(8,128)(2,1)S(1)}, u32[]{:S(2)}, u32[]{:S(2)}) %collective-permute-start.6) | collective-permute-done | bytes 196640 | tf_op jit(solution)/shard_map/land/ppermute | solution.py:594
  39.2 4.0 shard_map.255
  46.8 4.3 %shard_map.258 = (f32[6,72,256]{2,1,0:T(8,128)S(1)}, bf16[1024,1536]{1,0:T(8,128)(2,1)S(1)}) custom-call(s32[1024,1]{1,0:T(8,128)S(1)} %copy.59.code_ref, bf16[1024,384]{1,0:T(8,128)(2,1)S(1)} %get-tuple-element.209.k_ref, bf16[1152,384]{1,0:T(8,128)(2,1)S(1)} %get-tuple-element.235.v_ref, bf16[6,64,256]{2,1,0:T(8,128)(2,1)S(1)} %get-tuple-element.211.lq_ref), custom_call_target="tpu_custom_call" | custom-call | flops 8053063 | bytes 94371 | tf_op jit(solution)/shard_map/pallas_call | solution.py:720
  57.4 4.0 shard_map.256
  62.3 4.0 shard_map.260
  69.2 5.4 %shard_map.261 = (f32[3,64,256]{2,1,0:T(8,128)S(1)}, f32[3,64,256]{2,1,0:T(8,128)S(1)}, f32[6,3,4,64,256]{4,3,2,1,0:T(8,128)S(1)}) custom-call(bf16[3,64,256]{2,1,0:T(8,128)(2,1)S(1)} %slice.235.lq_ref, bf16[3,64,256]{2,1,0:T(8,128)(2,1)S(1)} %slice.236.lk_ref), custom_call_target="tpu_custom_call" | custom-call | flops 36238784 | bytes 94371 | tf_op jit(solution)/shard_map/pallas_call | solution.py:730
  78.9 4.1 shard_map.263.p_ref
  83.1 4.7 %shard_map.264.p_ref = bf16[1024,1536]{1,0:T(8,128)(2,1)S(1)} custom-call(s32[1024,1]{1,0:T(8,128)S(1)} %copy.59.code_ref, bf16[1024,384]{1,0:T(8,128)(2,1)S(1)} %copy-done.46, bf16[6,64,256]{2,1,0:T(8,128)(2,1)S(1)} %copy-done.74), custom_call_target="tpu_custom_call" | custom-call | flops 4026531 | bytes 78643 | tf_op jit(solution)/shard_map/pallas_call | solution.py:774
  92.5 3.0 shard_map.266.conv_ref
  95.5 3.0 shard_map.267.conv_ref
  106.0 16.5 %shard_map.270 = (bf16[1024,3072]{1,0:T(8,128)(2,1)S(1)}, bf16[1024,3072]{1,0:T(8,128)(2,1)}, f32[1024,768]{1,0:T(8,128)S(1)}) custom-call(bf16[1024,768]{1,0:T(8,128)(2,1)S(1)} %fusion.8.x_ref, bf16[768,3072]{1,0:T(8,128)(2,1)S(1)} %bitcast.96, bf16[3072,768]{1,0:T(8,128)(2,1)S(1)} %bitcast.98), custom_call_target="tpu_custom_call" | custom-call | flops 193273536 | bytes 534773 | tf_op jit(solution)/shard_map/pallas_call | solution.py:805
  130.9 17.8 %shard_map.271 = (bf16[2,768,768]{2,1,0:T(8,128)(2,1)}, bf16[2,768,768]{2,1,0:T(8,128)(2,1)}, f32[1024,768]{1,0:T(8,128)S(1)}) custom-call(s32[4]{0:T(128)S(1)} %get-tuple-element.462.table, bf16[1024,768]{1,0:T(8,128)(2,1)S(1)} %get-tuple-element.408.og_ref, bf16[1024,768]{1,0:T(8,128)(2,1)S(1)} %fusion.8.x_ref, bf16[768,3072]{1,0:T(8,128)(2,1)} %wi_ref.5, ...), custom_call_target="tpu_custom_call" | custom-call | flops 9663676416 | bytes 25165824 | tf_op jit(solution)/shard_map/pallas_call | solution.py:851
  158.5 17.3 %shard_map.272 = (bf16[2,768,768]{2,1,0:T(8,128)(2,1)S(1)}, bf16[2,768,768]{2,1,0:T(8,128)(2,1)S(1)}, f32[1024,768]{1,0:T(8,128)S(1)}) custom-call(s32[4]{0:T(128)S(1)} %get-tuple-element.461.table, bf16[1024,768]{1,0:T(8,128)(2,1)S(1)} %copy-done.61, bf16[1024,768]{1,0:T(8,128)(2,1)S(1)} %copy-done.26, bf16[768,3072]{1,0:T(8,128)(2,1)} %wi_ref.5, ...), custom_call_target="tpu_custom_call" | custom-call | flops 9663676416 | bytes 25165824 | tf_op jit(solution)/shard_map/pallas_call | solution.py:851
  192.6 3.0 collective-permute-start.19
  199.0 4.8 %shard_map.275 = (bf16[1024,384]{1,0:T(8,128)(2,1)S(1)}, f32[6,64,256]{2,1,0:T(8,128)S(1)}) custom-call(bf16[1024,384]{1,0:T(8,128)(2,1)S(1)} %select_convert_fusion.1.hg_ref, bf16[1024,1536]{1,0:T(8,128)(2,1)S(1)} %copy-done.3, bf16[1024,384]{1,0:T(8,128)(2,1)S(1)} %copy-done.44, bf16[6,80,256]{2,1,0:T(8,128)(2,1)S(1)} %pad_maximum_fusion.12.mix_ref, ...), custom_call_target="tpu_custom_call" | custom-call | flops 12079595 | bytes 110100 | tf_op jit(solution)/shard_map/pallas_call | solution.py:997
  204.0 5.2 %shard_map.276 = (bf16[1024,384]{1,0:T(8,128)(2,1)S(1)}, f32[6,64,256]{2,1,0:T(8,128)S(1)}) custom-call(bf16[1024,384]{1,0:T(8,128)(2,1)S(1)} %select_convert_fusion.hg_ref, bf16[1024,1536]{1,0:T(8,128)(2,1)S(1)} %copy-done.1, bf16[1024,384]{1,0:T(8,128)(2,1)S(1)} %copy-done.47, bf16[6,80,256]{2,1,0:T(8,128)(2,1)S(1)} %pad_maximum_fusion.13.mix_ref, ...), custom_call_target="tpu_custom_call" | custom-call | flops 12079595 | bytes 110100 | tf_op jit(solution)/shard_map/pallas_call | solution.py:997
  214.1 16.1 %collective-permute-done.21.b_ref = f32[3,64,256]{2,1,0:T(8,128)S(1)} collective-permute-done((f32[3,64,256]{2,1,0:T(8,128)S(1)}, f32[3,64,256]{2,1,0:T(8,128)S(1)}, u32[]{:S(2)}, u32[]{:S(2)}) %collective-permute-start.21) | collective-permute-done | bytes 196640 | tf_op jit(solution)/shard_map/mixed_grad_x/ppermute | solution.py:594
  239.5 10.1 %shard_map.279 = (f32[3,64,256]{2,1,0:T(8,128)S(1)}, f32[3,64,256]{2,1,0:T(8,128)S(1)}) custom-call(f32[3,64,256]{2,1,0:T(8,128)S(1)} %get-tuple-element.288.mg_ref, f32[3,64,256]{2,1,0:T(8,128)S(1)} %copy-done.79, f32[3,64,256]{2,1,0:T(8,128)S(1)} %copy-done.88, f32[6,3,4,64,256]{4,3,2,1,0:T(8,128)S(1)} %bitcast.94, bf16[3,64,256]{2,1,0:T(8,128)(2,1)S(1)} %copy-done.70, ...), custom_call_target="tpu_custom_call" | custom-call | tf_op jit(solution)/shard_map/pallas_call | solution.py:1027
  249.8 4.8 %shard_map.280 = (bf16[1024,384]{1,0:T(8,128)(2,1)S(1)}, f32[1024,384]{1,0:T(8,128)S(1)}, f32[6,64,256]{2,1,0:T(8,128)S(1)}) custom-call(bf16[1024,384]{1,0:T(8,128)(2,1)S(1)} %copy-done.53, bf16[1152,384]{1,0:T(8,128)(2,1)S(1)} %copy-done.7, bf16[1024,1536]{1,0:T(8,128)(2,1)S(1)} %copy-done.51, f32[6,1,256]{2,1,0:T(1,128)S(1)} %subtract_exponential_fusion.1.f_ref, ...), custom_call_target="tpu_custom_call" | custom-call | flops 16106127 | bytes 157286 | tf_op jit(solution)/shard_map/pallas_call | solution.py:1049
  258.2 4.6 %shard_map.281 = (bf16[1024,384]{1,0:T(8,128)(2,1)S(1)}, f32[1024,384]{1,0:T(8,128)S(1)}, f32[6,64,256]{2,1,0:T(8,128)S(1)}) custom-call(bf16[1024,384]{1,0:T(8,128)(2,1)S(1)} %copy-done.55, bf16[1152,384]{1,0:T(8,128)(2,1)S(1)} %copy-done.11, bf16[1024,1536]{1,0:T(8,128)(2,1)S(1)} %copy-done.49, f32[6,1,256]{2,1,0:T(1,128)S(1)} %subtract_exponential_fusion.f_ref, ...), custom_call_target="tpu_custom_call" | custom-call | flops 16106127 | bytes 157286 | tf_op jit(solution)/shard_map/pallas_call | solution.py:1049
  265.8 4.3 %shard_map.282 = (bf16[2,384,768]{2,1,0:T(8,128)(2,1)S(1)}, bf16[2,384,768]{2,1,0:T(8,128)(2,1)}) custom-call(bf16[1024,768]{1,0:T(8,128)(2,1)S(1)} %copy-done.4, bf16[1024,384]{1,0:T(8,128)(2,1)S(1)} %get-tuple-element.314.refs_0_.refs_2_, bf16[1024,384]{1,0:T(8,128)(2,1)S(1)} %get-tuple-element.315.refs_1_.refs_3_, ...), custom_call_target="tpu_custom_call" | custom-call | tf_op jit(solution)/shard_map/pallas_call | solution.py:988
  278.7 5.8 %shard_map.283 = (bf16[1024,384]{1,0:T(8,128)(2,1)S(1)}, f32[6,8,256]{2,1,0:T(8,128)S(1)}) custom-call(s32[1024,1]{1,0:T(8,128)S(1)} %copy.59.code_ref, s32[1,1152]{1,0:T(1,128)S(1)} %reshape.159.line_ref, bf16[1024,384]{1,0:T(8,128)(2,1)S(1)} %copy-done.22, bf16[32,384]{1,0:T(8,128)(2,1)S(1)} %fusion.16.edge_ref, bf16[1152,384]{1,0:T(8,128)(2,1)S(1)} %copy-done.8, ...), custom_call_target="tpu_custom_call" | custom-call | flops 8053063 | bytes 78643 | tf_op jit(solution)/shard_map/pallas_call | solution.py:1096
  285.7 2.8 collective-permute-start.33
  291.6 6.0 %shard_map.284 = (bf16[1024,384]{1,0:T(8,128)(2,1)S(1)}, f32[6,8,256]{2,1,0:T(8,128)S(1)}) custom-call(s32[1024,1]{1,0:T(8,128)S(1)} %copy.59.code_ref, s32[1,1152]{1,0:T(1,128)S(1)} %reshape.159.line_ref, bf16[1024,384]{1,0:T(8,128)(2,1)S(1)} %copy-done.20, bf16[32,384]{1,0:T(8,128)(2,1)S(1)} %fusion.17.edge_ref, bf16[1152,384]{1,0:T(8,128)(2,1)S(1)} %copy-done.12, ...), custom_call_target="tpu_custom_call" | custom-call | flops 8053063 | bytes 78643 | tf_op jit(solution)/shard_map/pallas_call | solution.py:1096
  300.6 12.7 %collective-permute-done.32 = bf16[384,768]{1,0:T(8,128)(2,1)S(1)} collective-permute-done((bf16[384,768]{1,0:T(8,128)(2,1)S(1)}, bf16[384,768]{1,0:T(8,128)(2,1)S(1)}, u32[]{:S(2)}, u32[]{:S(2)}) %collective-permute-start.32) | collective-permute-done | bytes 589856 | tf_op jit(solution)/shard_map/inner_z/ppermute | solution.py:598
  337.7 7.1 %shard_map.286 = f32[1024,768]{1,0:T(8,128)S(1)} custom-call(f32[1024,768]{1,0:T(8,128)S(1)} %copy-done.13, bf16[1024,384]{1,0:T(8,128)(2,1)S(1)} %copy-done.29, bf16[1024,384]{1,0:T(8,128)(2,1)S(1)} %copy-done.31, bf16[1024,384]{1,0:T(8,128)(2,1)S(1)} %copy-done.33, bf16[1024,384]{1,0:T(8,128)(2,1)S(1)} %copy-done.35, bf16[1024,384]{1,0:T(8,128)(2,1)S(1)} %copy-done.38, ...), custom_call_target="tpu_custom_call" | custom-call | tf_op jit(solution)/shard_map/pallas_call | solution.py:1138
  353.6 17.0 %collective-permute-done.43 = bf16[192,768]{1,0:T(8,128)(2,1)S(1)} collective-permute-done((bf16[192,768]{1,0:T(8,128)(2,1)S(1)}, bf16[192,768]{1,0:T(8,128)(2,1)S(1)}, u32[]{:S(2)}, u32[]{:S(2)}) %collective-permute-start.43) | collective-permute-done | bytes 294944 | tf_op jit(solution)/shard_map/pair_w/ppermute | solution.py:598
  373.5 6.0 %collective-permute-done.47 = bf16[192,768]{1,0:T(8,128)(2,1)S(1)} collective-permute-done((bf16[192,768]{1,0:T(8,128)(2,1)S(1)}, bf16[192,768]{1,0:T(8,128)(2,1)S(1)}, u32[]{:S(2)}, u32[]{:S(2)}) %collective-permute-start.47) | collective-permute-done | bytes 294944 | tf_op jit(solution)/shard_map/out_z/ppermute | solution.py:598
  379.6 4.2 %collective-permute-start.49 = (bf16[208,768]{1,0:T(8,128)(2,1)S(1)}, bf16[208,768]{1,0:T(8,128)(2,1)S(1)}, u32[]{:S(2)}, u32[]{:S(2)}) collective-permute-start(bf16[208,768]{1,0:T(8,128)(2,1)S(1)} %add_convert_fusion.13), channel_id=1, source_target_pairs={{0,16},{4,20},{8,24},{12,28},{16,0},{20,4},{24,8},{28,12},{1,17},{... | collective-permute-start | bytes 958472 | tf_op jit(solution)/shard_map/val_w/ppermute | solution.py:598
  385.9 18.6 %collective-permute-done.49 = bf16[208,768]{1,0:T(8,128)(2,1)S(1)} collective-permute-done((bf16[208,768]{1,0:T(8,128)(2,1)S(1)}, bf16[208,768]{1,0:T(8,128)(2,1)S(1)}, u32[]{:S(2)}, u32[]{:S(2)}) %collective-permute-start.49) | collective-permute-done | bytes 319520 | tf_op jit(solution)/shard_map/val_w/ppermute | solution.py:598
  404.8 3.6 collective-permute-done.52
  (572 shorter events, 168.6 us)
Async XLA Ops:
  6.8 31.1 %collective-permute-start.2 = (bf16[592,768]{1,0:T(8,128)(2,1)S(1)}, bf16[592,768]{1,0:T(8,128)(2,1)}, u32[]{:S(2)}, u32[]{:S(2)}) collective-permute-start(bf16[592,768]{1,0:T(8,128)(2,1)S(1)} %fusion.20.one_ref.refs_6_), channel_id=1, source_target_pairs={{0,1},{1,0},{2,3},{3,2},{4,5},{5,4},{6,7},{7,6},{8,9},{9,8},{10,11... | collective-permute-start | bytes 2727944 | tf_op jit(solution)/shard_map/weights/ppermute | solution.py:594
  7.2 28.3 %collective-permute-start.3 = (bf16[592,768]{1,0:T(8,128)(2,1)S(1)}, bf16[592,768]{1,0:T(8,128)(2,1)}, u32[]{:S(2)}, u32[]{:S(2)}) collective-permute-start(bf16[592,768]{1,0:T(8,128)(2,1)S(1)} %fusion.20.one_ref.refs_6_), channel_id=1, source_target_pairs={{0,2},{1,3},{2,0},{3,1},{4,6},{5,7},{6,4},{7,5},{8,10},{9,11},{10,... | collective-permute-start | bytes 2727944 | tf_op jit(solution)/shard_map/weights/ppermute | solution.py:594
  9.7 25.4 %collective-permute-start.1 = (bf16[16,768]{1,0:T(8,128)(2,1)S(1)}, bf16[16,768]{1,0:T(8,128)(2,1)S(1)}, u32[]{:S(2)}, u32[]{:S(2)}) collective-permute-start(bf16[16,768]{1,0:T(8,128)(2,1)S(1)} %get-tuple-element.418), channel_id=1, source_target_pairs={{1,0},{2,1},{3,2},{5,4},{6,5},{7,6},{9,8},{10,9},{11,10},{13,12},{... | collective-permute-start | bytes 73736 | tf_op jit(solution)/shard_map/ppermute | solution.py:676
  11.0 24.2 %collective-permute-start = (bf16[16,768]{1,0:T(8,128)(2,1)S(1)}, bf16[16,768]{1,0:T(8,128)(2,1)S(1)}, u32[]{:S(2)}, u32[]{:S(2)}) collective-permute-start(bf16[16,768]{1,0:T(8,128)(2,1)S(1)} %get-tuple-element.417), channel_id=1, source_target_pairs={{0,1},{1,2},{2,3},{4,5},{5,6},{6,7},{8,9},{9,10},{10,11},{12,13},{... | collective-permute-start | bytes 73736 | tf_op jit(solution)/shard_map/ppermute | solution.py:675
  15.1 19.9 %collective-permute-start.6 = (bf16[128,768]{1,0:T(8,128)(2,1)S(1)}, bf16[128,768]{1,0:T(8,128)(2,1)S(1)}, u32[]{:S(2)}, u32[]{:S(2)}) collective-permute-start(bf16[128,768]{1,0:T(8,128)(2,1)S(1)} %add_convert_fusion.23), channel_id=1, source_target_pairs={{0,2},{1,3},{2,0},{3,1},{4,6},{5,7},{6,4},{7,5},{8,10},{9,11},{10,... | collective-permute-start | bytes 589832 | tf_op jit(solution)/shard_map/land/ppermute | solution.py:594
  150.3 25.4 %collective-permute-start.16 = (bf16[2,768,768]{2,1,0:T(8,128)(2,1)}, bf16[2,768,768]{2,1,0:T(8,128)(2,1)}, u32[]{:S(2)}, u32[]{:S(2)}) collective-permute-start(bf16[2,768,768]{2,1,0:T(8,128)(2,1)} %get-tuple-element.251), channel_id=1, source_target_pairs={{0,1},{1,0},{2,3},{3,2},{4,5},{5,4},{6,7},{7,6},{8,9},{9,8},{10,11... | collective-permute-start | bytes 7077896 | tf_op jit(solution)/shard_map/inner_core/ppermute | solution.py:594
  150.3 25.5 %collective-permute-start.17 = (bf16[2,768,768]{2,1,0:T(8,128)(2,1)}, bf16[2,768,768]{2,1,0:T(8,128)(2,1)}, u32[]{:S(2)}, u32[]{:S(2)}) collective-permute-start(bf16[2,768,768]{2,1,0:T(8,128)(2,1)} %get-tuple-element.252), channel_id=1, source_target_pairs={{0,1},{1,0},{2,3},{3,2},{4,5},{5,4},{6,7},{7,6},{8,9},{9,8},{10,11... | collective-permute-start | bytes 7077896 | tf_op jit(solution)/shard_map/outer_core/ppermute | solution.py:594
  195.7 35.8 %collective-permute-start.23 = (bf16[2,384,768]{2,1,0:T(8,128)(2,1)S(1)}, bf16[2,384,768]{2,1,0:T(8,128)(2,1)S(1)}, u32[]{:S(2)}, u32[]{:S(2)}) collective-permute-start(bf16[2,384,768]{2,1,0:T(8,128)(2,1)S(1)} %add_convert_fusion.4), channel_id=1, source_target_pairs={{0,4},{4,0},{8,12},{12,8},{16,20},{20,16},{24,28},{28,24},{1,5},{5... | collective-permute-start | bytes 3538952 | tf_op jit(solution)/shard_map/outer_y/ppermute | solution.py:598
  197.5 34.0 %collective-permute-start.24 = (bf16[768,768]{1,0:T(8,128)(2,1)S(1)}, bf16[768,768]{1,0:T(8,128)(2,1)S(1)}, u32[]{:S(2)}, u32[]{:S(2)}) collective-permute-start(bf16[768,768]{1,0:T(8,128)(2,1)S(1)} %fusion.14), channel_id=1, source_target_pairs={{0,2},{1,3},{2,0},{3,1},{4,6},{5,7},{6,4},{7,5},{8,10},{9,11},{10,... | collective-permute-start | bytes 3538952 | tf_op jit(solution)/shard_map/inner_x/ppermute | solution.py:594
  210.7 19.5 %collective-permute-start.22 = (bf16[2,192,768]{2,1,0:T(8,128)(2,1)S(1)}, bf16[2,192,768]{2,1,0:T(8,128)(2,1)S(1)}, u32[]{:S(2)}, u32[]{:S(2)}) collective-permute-start(bf16[2,192,768]{2,1,0:T(8,128)(2,1)S(1)} %get-tuple-element.277), channel_id=1, source_target_pairs={{0,1},{1,0},{2,3},{3,2},{4,5},{5,4},{6,7},{7,6},{8,9},{9,8},{10,11... | collective-permute-start | bytes 1769480 | tf_op jit(solution)/shard_map/out_core/ppermute | solution.py:594
  211.7 18.4 %collective-permute-start.21 = (f32[3,64,256]{2,1,0:T(8,128)S(1)}, f32[3,64,256]{2,1,0:T(8,128)S(1)}, u32[]{:S(2)}, u32[]{:S(2)}) collective-permute-start(f32[3,64,256]{2,1,0:T(8,128)S(1)} %slice.251), channel_id=1, source_target_pairs={{0,2},{1,3},{2,0},{3,1},{4,6},{5,7},{6,4},{7,5},{8,10},{9,11},{10,... | collective-permute-start | bytes 589832 | tf_op jit(solution)/shard_map/mixed_grad_x/ppermute | solution.py:594
  231.4 18.1 %collective-permute-start.25 = (bf16[3,80,256]{2,1,0:T(8,128)(2,1)S(1)}, bf16[3,80,256]{2,1,0:T(8,128)(2,1)S(1)}, u32[]{:S(2)}, u32[]{:S(2)}) collective-permute-start(bf16[3,80,256]{2,1,0:T(8,128)(2,1)S(1)} %get-tuple-element.293), channel_id=1, source_target_pairs={{0,1},{1,0},{2,3},{3,2},{4,5},{5,4},{6,7},{7,6},{8,9},{9,8},{10,11... | collective-permute-start | bytes 368648 | tf_op jit(solution)/shard_map/carried_grad/ppermute | solution.py:594
  231.7 17.9 %collective-permute-start.27 = (bf16[3,80,256]{2,1,0:T(8,128)(2,1)S(1)}, bf16[3,80,256]{2,1,0:T(8,128)(2,1)S(1)}, u32[]{:S(2)}, u32[]{:S(2)}) collective-permute-start(bf16[3,80,256]{2,1,0:T(8,128)(2,1)S(1)} %get-tuple-element.293), channel_id=1, source_target_pairs={{0,3},{1,2},{2,1},{3,0},{4,7},{5,6},{6,5},{7,4},{8,11},{9,10},{10,... | collective-permute-start | bytes 368648 | tf_op jit(solution)/shard_map/carried_grad/ppermute | solution.py:594
  232.6 17.0 %collective-permute-start.26 = (bf16[3,80,256]{2,1,0:T(8,128)(2,1)S(1)}, bf16[3,80,256]{2,1,0:T(8,128)(2,1)S(1)}, u32[]{:S(2)}, u32[]{:S(2)}) collective-permute-start(bf16[3,80,256]{2,1,0:T(8,128)(2,1)S(1)} %get-tuple-element.293), channel_id=1, source_target_pairs={{0,2},{1,3},{2,0},{3,1},{4,6},{5,7},{6,4},{7,5},{8,10},{9,11},{10,... | collective-permute-start | bytes 368648 | tf_op jit(solution)/shard_map/carried_grad/ppermute | solution.py:594
  237.3 17.4 %collective-permute-start.28 = (bf16[384,768]{1,0:T(8,128)(2,1)S(1)}, bf16[384,768]{1,0:T(8,128)(2,1)S(1)}, u32[]{:S(2)}, u32[]{:S(2)}) collective-permute-start(bf16[384,768]{1,0:T(8,128)(2,1)S(1)} %constant_dynamic-slice_fusion.3), channel_id=1, source_target_pairs={{0,4},{4,0},{8,12},{12,8},{16,20},{20,16},{24,28},{28,24},{1,5},{5... | collective-permute-start | bytes 1769480 | tf_op jit(solution)/shard_map/inner_y/ppermute | solution.py:598
  237.6 17.1 %collective-permute-start.29 = (bf16[2,192,768]{2,1,0:T(8,128)(2,1)S(1)}, bf16[2,192,768]{2,1,0:T(8,128)(2,1)S(1)}, u32[]{:S(2)}, u32[]{:S(2)}) collective-permute-start(bf16[2,192,768]{2,1,0:T(8,128)(2,1)S(1)} %constant_dynamic-slice_fusion.2), channel_id=1, source_target_pairs={{0,8},{4,12},{8,0},{12,4},{16,24},{20,28},{24,16},{28,20},{1,9},{5... | collective-permute-start | bytes 1769480 | tf_op jit(solution)/shard_map/outer_z/ppermute | solution.py:598
  271.1 18.3 %collective-permute-start.30 = (bf16[2,384,768]{2,1,0:T(8,128)(2,1)}, bf16[2,384,768]{2,1,0:T(8,128)(2,1)}, u32[]{:S(2)}, u32[]{:S(2)}) collective-permute-start(bf16[2,384,768]{2,1,0:T(8,128)(2,1)} %get-tuple-element.323), channel_id=1, source_target_pairs={{0,1},{1,0},{2,3},{3,2},{4,5},{5,4},{6,7},{7,6},{8,9},{9,8},{10,11... | collective-permute-start | bytes 3538952 | tf_op jit(solution)/shard_map/pair_core/ppermute | solution.py:594
  273.0 16.4 %collective-permute-start.31 = (f32[128,768]{1,0:T(8,128)}, f32[128,768]{1,0:T(8,128)S(1)}, u32[]{:S(2)}, u32[]{:S(2)}) collective-permute-start(f32[128,768]{1,0:T(8,128)} %constant_dynamic-slice_fusion.1), channel_id=1, source_target_pairs={{0,1},{1,0},{2,3},{3,2},{4,5},{5,4},{6,7},{7,6},{8,9},{9,8},{10,11... | collective-permute-start | bytes 1179656 | tf_op jit(solution)/shard_map/land_core/ppermute | solution.py:594
  285.4 28.0 %collective-permute-start.32 = (bf16[384,768]{1,0:T(8,128)(2,1)S(1)}, bf16[384,768]{1,0:T(8,128)(2,1)S(1)}, u32[]{:S(2)}, u32[]{:S(2)}) collective-permute-start(bf16[384,768]{1,0:T(8,128)(2,1)S(1)} %copy-done.106), channel_id=1, source_target_pairs={{0,8},{4,12},{8,0},{12,4},{16,24},{20,28},{24,16},{28,20},{1,9},{5... | collective-permute-start | bytes 1769480 | tf_op jit(solution)/shard_map/inner_z/ppermute | solution.py:598
  285.7 27.6 %collective-permute-start.33 = (bf16[2,192,768]{2,1,0:T(8,128)(2,1)S(1)}, bf16[2,192,768]{2,1,0:T(8,128)(2,1)S(1)}, u32[]{:S(2)}, u32[]{:S(2)}) collective-permute-start(bf16[2,192,768]{2,1,0:T(8,128)(2,1)S(1)} %copy-done.104), channel_id=1, source_target_pairs={{0,16},{4,20},{8,24},{12,28},{16,0},{20,4},{24,8},{28,12},{1,17},{... | collective-permute-start | bytes 1769480 | tf_op jit(solution)/shard_map/outer_w/ppermute | solution.py:598
  299.7 22.3 %collective-permute-start.36 = (bf16[384,768]{1,0:T(8,128)(2,1)}, bf16[384,768]{1,0:T(8,128)(2,1)}, u32[]{:S(2)}, u32[]{:S(2)}) collective-permute-start(bf16[384,768]{1,0:T(8,128)(2,1)} %fusion.22), channel_id=1, source_target_pairs={{0,2},{1,3},{2,0},{3,1},{4,6},{5,7},{6,4},{7,5},{8,10},{9,11},{10,... | collective-permute-start | bytes 1769480 | tf_op jit(solution)/shard_map/pair_x/ppermute | solution.py:594
  326.8 18.0 %collective-permute-start.39 = (bf16[192,768]{1,0:T(8,128)(2,1)S(1)}, bf16[192,768]{1,0:T(8,128)(2,1)S(1)}, u32[]{:S(2)}, u32[]{:S(2)}) collective-permute-start(bf16[192,768]{1,0:T(8,128)(2,1)S(1)} %slice_bitcast_fusion), channel_id=1, source_target_pairs={{0,2},{1,3},{2,0},{3,1},{4,6},{5,7},{6,4},{7,5},{8,10},{9,11},{10,... | collective-permute-start | bytes 884744 | tf_op jit(solution)/shard_map/outer_x/ppermute | solution.py:594
  327.8 17.0 %collective-permute-start.42 = (bf16[192,768]{1,0:T(8,128)(2,1)S(1)}, bf16[192,768]{1,0:T(8,128)(2,1)S(1)}, u32[]{:S(2)}, u32[]{:S(2)}) collective-permute-start(bf16[192,768]{1,0:T(8,128)(2,1)S(1)} %fusion.38), channel_id=1, source_target_pairs={{0,4},{4,0},{8,12},{12,8},{16,20},{20,16},{24,28},{28,24},{1,5},{5... | collective-permute-start | bytes 884744 | tf_op jit(solution)/shard_map/out_y/ppermute | solution.py:598
  329.4 44.2 %collective-permute-start.46 = (bf16[384,768]{1,0:T(8,128)(2,1)}, bf16[384,768]{1,0:T(8,128)(2,1)S(1)}, u32[]{:S(2)}, u32[]{:S(2)}) collective-permute-start(bf16[384,768]{1,0:T(8,128)(2,1)} %add_convert_fusion.7), channel_id=1, source_target_pairs={{0,16},{4,20},{8,24},{12,28},{16,0},{20,4},{24,8},{28,12},{1,17},{... | collective-permute-start | bytes 1769480 | tf_op jit(solution)/shard_map/inner_w/ppermute | solution.py:598
  345.0 25.6 %collective-permute-start.43 = (bf16[192,768]{1,0:T(8,128)(2,1)S(1)}, bf16[192,768]{1,0:T(8,128)(2,1)S(1)}, u32[]{:S(2)}, u32[]{:S(2)}) collective-permute-start(bf16[192,768]{1,0:T(8,128)(2,1)S(1)} %add_convert_fusion.20), channel_id=1, source_target_pairs={{0,16},{4,20},{8,24},{12,28},{16,0},{20,4},{24,8},{28,12},{1,17},{... | collective-permute-start | bytes 884744 | tf_op jit(solution)/shard_map/pair_w/ppermute | solution.py:598
  347.7 25.5 %collective-permute-start.44 = (bf16[208,768]{1,0:T(8,128)(2,1)S(1)}, bf16[208,768]{1,0:T(8,128)(2,1)S(1)}, u32[]{:S(2)}, u32[]{:S(2)}) collective-permute-start(bf16[208,768]{1,0:T(8,128)(2,1)S(1)} %fusion.21), channel_id=1, source_target_pairs={{0,4},{4,0},{8,12},{12,8},{16,20},{20,16},{24,28},{28,24},{1,5},{5... | collective-permute-start | bytes 958472 | tf_op jit(solution)/shard_map/val_y/ppermute | solution.py:598
  349.3 23.9 %collective-permute-start.45 = (bf16[192,768]{1,0:T(8,128)(2,1)S(1)}, bf16[192,768]{1,0:T(8,128)(2,1)S(1)}, u32[]{:S(2)}, u32[]{:S(2)}) collective-permute-start(bf16[192,768]{1,0:T(8,128)(2,1)S(1)} %fusion.37), channel_id=1, source_target_pairs={{0,8},{4,12},{8,0},{12,4},{16,24},{20,28},{24,16},{28,20},{1,9},{5... | collective-permute-start | bytes 884744 | tf_op jit(solution)/shard_map/outer_z2/ppermute | solution.py:598
  352.1 27.5 %collective-permute-start.47 = (bf16[192,768]{1,0:T(8,128)(2,1)S(1)}, bf16[192,768]{1,0:T(8,128)(2,1)S(1)}, u32[]{:S(2)}, u32[]{:S(2)}) collective-permute-start(bf16[192,768]{1,0:T(8,128)(2,1)S(1)} %add_convert_fusion.19), channel_id=1, source_target_pairs={{0,8},{4,12},{8,0},{12,4},{16,24},{20,28},{24,16},{28,20},{1,9},{5... | collective-permute-start | bytes 884744 | tf_op jit(solution)/shard_map/out_z/ppermute | solution.py:598
  373.3 35.1 %collective-permute-start.51 = (bf16[384,768]{1,0:T(8,128)(2,1)S(1)}, bf16[384,768]{1,0:T(8,128)(2,1)S(1)}, u32[]{:S(2)}, u32[]{:S(2)}) collective-permute-start(bf16[384,768]{1,0:T(8,128)(2,1)S(1)} %pad_maximum_fusion.4), channel_id=1, source_target_pairs={{0,4},{4,0},{8,12},{12,8},{16,20},{20,16},{24,28},{28,24},{1,5},{5... | collective-permute-start | bytes 1769480 | tf_op jit(solution)/shard_map/outer_y2/ppermute | solution.py:598
  379.6 24.9 %collective-permute-start.49 = (bf16[208,768]{1,0:T(8,128)(2,1)S(1)}, bf16[208,768]{1,0:T(8,128)(2,1)S(1)}, u32[]{:S(2)}, u32[]{:S(2)}) collective-permute-start(bf16[208,768]{1,0:T(8,128)(2,1)S(1)} %add_convert_fusion.13), channel_id=1, source_target_pairs={{0,16},{4,20},{8,24},{12,28},{16,0},{20,4},{24,8},{28,12},{1,17},{... | collective-permute-start | bytes 958472 | tf_op jit(solution)/shard_map/val_w/ppermute | solution.py:598
  383.9 24.5 %collective-permute-start.52 = (bf16[192,768]{1,0:T(8,128)(2,1)S(1)}, bf16[192,768]{1,0:T(8,128)(2,1)S(1)}, u32[]{:S(2)}, u32[]{:S(2)}) collective-permute-start(bf16[192,768]{1,0:T(8,128)(2,1)S(1)} %add_convert_fusion.16), channel_id=1, source_target_pairs={{0,16},{4,20},{8,24},{12,28},{16,0},{20,4},{24,8},{28,12},{1,17},{... | collective-permute-start | bytes 884744 | tf_op jit(solution)/shard_map/out_w/ppermute | solution.py:598
  384.1 26.1 %collective-permute-start.54 = (bf16[384,768]{1,0:T(8,128)(2,1)S(1)}, bf16[384,768]{1,0:T(8,128)(2,1)S(1)}, u32[]{:S(2)}, u32[]{:S(2)}) collective-permute-start(bf16[384,768]{1,0:T(8,128)(2,1)S(1)} %add_convert_fusion.5), channel_id=1, source_target_pairs={{0,4},{4,0},{8,12},{12,8},{16,20},{20,16},{24,28},{28,24},{1,5},{5... | collective-permute-start | bytes 1769480 | tf_op jit(solution)/shard_map/inner_y2/ppermute | solution.py:598
  (164 other events, 1379.4 us)

commit v5 on v4

--- a/solution.py
+++ b/solution.py
@@ -640,13 +640,14 @@
     code = line[HALF : HALF + rows].reshape(rows, 1)
     line = line.reshape(1, ext)
     segment_row = jnp.where(pad_mask > 0, doc_ids * LAND + landmark_ids, -1)
+    tap_pad = jnp.pad(conv_weight, ((0, TAP_ROWS - own), (0, width - KW)))
+    packed = jnp.concatenate([w_query.T, w_key.T, w_value.T, tap_pad], axis=0)
+    packed, segment_row = gate(packed, segment_row)
     columns = jnp.arange(SEGS, dtype=jnp.int32)
     counts = jnp.sum((segment_row[:, None] == columns[None, :]).astype(F32), axis=0)
     segment = lax.dynamic_slice_in_dim(segment_row, me * rows, rows, 0)
     member = (segment[:, None] == columns[None, :]).astype(BF)
 
-    tap_pad = jnp.pad(conv_weight, ((0, TAP_ROWS - own), (0, width - KW)))
-    packed = jnp.concatenate([w_query.T, w_key.T, w_value.T, tap_pad], axis=0)
     packed, member_in = gate(packed, member)
     got = spread(packed, "weights")
     out_packed, far_weights = gate(w_output, got[2])

time: 424 us -> 424 us (level)
  no operation moved by 1% of the time
where the time goes in v5:
time: 424 us; the launch traced here: 418 us
  Pallas kernels  157 us (37%)
  waiting for transfers between devices  97.7 us (23%)
  other arithmetic  54.6 us (13%)
  starting transfers between devices  52.4 us (12%)
  local copies, waits for them, and re-layouts  42.9 us (10%)
  matrix products  9.64 us (2%)
    ppermute x19, waiting for transfers between devices, swap_batch(): lax.ppermute(value, 'batch', [(i, i ^ bit) for i in range(batch_size)])  63.5 us
    pallas_call x2, Pallas kernels, feed_back(): pl.pallas_call(feed_back_kernel, grid_spec=grid_spec, out_shape=[shape_of...  35.1 us
    ppermute x32, waiting for transfers between devices, swap(): return lax.ppermute(value, 'head', [(i, i ^ bit) for i in range(groups)])  34.2 us
    unnamed x282, local copies, waits for them, and re-layouts  32.7 us
    ppermute x32, starting transfers between devices, swap(): return lax.ppermute(value, 'head', [(i, i ^ bit) for i in range(groups)])  22.6 us
    ppermute x19, starting transfers between devices, swap_batch(): lax.ppermute(value, 'batch', [(i, i ^ bit) for i in range(batch_size)])  21.1 us
    pallas_call x1, Pallas kernels, shards(): call(feed_kernel, (ff // block,), [whole((rows, width)), column(width, bl...  16.5 us
    pallas_call x2, Pallas kernels, shards(): conv_back_call(code, line, heads_grad[half], edge_parts[half], values[hal...  11.8 us
  transfers between devices with their start and end apart: 55, of which 11 were waited for; matrix products, arithmetic and copies ran while one was open for 10% of the time, Pallas kernels for 23%

profile of v5, /device:TPU:0, one launch (start us, length us, event | category | flops | bytes accessed | tf_op | source)
XLA Modules:
  0.0 417.7 jit_solution(13860604969081461287)
XLA Ops:
  11.2 3.0 collective-permute-start
  17.3 18.0 %collective-permute-done.6 = bf16[128,768]{1,0:T(8,128)(2,1)S(1)} collective-permute-done((bf16[128,768]{1,0:T(8,128)(2,1)S(1)}, bf16[128,768]{1,0:T(8,128)(2,1)S(1)}, u32[]{:S(2)}, u32[]{:S(2)}) %collective-permute-start.6) | collective-permute-done | bytes 196640 | tf_op jit(solution)/shard_map/land/ppermute | solution.py:594
  39.4 4.0 shard_map.255
  47.1 4.3 %shard_map.258 = (f32[6,72,256]{2,1,0:T(8,128)S(1)}, bf16[1024,1536]{1,0:T(8,128)(2,1)S(1)}) custom-call(s32[1024,1]{1,0:T(8,128)S(1)} %copy.59.code_ref, bf16[1024,384]{1,0:T(8,128)(2,1)S(1)} %get-tuple-element.213.k_ref, bf16[1152,384]{1,0:T(8,128)(2,1)S(1)} %get-tuple-element.239.v_ref, bf16[6,64,256]{2,1,0:T(8,128)(2,1)S(1)} %get-tuple-element.215.lq_ref), custom_call_target="tpu_custom_call" | custom-call | flops 8053063 | bytes 94371 | tf_op jit(solution)/shard_map/pallas_call | solution.py:721
  57.6 4.0 shard_map.256
  62.5 4.0 shard_map.260
  69.4 5.4 %shard_map.261 = (f32[3,64,256]{2,1,0:T(8,128)S(1)}, f32[3,64,256]{2,1,0:T(8,128)S(1)}, f32[6,3,4,64,256]{4,3,2,1,0:T(8,128)S(1)}) custom-call(bf16[3,64,256]{2,1,0:T(8,128)(2,1)S(1)} %slice.235.lq_ref, bf16[3,64,256]{2,1,0:T(8,128)(2,1)S(1)} %slice.236.lk_ref), custom_call_target="tpu_custom_call" | custom-call | flops 36238784 | bytes 94371 | tf_op jit(solution)/shard_map/pallas_call | solution.py:731
  79.1 4.1 shard_map.263.p_ref
  83.3 4.7 %shard_map.264.p_ref = bf16[1024,1536]{1,0:T(8,128)(2,1)S(1)} custom-call(s32[1024,1]{1,0:T(8,128)S(1)} %copy.59.code_ref, bf16[1024,384]{1,0:T(8,128)(2,1)S(1)} %copy-done.46, bf16[6,64,256]{2,1,0:T(8,128)(2,1)S(1)} %copy-done.74), custom_call_target="tpu_custom_call" | custom-call | flops 4026531 | bytes 78643 | tf_op jit(solution)/shard_map/pallas_call | solution.py:775
  92.7 3.0 shard_map.266.conv_ref
  95.8 3.0 shard_map.267.conv_ref
  106.2 16.5 %shard_map.270 = (bf16[1024,3072]{1,0:T(8,128)(2,1)S(1)}, bf16[1024,3072]{1,0:T(8,128)(2,1)}, f32[1024,768]{1,0:T(8,128)S(1)}) custom-call(bf16[1024,768]{1,0:T(8,128)(2,1)S(1)} %fusion.8.x_ref, bf16[768,3072]{1,0:T(8,128)(2,1)S(1)} %bitcast.96, bf16[3072,768]{1,0:T(8,128)(2,1)S(1)} %bitcast.98), custom_call_target="tpu_custom_call" | custom-call | flops 193273536 | bytes 534773 | tf_op jit(solution)/shard_map/pallas_call | solution.py:806
  131.1 17.8 %shard_map.271 = (bf16[2,768,768]{2,1,0:T(8,128)(2,1)}, bf16[2,768,768]{2,1,0:T(8,128)(2,1)}, f32[1024,768]{1,0:T(8,128)S(1)}) custom-call(s32[4]{0:T(128)S(1)} %get-tuple-element.466.table, bf16[1024,768]{1,0:T(8,128)(2,1)S(1)} %get-tuple-element.412.og_ref, bf16[1024,768]{1,0:T(8,128)(2,1)S(1)} %fusion.8.x_ref, bf16[768,3072]{1,0:T(8,128)(2,1)} %wi_ref.5, ...), custom_call_target="tpu_custom_call" | custom-call | flops 9663676416 | bytes 25165824 | tf_op jit(solution)/shard_map/pallas_call | solution.py:852
  158.7 17.3 %shard_map.272 = (bf16[2,768,768]{2,1,0:T(8,128)(2,1)S(1)}, bf16[2,768,768]{2,1,0:T(8,128)(2,1)S(1)}, f32[1024,768]{1,0:T(8,128)S(1)}) custom-call(s32[4]{0:T(128)S(1)} %get-tuple-element.465.table, bf16[1024,768]{1,0:T(8,128)(2,1)S(1)} %copy-done.61, bf16[1024,768]{1,0:T(8,128)(2,1)S(1)} %copy-done.26, bf16[768,3072]{1,0:T(8,128)(2,1)} %wi_ref.5, ...), custom_call_target="tpu_custom_call" | custom-call | flops 9663676416 | bytes 25165824 | tf_op jit(solution)/shard_map/pallas_call | solution.py:852
  192.8 3.0 collective-permute-start.19
  199.3 4.8 %shard_map.275 = (bf16[1024,384]{1,0:T(8,128)(2,1)S(1)}, f32[6,64,256]{2,1,0:T(8,128)S(1)}) custom-call(bf16[1024,384]{1,0:T(8,128)(2,1)S(1)} %select_convert_fusion.1.hg_ref, bf16[1024,1536]{1,0:T(8,128)(2,1)S(1)} %copy-done.3, bf16[1024,384]{1,0:T(8,128)(2,1)S(1)} %copy-done.44, bf16[6,80,256]{2,1,0:T(8,128)(2,1)S(1)} %pad_maximum_fusion.12.mix_ref, ...), custom_call_target="tpu_custom_call" | custom-call | flops 12079595 | bytes 110100 | tf_op jit(solution)/shard_map/pallas_call | solution.py:998
  204.2 5.2 %shard_map.276 = (bf16[1024,384]{1,0:T(8,128)(2,1)S(1)}, f32[6,64,256]{2,1,0:T(8,128)S(1)}) custom-call(bf16[1024,384]{1,0:T(8,128)(2,1)S(1)} %select_convert_fusion.hg_ref, bf16[1024,1536]{1,0:T(8,128)(2,1)S(1)} %copy-done.1, bf16[1024,384]{1,0:T(8,128)(2,1)S(1)} %copy-done.47, bf16[6,80,256]{2,1,0:T(8,128)(2,1)S(1)} %pad_maximum_fusion.13.mix_ref, ...), custom_call_target="tpu_custom_call" | custom-call | flops 12079595 | bytes 110100 | tf_op jit(solution)/shard_map/pallas_call | solution.py:998
  214.3 16.1 %collective-permute-done.21.b_ref = f32[3,64,256]{2,1,0:T(8,128)S(1)} collective-permute-done((f32[3,64,256]{2,1,0:T(8,128)S(1)}, f32[3,64,256]{2,1,0:T(8,128)S(1)}, u32[]{:S(2)}, u32[]{:S(2)}) %collective-permute-start.21) | collective-permute-done | bytes 196640 | tf_op jit(solution)/shard_map/mixed_grad_x/ppermute | solution.py:594
  239.7 10.1 %shard_map.279 = (f32[3,64,256]{2,1,0:T(8,128)S(1)}, f32[3,64,256]{2,1,0:T(8,128)S(1)}) custom-call(f32[3,64,256]{2,1,0:T(8,128)S(1)} %get-tuple-element.292.mg_ref, f32[3,64,256]{2,1,0:T(8,128)S(1)} %copy-done.79, f32[3,64,256]{2,1,0:T(8,128)S(1)} %copy-done.88, f32[6,3,4,64,256]{4,3,2,1,0:T(8,128)S(1)} %bitcast.94, bf16[3,64,256]{2,1,0:T(8,128)(2,1)S(1)} %copy-done.70, ...), custom_call_target="tpu_custom_call" | custom-call | tf_op jit(solution)/shard_map/pallas_call | solution.py:1028
  250.0 4.8 %shard_map.280 = (bf16[1024,384]{1,0:T(8,128)(2,1)S(1)}, f32[1024,384]{1,0:T(8,128)S(1)}, f32[6,64,256]{2,1,0:T(8,128)S(1)}) custom-call(bf16[1024,384]{1,0:T(8,128)(2,1)S(1)} %copy-done.53, bf16[1152,384]{1,0:T(8,128)(2,1)S(1)} %copy-done.7, bf16[1024,1536]{1,0:T(8,128)(2,1)S(1)} %copy-done.51, f32[6,1,256]{2,1,0:T(1,128)S(1)} %subtract_exponential_fusion.1.f_ref, ...), custom_call_target="tpu_custom_call" | custom-call | flops 16106127 | bytes 157286 | tf_op jit(solution)/shard_map/pallas_call | solution.py:1050
  258.5 4.6 %shard_map.281 = (bf16[1024,384]{1,0:T(8,128)(2,1)S(1)}, f32[1024,384]{1,0:T(8,128)S(1)}, f32[6,64,256]{2,1,0:T(8,128)S(1)}) custom-call(bf16[1024,384]{1,0:T(8,128)(2,1)S(1)} %copy-done.55, bf16[1152,384]{1,0:T(8,128)(2,1)S(1)} %copy-done.11, bf16[1024,1536]{1,0:T(8,128)(2,1)S(1)} %copy-done.49, f32[6,1,256]{2,1,0:T(1,128)S(1)} %subtract_exponential_fusion.f_ref, ...), custom_call_target="tpu_custom_call" | custom-call | flops 16106127 | bytes 157286 | tf_op jit(solution)/shard_map/pallas_call | solution.py:1050
  266.0 4.3 %shard_map.282 = (bf16[2,384,768]{2,1,0:T(8,128)(2,1)S(1)}, bf16[2,384,768]{2,1,0:T(8,128)(2,1)}) custom-call(bf16[1024,768]{1,0:T(8,128)(2,1)S(1)} %copy-done.4, bf16[1024,384]{1,0:T(8,128)(2,1)S(1)} %get-tuple-element.318.refs_0_.refs_2_, bf16[1024,384]{1,0:T(8,128)(2,1)S(1)} %get-tuple-element.319.refs_1_.refs_3_, ...), custom_call_target="tpu_custom_call" | custom-call | tf_op jit(solution)/shard_map/pallas_call | solution.py:989
  278.9 5.8 %shard_map.283 = (bf16[1024,384]{1,0:T(8,128)(2,1)S(1)}, f32[6,8,256]{2,1,0:T(8,128)S(1)}) custom-call(s32[1024,1]{1,0:T(8,128)S(1)} %copy.59.code_ref, s32[1,1152]{1,0:T(1,128)S(1)} %reshape.159.line_ref, bf16[1024,384]{1,0:T(8,128)(2,1)S(1)} %copy-done.22, bf16[32,384]{1,0:T(8,128)(2,1)S(1)} %fusion.16.edge_ref, bf16[1152,384]{1,0:T(8,128)(2,1)S(1)} %copy-done.8, ...), custom_call_target="tpu_custom_call" | custom-call | flops 8053063 | bytes 78643 | tf_op jit(solution)/shard_map/pallas_call | solution.py:1097
  286.0 2.8 collective-permute-start.33
  291.9 6.0 %shard_map.284 = (bf16[1024,384]{1,0:T(8,128)(2,1)S(1)}, f32[6,8,256]{2,1,0:T(8,128)S(1)}) custom-call(s32[1024,1]{1,0:T(8,128)S(1)} %copy.59.code_ref, s32[1,1152]{1,0:T(1,128)S(1)} %reshape.159.line_ref, bf16[1024,384]{1,0:T(8,128)(2,1)S(1)} %copy-done.20, bf16[32,384]{1,0:T(8,128)(2,1)S(1)} %fusion.17.edge_ref, bf16[1152,384]{1,0:T(8,128)(2,1)S(1)} %copy-done.12, ...), custom_call_target="tpu_custom_call" | custom-call | flops 8053063 | bytes 78643 | tf_op jit(solution)/shard_map/pallas_call | solution.py:1097
  300.9 12.7 %collective-permute-done.32 = bf16[384,768]{1,0:T(8,128)(2,1)S(1)} collective-permute-done((bf16[384,768]{1,0:T(8,128)(2,1)S(1)}, bf16[384,768]{1,0:T(8,128)(2,1)S(1)}, u32[]{:S(2)}, u32[]{:S(2)}) %collective-permute-start.32) | collective-permute-done | bytes 589856 | tf_op jit(solution)/shard_map/inner_z/ppermute | solution.py:598
  337.9 7.1 %shard_map.286 = f32[1024,768]{1,0:T(8,128)S(1)} custom-call(f32[1024,768]{1,0:T(8,128)S(1)} %copy-done.13, bf16[1024,384]{1,0:T(8,128)(2,1)S(1)} %copy-done.29, bf16[1024,384]{1,0:T(8,128)(2,1)S(1)} %copy-done.31, bf16[1024,384]{1,0:T(8,128)(2,1)S(1)} %copy-done.33, bf16[1024,384]{1,0:T(8,128)(2,1)S(1)} %copy-done.35, bf16[1024,384]{1,0:T(8,128)(2,1)S(1)} %copy-done.38, ...), custom_call_target="tpu_custom_call" | custom-call | tf_op jit(solution)/shard_map/pallas_call | solution.py:1139
  353.8 17.0 %collective-permute-done.43 = bf16[192,768]{1,0:T(8,128)(2,1)S(1)} collective-permute-done((bf16[192,768]{1,0:T(8,128)(2,1)S(1)}, bf16[192,768]{1,0:T(8,128)(2,1)S(1)}, u32[]{:S(2)}, u32[]{:S(2)}) %collective-permute-start.43) | collective-permute-done | bytes 294944 | tf_op jit(solution)/shard_map/pair_w/ppermute | solution.py:598
  373.8 6.0 %collective-permute-done.47 = bf16[192,768]{1,0:T(8,128)(2,1)S(1)} collective-permute-done((bf16[192,768]{1,0:T(8,128)(2,1)S(1)}, bf16[192,768]{1,0:T(8,128)(2,1)S(1)}, u32[]{:S(2)}, u32[]{:S(2)}) %collective-permute-start.47) | collective-permute-done | bytes 294944 | tf_op jit(solution)/shard_map/out_z/ppermute | solution.py:598
  379.8 4.2 %collective-permute-start.49 = (bf16[208,768]{1,0:T(8,128)(2,1)S(1)}, bf16[208,768]{1,0:T(8,128)(2,1)S(1)}, u32[]{:S(2)}, u32[]{:S(2)}) collective-permute-start(bf16[208,768]{1,0:T(8,128)(2,1)S(1)} %add_convert_fusion.13), channel_id=1, source_target_pairs={{0,16},{4,20},{8,24},{12,28},{16,0},{20,4},{24,8},{28,12},{1,17},{... | collective-permute-start | bytes 958472 | tf_op jit(solution)/shard_map/val_w/ppermute | solution.py:598
  386.1 18.6 %collective-permute-done.49 = bf16[208,768]{1,0:T(8,128)(2,1)S(1)} collective-permute-done((bf16[208,768]{1,0:T(8,128)(2,1)S(1)}, bf16[208,768]{1,0:T(8,128)(2,1)S(1)}, u32[]{:S(2)}, u32[]{:S(2)}) %collective-permute-start.49) | collective-permute-done | bytes 319520 | tf_op jit(solution)/shard_map/val_w/ppermute | solution.py:598
  405.1 3.6 collective-permute-done.52
  (572 shorter events, 168.8 us)
Async XLA Ops:
  7.0 31.1 %collective-permute-start.2 = (bf16[592,768]{1,0:T(8,128)(2,1)S(1)}, bf16[592,768]{1,0:T(8,128)(2,1)}, u32[]{:S(2)}, u32[]{:S(2)}) collective-permute-start(bf16[592,768]{1,0:T(8,128)(2,1)S(1)} %fusion.20.one_ref.refs_6_), channel_id=1, source_target_pairs={{0,1},{1,0},{2,3},{3,2},{4,5},{5,4},{6,7},{7,6},{8,9},{9,8},{10,11... | collective-permute-start | bytes 2727944 | tf_op jit(solution)/shard_map/weights/ppermute | solution.py:594
  7.5 28.3 %collective-permute-start.3 = (bf16[592,768]{1,0:T(8,128)(2,1)S(1)}, bf16[592,768]{1,0:T(8,128)(2,1)}, u32[]{:S(2)}, u32[]{:S(2)}) collective-permute-start(bf16[592,768]{1,0:T(8,128)(2,1)S(1)} %fusion.20.one_ref.refs_6_), channel_id=1, source_target_pairs={{0,2},{1,3},{2,0},{3,1},{4,6},{5,7},{6,4},{7,5},{8,10},{9,11},{10,... | collective-permute-start | bytes 2727944 | tf_op jit(solution)/shard_map/weights/ppermute | solution.py:594
  9.9 25.4 %collective-permute-start.1 = (bf16[16,768]{1,0:T(8,128)(2,1)S(1)}, bf16[16,768]{1,0:T(8,128)(2,1)S(1)}, u32[]{:S(2)}, u32[]{:S(2)}) collective-permute-start(bf16[16,768]{1,0:T(8,128)(2,1)S(1)} %get-tuple-element.422), channel_id=1, source_target_pairs={{1,0},{2,1},{3,2},{5,4},{6,5},{7,6},{9,8},{10,9},{11,10},{13,12},{... | collective-permute-start | bytes 73736 | tf_op jit(solution)/shard_map/ppermute | solution.py:677
  11.2 24.2 %collective-permute-start = (bf16[16,768]{1,0:T(8,128)(2,1)S(1)}, bf16[16,768]{1,0:T(8,128)(2,1)S(1)}, u32[]{:S(2)}, u32[]{:S(2)}) collective-permute-start(bf16[16,768]{1,0:T(8,128)(2,1)S(1)} %get-tuple-element.421), channel_id=1, source_target_pairs={{0,1},{1,2},{2,3},{4,5},{5,6},{6,7},{8,9},{9,10},{10,11},{12,13},{... | collective-permute-start | bytes 73736 | tf_op jit(solution)/shard_map/ppermute | solution.py:676
  15.3 19.9 %collective-permute-start.6 = (bf16[128,768]{1,0:T(8,128)(2,1)S(1)}, bf16[128,768]{1,0:T(8,128)(2,1)S(1)}, u32[]{:S(2)}, u32[]{:S(2)}) collective-permute-start(bf16[128,768]{1,0:T(8,128)(2,1)S(1)} %add_convert_fusion.23), channel_id=1, source_target_pairs={{0,2},{1,3},{2,0},{3,1},{4,6},{5,7},{6,4},{7,5},{8,10},{9,11},{10,... | collective-permute-start | bytes 589832 | tf_op jit(solution)/shard_map/land/ppermute | solution.py:594
  150.6 25.4 %collective-permute-start.16 = (bf16[2,768,768]{2,1,0:T(8,128)(2,1)}, bf16[2,768,768]{2,1,0:T(8,128)(2,1)}, u32[]{:S(2)}, u32[]{:S(2)}) collective-permute-start(bf16[2,768,768]{2,1,0:T(8,128)(2,1)} %get-tuple-element.255), channel_id=1, source_target_pairs={{0,1},{1,0},{2,3},{3,2},{4,5},{5,4},{6,7},{7,6},{8,9},{9,8},{10,11... | collective-permute-start | bytes 7077896 | tf_op jit(solution)/shard_map/inner_core/ppermute | solution.py:594
  150.6 25.5 %collective-permute-start.17 = (bf16[2,768,768]{2,1,0:T(8,128)(2,1)}, bf16[2,768,768]{2,1,0:T(8,128)(2,1)}, u32[]{:S(2)}, u32[]{:S(2)}) collective-permute-start(bf16[2,768,768]{2,1,0:T(8,128)(2,1)} %get-tuple-element.256), channel_id=1, source_target_pairs={{0,1},{1,0},{2,3},{3,2},{4,5},{5,4},{6,7},{7,6},{8,9},{9,8},{10,11... | collective-permute-start | bytes 7077896 | tf_op jit(solution)/shard_map/outer_core/ppermute | solution.py:594
  195.9 35.8 %collective-permute-start.23 = (bf16[2,384,768]{2,1,0:T(8,128)(2,1)S(1)}, bf16[2,384,768]{2,1,0:T(8,128)(2,1)S(1)}, u32[]{:S(2)}, u32[]{:S(2)}) collective-permute-start(bf16[2,384,768]{2,1,0:T(8,128)(2,1)S(1)} %add_convert_fusion.4), channel_id=1, source_target_pairs={{0,4},{4,0},{8,12},{12,8},{16,20},{20,16},{24,28},{28,24},{1,5},{5... | collective-permute-start | bytes 3538952 | tf_op jit(solution)/shard_map/outer_y/ppermute | solution.py:598
  197.7 34.0 %collective-permute-start.24 = (bf16[768,768]{1,0:T(8,128)(2,1)S(1)}, bf16[768,768]{1,0:T(8,128)(2,1)S(1)}, u32[]{:S(2)}, u32[]{:S(2)}) collective-permute-start(bf16[768,768]{1,0:T(8,128)(2,1)S(1)} %fusion.14), channel_id=1, source_target_pairs={{0,2},{1,3},{2,0},{3,1},{4,6},{5,7},{6,4},{7,5},{8,10},{9,11},{10,... | collective-permute-start | bytes 3538952 | tf_op jit(solution)/shard_map/inner_x/ppermute | solution.py:594
  210.9 19.5 %collective-permute-start.22 = (bf16[2,192,768]{2,1,0:T(8,128)(2,1)S(1)}, bf16[2,192,768]{2,1,0:T(8,128)(2,1)S(1)}, u32[]{:S(2)}, u32[]{:S(2)}) collective-permute-start(bf16[2,192,768]{2,1,0:T(8,128)(2,1)S(1)} %get-tuple-element.281), channel_id=1, source_target_pairs={{0,1},{1,0},{2,3},{3,2},{4,5},{5,4},{6,7},{7,6},{8,9},{9,8},{10,11... | collective-permute-start | bytes 1769480 | tf_op jit(solution)/shard_map/out_core/ppermute | solution.py:594
  211.9 18.4 %collective-permute-start.21 = (f32[3,64,256]{2,1,0:T(8,128)S(1)}, f32[3,64,256]{2,1,0:T(8,128)S(1)}, u32[]{:S(2)}, u32[]{:S(2)}) collective-permute-start(f32[3,64,256]{2,1,0:T(8,128)S(1)} %slice.251), channel_id=1, source_target_pairs={{0,2},{1,3},{2,0},{3,1},{4,6},{5,7},{6,4},{7,5},{8,10},{9,11},{10,... | collective-permute-start | bytes 589832 | tf_op jit(solution)/shard_map/mixed_grad_x/ppermute | solution.py:594
  231.7 18.1 %collective-permute-start.25 = (bf16[3,80,256]{2,1,0:T(8,128)(2,1)S(1)}, bf16[3,80,256]{2,1,0:T(8,128)(2,1)S(1)}, u32[]{:S(2)}, u32[]{:S(2)}) collective-permute-start(bf16[3,80,256]{2,1,0:T(8,128)(2,1)S(1)} %get-tuple-element.297), channel_id=1, source_target_pairs={{0,1},{1,0},{2,3},{3,2},{4,5},{5,4},{6,7},{7,6},{8,9},{9,8},{10,11... | collective-permute-start | bytes 368648 | tf_op jit(solution)/shard_map/carried_grad/ppermute | solution.py:594
  231.9 17.9 %collective-permute-start.27 = (bf16[3,80,256]{2,1,0:T(8,128)(2,1)S(1)}, bf16[3,80,256]{2,1,0:T(8,128)(2,1)S(1)}, u32[]{:S(2)}, u32[]{:S(2)}) collective-permute-start(bf16[3,80,256]{2,1,0:T(8,128)(2,1)S(1)} %get-tuple-element.297), channel_id=1, source_target_pairs={{0,3},{1,2},{2,1},{3,0},{4,7},{5,6},{6,5},{7,4},{8,11},{9,10},{10,... | collective-permute-start | bytes 368648 | tf_op jit(solution)/shard_map/carried_grad/ppermute | solution.py:594
  232.8 17.0 %collective-permute-start.26 = (bf16[3,80,256]{2,1,0:T(8,128)(2,1)S(1)}, bf16[3,80,256]{2,1,0:T(8,128)(2,1)S(1)}, u32[]{:S(2)}, u32[]{:S(2)}) collective-permute-start(bf16[3,80,256]{2,1,0:T(8,128)(2,1)S(1)} %get-tuple-element.297), channel_id=1, source_target_pairs={{0,2},{1,3},{2,0},{3,1},{4,6},{5,7},{6,4},{7,5},{8,10},{9,11},{10,... | collective-permute-start | bytes 368648 | tf_op jit(solution)/shard_map/carried_grad/ppermute | solution.py:594
  237.5 17.4 %collective-permute-start.28 = (bf16[384,768]{1,0:T(8,128)(2,1)S(1)}, bf16[384,768]{1,0:T(8,128)(2,1)S(1)}, u32[]{:S(2)}, u32[]{:S(2)}) collective-permute-start(bf16[384,768]{1,0:T(8,128)(2,1)S(1)} %constant_dynamic-slice_fusion.3), channel_id=1, source_target_pairs={{0,4},{4,0},{8,12},{12,8},{16,20},{20,16},{24,28},{28,24},{1,5},{5... | collective-permute-start | bytes 1769480 | tf_op jit(solution)/shard_map/inner_y/ppermute | solution.py:598
  237.9 17.0 %collective-permute-start.29 = (bf16[2,192,768]{2,1,0:T(8,128)(2,1)S(1)}, bf16[2,192,768]{2,1,0:T(8,128)(2,1)S(1)}, u32[]{:S(2)}, u32[]{:S(2)}) collective-permute-start(bf16[2,192,768]{2,1,0:T(8,128)(2,1)S(1)} %constant_dynamic-slice_fusion.2), channel_id=1, source_target_pairs={{0,8},{4,12},{8,0},{12,4},{16,24},{20,28},{24,16},{28,20},{1,9},{5... | collective-permute-start | bytes 1769480 | tf_op jit(solution)/shard_map/outer_z/ppermute | solution.py:598
  271.4 18.3 %collective-permute-start.30 = (bf16[2,384,768]{2,1,0:T(8,128)(2,1)}, bf16[2,384,768]{2,1,0:T(8,128)(2,1)}, u32[]{:S(2)}, u32[]{:S(2)}) collective-permute-start(bf16[2,384,768]{2,1,0:T(8,128)(2,1)} %get-tuple-element.327), channel_id=1, source_target_pairs={{0,1},{1,0},{2,3},{3,2},{4,5},{5,4},{6,7},{7,6},{8,9},{9,8},{10,11... | collective-permute-start | bytes 3538952 | tf_op jit(solution)/shard_map/pair_core/ppermute | solution.py:594
  273.3 16.4 %collective-permute-start.31 = (f32[128,768]{1,0:T(8,128)}, f32[128,768]{1,0:T(8,128)S(1)}, u32[]{:S(2)}, u32[]{:S(2)}) collective-permute-start(f32[128,768]{1,0:T(8,128)} %constant_dynamic-slice_fusion.1), channel_id=1, source_target_pairs={{0,1},{1,0},{2,3},{3,2},{4,5},{5,4},{6,7},{7,6},{8,9},{9,8},{10,11... | collective-permute-start | bytes 1179656 | tf_op jit(solution)/shard_map/land_core/ppermute | solution.py:594
  285.6 28.0 %collective-permute-start.32 = (bf16[384,768]{1,0:T(8,128)(2,1)S(1)}, bf16[384,768]{1,0:T(8,128)(2,1)S(1)}, u32[]{:S(2)}, u32[]{:S(2)}) collective-permute-start(bf16[384,768]{1,0:T(8,128)(2,1)S(1)} %copy-done.106), channel_id=1, source_target_pairs={{0,8},{4,12},{8,0},{12,4},{16,24},{20,28},{24,16},{28,20},{1,9},{5... | collective-permute-start | bytes 1769480 | tf_op jit(solution)/shard_map/inner_z/ppermute | solution.py:598
  286.0 27.6 %collective-permute-start.33 = (bf16[2,192,768]{2,1,0:T(8,128)(2,1)S(1)}, bf16[2,192,768]{2,1,0:T(8,128)(2,1)S(1)}, u32[]{:S(2)}, u32[]{:S(2)}) collective-permute-start(bf16[2,192,768]{2,1,0:T(8,128)(2,1)S(1)} %copy-done.104), channel_id=1, source_target_pairs={{0,16},{4,20},{8,24},{12,28},{16,0},{20,4},{24,8},{28,12},{1,17},{... | collective-permute-start | bytes 1769480 | tf_op jit(solution)/shard_map/outer_w/ppermute | solution.py:598
  299.9 22.3 %collective-permute-start.36 = (bf16[384,768]{1,0:T(8,128)(2,1)}, bf16[384,768]{1,0:T(8,128)(2,1)}, u32[]{:S(2)}, u32[]{:S(2)}) collective-permute-start(bf16[384,768]{1,0:T(8,128)(2,1)} %fusion.22), channel_id=1, source_target_pairs={{0,2},{1,3},{2,0},{3,1},{4,6},{5,7},{6,4},{7,5},{8,10},{9,11},{10,... | collective-permute-start | bytes 1769480 | tf_op jit(solution)/shard_map/pair_x/ppermute | solution.py:594
  327.0 18.0 %collective-permute-start.39 = (bf16[192,768]{1,0:T(8,128)(2,1)S(1)}, bf16[192,768]{1,0:T(8,128)(2,1)S(1)}, u32[]{:S(2)}, u32[]{:S(2)}) collective-permute-start(bf16[192,768]{1,0:T(8,128)(2,1)S(1)} %slice_bitcast_fusion), channel_id=1, source_target_pairs={{0,2},{1,3},{2,0},{3,1},{4,6},{5,7},{6,4},{7,5},{8,10},{9,11},{10,... | collective-permute-start | bytes 884744 | tf_op jit(solution)/shard_map/outer_x/ppermute | solution.py:594
  328.1 17.0 %collective-permute-start.42 = (bf16[192,768]{1,0:T(8,128)(2,1)S(1)}, bf16[192,768]{1,0:T(8,128)(2,1)S(1)}, u32[]{:S(2)}, u32[]{:S(2)}) collective-permute-start(bf16[192,768]{1,0:T(8,128)(2,1)S(1)} %fusion.38), channel_id=1, source_target_pairs={{0,4},{4,0},{8,12},{12,8},{16,20},{20,16},{24,28},{28,24},{1,5},{5... | collective-permute-start | bytes 884744 | tf_op jit(solution)/shard_map/out_y/ppermute | solution.py:598
  329.6 44.2 %collective-permute-start.46 = (bf16[384,768]{1,0:T(8,128)(2,1)}, bf16[384,768]{1,0:T(8,128)(2,1)S(1)}, u32[]{:S(2)}, u32[]{:S(2)}) collective-permute-start(bf16[384,768]{1,0:T(8,128)(2,1)} %add_convert_fusion.7), channel_id=1, source_target_pairs={{0,16},{4,20},{8,24},{12,28},{16,0},{20,4},{24,8},{28,12},{1,17},{... | collective-permute-start | bytes 1769480 | tf_op jit(solution)/shard_map/inner_w/ppermute | solution.py:598
  345.2 25.6 %collective-permute-start.43 = (bf16[192,768]{1,0:T(8,128)(2,1)S(1)}, bf16[192,768]{1,0:T(8,128)(2,1)S(1)}, u32[]{:S(2)}, u32[]{:S(2)}) collective-permute-start(bf16[192,768]{1,0:T(8,128)(2,1)S(1)} %add_convert_fusion.20), channel_id=1, source_target_pairs={{0,16},{4,20},{8,24},{12,28},{16,0},{20,4},{24,8},{28,12},{1,17},{... | collective-permute-start | bytes 884744 | tf_op jit(solution)/shard_map/pair_w/ppermute | solution.py:598
  347.9 25.5 %collective-permute-start.44 = (bf16[208,768]{1,0:T(8,128)(2,1)S(1)}, bf16[208,768]{1,0:T(8,128)(2,1)S(1)}, u32[]{:S(2)}, u32[]{:S(2)}) collective-permute-start(bf16[208,768]{1,0:T(8,128)(2,1)S(1)} %fusion.21), channel_id=1, source_target_pairs={{0,4},{4,0},{8,12},{12,8},{16,20},{20,16},{24,28},{28,24},{1,5},{5... | collective-permute-start | bytes 958472 | tf_op jit(solution)/shard_map/val_y/ppermute | solution.py:598
  349.5 23.9 %collective-permute-start.45 = (bf16[192,768]{1,0:T(8,128)(2,1)S(1)}, bf16[192,768]{1,0:T(8,128)(2,1)S(1)}, u32[]{:S(2)}, u32[]{:S(2)}) collective-permute-start(bf16[192,768]{1,0:T(8,128)(2,1)S(1)} %fusion.37), channel_id=1, source_target_pairs={{0,8},{4,12},{8,0},{12,4},{16,24},{20,28},{24,16},{28,20},{1,9},{5... | collective-permute-start | bytes 884744 | tf_op jit(solution)/shard_map/outer_z2/ppermute | solution.py:598
  352.3 27.5 %collective-permute-start.47 = (bf16[192,768]{1,0:T(8,128)(2,1)S(1)}, bf16[192,768]{1,0:T(8,128)(2,1)S(1)}, u32[]{:S(2)}, u32[]{:S(2)}) collective-permute-start(bf16[192,768]{1,0:T(8,128)(2,1)S(1)} %add_convert_fusion.19), channel_id=1, source_target_pairs={{0,8},{4,12},{8,0},{12,4},{16,24},{20,28},{24,16},{28,20},{1,9},{5... | collective-permute-start | bytes 884744 | tf_op jit(solution)/shard_map/out_z/ppermute | solution.py:598
  373.5 35.1 %collective-permute-start.51 = (bf16[384,768]{1,0:T(8,128)(2,1)S(1)}, bf16[384,768]{1,0:T(8,128)(2,1)S(1)}, u32[]{:S(2)}, u32[]{:S(2)}) collective-permute-start(bf16[384,768]{1,0:T(8,128)(2,1)S(1)} %pad_maximum_fusion.4), channel_id=1, source_target_pairs={{0,4},{4,0},{8,12},{12,8},{16,20},{20,16},{24,28},{28,24},{1,5},{5... | collective-permute-start | bytes 1769480 | tf_op jit(solution)/shard_map/outer_y2/ppermute | solution.py:598
  379.8 24.9 %collective-permute-start.49 = (bf16[208,768]{1,0:T(8,128)(2,1)S(1)}, bf16[208,768]{1,0:T(8,128)(2,1)S(1)}, u32[]{:S(2)}, u32[]{:S(2)}) collective-permute-start(bf16[208,768]{1,0:T(8,128)(2,1)S(1)} %add_convert_fusion.13), channel_id=1, source_target_pairs={{0,16},{4,20},{8,24},{12,28},{16,0},{20,4},{24,8},{28,12},{1,17},{... | collective-permute-start | bytes 958472 | tf_op jit(solution)/shard_map/val_w/ppermute | solution.py:598
  384.1 24.5 %collective-permute-start.52 = (bf16[192,768]{1,0:T(8,128)(2,1)S(1)}, bf16[192,768]{1,0:T(8,128)(2,1)S(1)}, u32[]{:S(2)}, u32[]{:S(2)}) collective-permute-start(bf16[192,768]{1,0:T(8,128)(2,1)S(1)} %add_convert_fusion.16), channel_id=1, source_target_pairs={{0,16},{4,20},{8,24},{12,28},{16,0},{20,4},{24,8},{28,12},{1,17},{... | collective-permute-start | bytes 884744 | tf_op jit(solution)/shard_map/out_w/ppermute | solution.py:598
  384.3 26.1 %collective-permute-start.54 = (bf16[384,768]{1,0:T(8,128)(2,1)S(1)}, bf16[384,768]{1,0:T(8,128)(2,1)S(1)}, u32[]{:S(2)}, u32[]{:S(2)}) collective-permute-start(bf16[384,768]{1,0:T(8,128)(2,1)S(1)} %add_convert_fusion.5), channel_id=1, source_target_pairs={{0,4},{4,0},{8,12},{12,8},{16,20},{20,16},{24,28},{28,24},{1,5},{5... | collective-permute-start | bytes 1769480 | tf_op jit(solution)/shard_map/inner_y2/ppermute | solution.py:598
  (164 other events, 1378.6 us)
